TPU v7x, 32 devices: a whole 2x2x4 slice. The times are simulated.
32 devices in a mesh: parts: 2 (over y), dp: 4 (over x, core), tensor: 4 (over z).
Axes of the slice: x: 2, y: 2, z: 4, core: 2. Of those that a mesh axis runs over, the one named last changes fastest.
Arguments:
- tokens: bfloat16 [1024, 4096], P(('parts', 'dp')), parts along dimension 0, may hold values from -6 to 6
- cotangent: bfloat16 [1024, 4096], P(('parts', 'dp')), parts along dimension 0, may hold values from -6 to 6
- gate_blocks: bfloat16 [4, 112, 128, 128], P('tensor', 'dp'), may hold values from -0.25 to 0.25
- up_blocks: bfloat16 [4, 112, 128, 128], P('tensor', 'dp'), may hold values from -0.25 to 0.25
- down_blocks: bfloat16 [4, 112, 128, 128], P('tensor', 'dp'), may hold values from -0.125 to 0.125
- gate_index: int32 [2, 4, 112], P(None, 'tensor'), may hold values from 0 to 31, as said below
- up_index: int32 [2, 4, 112], P(None, 'tensor'), may hold values from 0 to 31, as said below
- down_index: int32 [2, 4, 112], P(None, 'tensor'), may hold values from 0 to 31, as said below
- block_counts: int32 [3, 4], P(None, 'tensor'), may hold values from 28 to 112, as said below
Outputs:
- layer_out: bfloat16 [1024, 4096], P(('parts', 'dp'), 'tensor'), parts along dimension 0
- token_grad: bfloat16 [1024, 4096], P(('parts', 'dp'), 'tensor'), parts along dimension 0
- gate_grad: bfloat16 [8, 112, 128, 128], P(('parts', 'tensor'), 'dp'), parts along dimension 0
- up_grad: bfloat16 [8, 112, 128, 128], P(('parts', 'tensor'), 'dp'), parts along dimension 0
- down_grad: bfloat16 [8, 112, 128, 128], P(('parts', 'tensor'), 'dp'), parts along dimension 0
There are 2 independent parts, one for each index of `parts`. A program takes and returns all parts, laid end to end along the dimension named above; an argument that names none is the same for every part. Nothing has to cross between parts.
Inputs may be any that keep to these rules, and one draw needn't show every extreme that they name: `gate_index`: entry [0, r, s] is a feature block (below 32) and entry [1, r, s] a hidden block of group r (below 28); the 112 pairs of one group are distinct. `up_index`: as for gate_index. `down_index`: as for gate_index. `block_counts`: for each matrix some group uses all 112 slots.
All inputs are finite; a program needn't handle non-finite values.
Results may differ from a plain program's by a relative error of at most 0.0095.
Values may be sent and summed in bfloat16 or wider, within the bound.
No kernel may reach another device: no remote copies, remote signals or barrier semaphores. Data moves between devices by JAX's collectives and lax.ppermute only.
A program may use at most 128 MiB of HBM per device.

v0:
```python
import jax
import jax.numpy as jnp
from jax import lax
from jax.sharding import PartitionSpec as P

FF = 14336


def choose_blocks(source, positions, blocks_across):
    row_count = source.shape[0]
    lookup = (positions[:, None] == jnp.arange(blocks_across, dtype=jnp.int32)[None, :]).astype(
        source.dtype
    )
    picked = jnp.einsum(
        "tjc,kj->tkc",
        source.reshape(row_count, blocks_across, -1),
        lookup,
        preferred_element_type=jnp.float32,
    )
    return picked.astype(source.dtype)


def place_blocks(terms, positions, live_mask, blocks_across):
    row_count = terms.shape[0]
    masked = jnp.where(live_mask[None, :, None], terms, jnp.zeros_like(terms))
    placed = (
        jnp.zeros((row_count, blocks_across, terms.shape[2]), jnp.float32)
        .at[:, positions]
        .add(masked)
    )
    return placed.reshape(row_count, -1)


def slot_view(block_index, filled, slot_count):
    outer_ids = block_index[0, 0]
    inner_ids = block_index[1, 0]
    live_mask = jnp.arange(slot_count, dtype=jnp.int32) < filled
    return (outer_ids, inner_ids, live_mask)


def forward_product(picked, weights):
    return jnp.einsum("tkc,kcd->tkd", picked, weights, preferred_element_type=jnp.float32)


def backward_product(picked, weights):
    return jnp.einsum("tkd,kcd->tkc", picked, weights, preferred_element_type=jnp.float32)


def block_grads(left_pick, right_pick, live_mask):
    grads = jnp.einsum("tkc,tkd->kcd", left_pick, right_pick, preferred_element_type=jnp.float32)
    return (grads * live_mask[:, None, None].astype(jnp.float32))[None]


def per_device(
    tokens,
    cotangent,
    gate_blocks,
    up_blocks,
    down_blocks,
    gate_index,
    up_index,
    down_index,
    block_counts,
):
    token_count, model_width = tokens.shape
    slot_count = gate_index.shape[2]
    block_size = gate_blocks.shape[2]
    model_blocks = model_width // block_size
    hidden_blocks = FF // block_size // lax.axis_size("tensor")
    gate_filled = block_counts[0, 0]
    up_filled = block_counts[1, 0]
    down_filled = block_counts[2, 0]
    gate_outer, gate_inner, gate_live = slot_view(gate_index, gate_filled, slot_count)
    up_outer, up_inner, up_live = slot_view(up_index, up_filled, slot_count)
    down_outer, down_inner, down_live = slot_view(down_index, down_filled, slot_count)
    tokens_gate = choose_blocks(tokens, gate_outer, model_blocks)
    tokens_up = choose_blocks(tokens, up_outer, model_blocks)
    gathered = (
        lax.all_gather(gate_blocks, "dp", axis=1, tiled=True),
        lax.all_gather(up_blocks, "dp", axis=1, tiled=True),
        lax.all_gather(down_blocks, "dp", axis=1, tiled=True),
    )
    gate_full, up_full, down_full = (gathered[0][0], gathered[1][0], gathered[2][0])
    gate_value = place_blocks(
        forward_product(tokens_gate, gate_full), gate_inner, gate_live, hidden_blocks
    )
    up_value = place_blocks(forward_product(tokens_up, up_full), up_inner, up_live, hidden_blocks)
    sigmoid_gate = jax.nn.sigmoid(gate_value)
    silu_gate = gate_value * sigmoid_gate
    hidden = (silu_gate * up_value).astype(jnp.bfloat16)
    hidden_down = choose_blocks(hidden, down_inner, hidden_blocks)
    cot_down = choose_blocks(cotangent, down_outer, model_blocks)
    out_part = place_blocks(
        forward_product(hidden_down, down_full), down_outer, down_live, model_blocks
    )
    layer_out = lax.psum_scatter(
        out_part.astype(jnp.bfloat16), "tensor", scatter_dimension=1, tiled=True
    )
    hidden_grad = place_blocks(
        backward_product(cot_down, down_full), down_inner, down_live, hidden_blocks
    )
    down_result = block_grads(hidden_down, cot_down, down_live)
    up_grad_value = (hidden_grad * silu_gate).astype(jnp.bfloat16)
    gate_grad_value = (
        hidden_grad * up_value * sigmoid_gate * (1.0 + gate_value * (1.0 - sigmoid_gate))
    ).astype(jnp.bfloat16)
    pick_gate_grad = choose_blocks(gate_grad_value, gate_inner, hidden_blocks)
    pick_up_grad = choose_blocks(up_grad_value, up_inner, hidden_blocks)
    token_part = place_blocks(
        backward_product(pick_gate_grad, gate_full), gate_outer, gate_live, model_blocks
    )
    token_part = token_part + place_blocks(
        backward_product(pick_up_grad, up_full), up_outer, up_live, model_blocks
    )
    token_grad = lax.psum_scatter(
        token_part.astype(jnp.bfloat16), "tensor", scatter_dimension=1, tiled=True
    )
    gate_result = block_grads(tokens_gate, pick_gate_grad, gate_live)
    up_result = block_grads(tokens_up, pick_up_grad, up_live)
    gate_sum, up_sum, down_sum = (
        lax.psum_scatter(
            gate_result.astype(jnp.bfloat16), "dp", scatter_dimension=1, tiled=True
        ).astype(jnp.float32),
        lax.psum_scatter(
            up_result.astype(jnp.bfloat16), "dp", scatter_dimension=1, tiled=True
        ).astype(jnp.float32),
        lax.psum_scatter(
            down_result.astype(jnp.bfloat16), "dp", scatter_dimension=1, tiled=True
        ).astype(jnp.float32),
    )
    return (
        layer_out,
        token_grad,
        gate_sum.astype(jnp.bfloat16),
        up_sum.astype(jnp.bfloat16),
        down_sum.astype(jnp.bfloat16),
    )


def solution(mesh):
    return jax.shard_map(
        per_device,
        mesh=mesh,
        in_specs=(
            P(("parts", "dp"), None),
            P(("parts", "dp"), None),
            P("tensor", "dp", None, None),
            P("tensor", "dp", None, None),
            P("tensor", "dp", None, None),
            P(None, "tensor", None),
            P(None, "tensor", None),
            P(None, "tensor", None),
            P(None, "tensor"),
        ),
        out_specs=(
            P(("parts", "dp"), "tensor"),
            P(("parts", "dp"), "tensor"),
            P(("parts", "tensor"), "dp", None, None),
            P(("parts", "tensor"), "dp", None, None),
            P(("parts", "tensor"), "dp", None, None),
        ),
        check_vma=False,
    )
```

profile of v0, /device:TPU:0, one launch (start us, length us, event | category | flops | bytes accessed | tf_op | source)
XLA Modules:
  0.0 410.3 jit_solution(16169369521784867939)
XLA Ops:
  7.2 0.7 all-gather.4.cloned.1.call-update
  8.0 0.7 all-gather.6.cloned.1.call-update
  8.7 0.7 all-gather.8.cloned.1.call-update
  9.4 1.4 copy.70
  10.9 2.9 convert_bitcast_fusion.5
  13.9 6.4 %copy.62 = bf16[128,112,128]{0,2,1:T(8,128)(2,1)} copy(bf16[128,112,128]{2,1,0:T(8,128)(2,1)} %convert_bitcast_fusion.5) | data formatting | bytes 7340032 | tf_op jit(solution)/shard_map/convert_element_type | solution.py:20
  20.3 2.9 convert_bitcast_fusion.4
  23.2 6.4 %copy.64 = bf16[128,112,128]{0,2,1:T(8,128)(2,1)} copy(bf16[128,112,128]{2,1,0:T(8,128)(2,1)} %convert_bitcast_fusion.4) | data formatting | bytes 7340032 | tf_op jit(solution)/shard_map/convert_element_type | solution.py:20
  31.1 0.7 iota_compare_fusion.6
  31.8 0.7 iota_compare_fusion.8
  32.5 2.9 convert_bitcast_fusion.2
  35.5 8.3 %all-gather.4.cloned.1.call-done = bf16[1,112,128,128]{3,2,0,1:T(8,128)(2,1)} async-done(((bf16[1,28,128,128]{3,2,0,1:T(8,128)(2,1)}), bf16[1,112,128,128]{3,2,0,1:T(8,128)(2,1)}) %all-gather.4.cloned.1.call-update) | async-done | bytes 3670032 | tf_op jit(solution)/shard_map/all_gather | solution.py:79
  43.8 7.9 %broadcast_select_fusion.5 = f32[112,128,128]{2,1,0:T(8,128)} fusion(pred[112]{0:T(512)(128)(4,1)S(1)} %iota_compare_fusion.7, bf16[128,112,128]{0,2,1:T(8,128)(2,1)} %copy.62, bf16[1,112,128,128]{3,2,0,1:T(8,128)(2,1)} %all-gather.4.cloned.1.call-done), kind=kOutput, calls=%fused_computation.34 | convolution fusion | flops 471597056 | bytes 14680176 | tf_op jit(solution)/shard_map/tkc,kcd->tkd/dot_general | solution.py:42
  51.9 15.1 %scatter_fusion = f32[128,28,128]{2,0,1:T(8,128)S(1)} fusion(f32[128,28,128]{2,0,1:T(8,128)S(1)} %broadcast.153.clone.1, s32[112]{0:T(128)S(1)} %get-tuple-element.29, f32[112,128,128]{2,1,0:T(8,128)} %broadcast_select_fusion.5), kind=kCustom, calls=%fused_computation | custom fusion | flops 1835008 | bytes 22020544 | tf_op jit(solution)/shard_map/scatter-add | solution.py:29
  67.0 9.9 %all-gather.6.cloned.1.call-done = bf16[1,112,128,128]{3,2,0,1:T(8,128)(2,1)} async-done(((bf16[1,28,128,128]{3,2,0,1:T(8,128)(2,1)}), bf16[1,112,128,128]{3,2,0,1:T(8,128)(2,1)}) %all-gather.6.cloned.1.call-update) | async-done | bytes 3670032 | tf_op jit(solution)/shard_map/all_gather | solution.py:80
  76.9 7.9 %broadcast_select_fusion.4 = f32[112,128,128]{2,1,0:T(8,128)} fusion(pred[112]{0:T(512)(128)(4,1)S(1)} %iota_compare_fusion.6, bf16[128,112,128]{0,2,1:T(8,128)(2,1)} %copy.64, bf16[1,112,128,128]{3,2,0,1:T(8,128)(2,1)} %all-gather.6.cloned.1.call-done), kind=kOutput, calls=%fused_computation.33 | convolution fusion | flops 471597056 | bytes 14680176 | tf_op jit(solution)/shard_map/tkc,kcd->tkd/dot_general | solution.py:42
  84.8 1.4 broadcast.153.clone.2
  86.2 23.3 %scatter_fusion.1 = f32[128,28,128]{2,0,1:T(8,128)} fusion(f32[128,28,128]{2,0,1:T(8,128)} %broadcast.153.clone.2, s32[112]{0:T(128)S(1)} %get-tuple-element.21, f32[112,128,128]{2,1,0:T(8,128)} %broadcast_select_fusion.4), kind=kCustom, calls=%fused_computation.1 | custom fusion | flops 1835008 | bytes 22020544 | tf_op jit(solution)/shard_map/scatter-add | solution.py:29
  110.0 8.8 %broadcast_select_fusion.2 = f32[112,128,128]{2,1,0:T(8,128)} fusion(pred[112]{0:T(512)(128)(4,1)S(1)} %iota_compare_fusion.8, bf16[1,112,128,128]{3,2,0,1:T(8,128)(2,1)} %all-gather.8.cloned.1.call-done, bf16[128,112,128]{2,1,0:T(8,128)(2,1)} %convert_bitcast_fusion.2), kind=kOutput, calls=%fused_computation.31 | convolution fusion | flops 471597056 | bytes 14680176 | tf_op jit(solution)/shard_map/tkd,kcd->tkc/dot_general | solution.py:46
  118.8 1.5 broadcast.153.clone
  120.2 23.0 %scatter_fusion.3 = f32[128,28,128]{2,0,1:T(8,128)} fusion(f32[128,28,128]{2,0,1:T(8,128)} %broadcast.153.clone, s32[112]{0:T(128)S(1)} %get-tuple-element.26, f32[112,128,128]{2,1,0:T(8,128)} %broadcast_select_fusion.2), kind=kCustom, calls=%fused_computation.3 | custom fusion | flops 1835008 | bytes 22020544 | tf_op jit(solution)/shard_map/scatter-add | solution.py:29
  143.3 3.3 multiply_convert_fusion.3
  146.6 1.2 convert_bitcast_fusion.1
  147.8 3.0 convert_bitcast_fusion
  150.8 5.6 %broadcast_select_fusion.1 = f32[112,128,128]{2,1,0:T(8,128)} fusion(pred[112]{0:T(512)(128)(4,1)S(1)} %iota_compare_fusion.7, bf16[1,112,128,128]{3,2,0,1:T(8,128)(2,1)S(1)} %copy-done.1, bf16[128,112,128]{2,1,0:T(8,128)(2,1)S(1)} %convert_bitcast_fusion.1), kind=kOutput, calls=%fused_computation.30 | convolution fusion | flops 471597056 | bytes 14680176 | tf_op jit(solution)/shard_map/tkd,kcd->tkc/dot_general | solution.py:46
  156.7 15.0 %scatter_fusion.4 = f32[128,32,128]{2,0,1:T(8,128)S(1)} fusion(f32[128,32,128]{2,0,1:T(8,128)S(1)} %broadcast.150.clone.1, s32[112]{0:T(128)S(1)} %get-tuple-element.28, f32[112,128,128]{2,1,0:T(8,128)} %broadcast_select_fusion.1), kind=kCustom, calls=%fused_computation.4 | custom fusion | flops 1835008 | bytes 22020544 | tf_op jit(solution)/shard_map/scatter-add | solution.py:29
  171.7 8.8 %broadcast_select_fusion = f32[112,128,128]{2,1,0:T(8,128)} fusion(pred[112]{0:T(512)(128)(4,1)S(1)} %iota_compare_fusion.6, bf16[1,112,128,128]{3,2,0,1:T(8,128)(2,1)} %all-gather.6.cloned.1.call-done, bf16[128,112,128]{2,1,0:T(8,128)(2,1)} %convert_bitcast_fusion), kind=kOutput, calls=%fused_computation.29 | convolution fusion | flops 471597056 | bytes 14680176 | tf_op jit(solution)/shard_map/tkd,kcd->tkc/dot_general | solution.py:46
  180.5 1.6 broadcast.150.clone.2
  182.0 23.2 %scatter_fusion.5 = f32[128,32,128]{2,0,1:T(8,128)} fusion(f32[128,32,128]{2,0,1:T(8,128)} %broadcast.150.clone.2, s32[112]{0:T(128)S(1)} %get-tuple-element.20, f32[112,128,128]{2,1,0:T(8,128)} %broadcast_select_fusion), kind=kCustom, calls=%fused_computation.5 | custom fusion | flops 1835008 | bytes 22020544 | tf_op jit(solution)/shard_map/scatter-add | solution.py:29
  205.2 2.9 add_convert_fusion
  208.1 2.3 copy.61
  210.5 3.0 convert_bitcast_fusion.3
  213.4 6.4 %copy.66 = bf16[128,112,128]{0,2,1:T(8,128)(2,1)} copy(bf16[128,112,128]{2,1,0:T(8,128)(2,1)} %convert_bitcast_fusion.3) | data formatting | bytes 7340032 | tf_op jit(solution)/shard_map/convert_element_type | solution.py:20
  219.8 7.9 %broadcast_select_fusion.3 = f32[112,128,128]{2,1,0:T(8,128)} fusion(pred[112]{0:T(512)(128)(4,1)S(1)} %iota_compare_fusion.8, bf16[128,112,128]{0,2,1:T(8,128)(2,1)} %copy.66, bf16[1,112,128,128]{3,2,0,1:T(8,128)(2,1)} %all-gather.8.cloned.1.call-done), kind=kOutput, calls=%fused_computation.32 | convolution fusion | flops 471597056 | bytes 14680176 | tf_op jit(solution)/shard_map/tkc,kcd->tkd/dot_general | solution.py:42
  227.9 15.0 %scatter_fusion.2 = f32[128,32,128]{2,0,1:T(8,128)S(1)} fusion(f32[128,32,128]{2,0,1:T(8,128)S(1)} %broadcast.150.clone, s32[112]{0:T(128)S(1)} %get-tuple-element.27, f32[112,128,128]{2,1,0:T(8,128)} %broadcast_select_fusion.3), kind=kCustom, calls=%fused_computation.2 | custom fusion | flops 1835008 | bytes 22020544 | tf_op jit(solution)/shard_map/scatter-add | solution.py:29
  243.1 1.3 copy.55
  244.5 0.7 fusion.77
  245.2 6.2 %fusion = bf16[1,112,128,128]{3,2,1,0:T(8,128)(2,1)} fusion(f32[112]{0:T(128)S(1)} %fusion.77, bf16[128,112,128]{0,2,1:T(8,128)(2,1)} %copy.62, bf16[128,112,128]{2,1,0:T(8,128)(2,1)} %copy-done), kind=kOutput, calls=%fused_computation.9 | convolution fusion | flops 473432064 | bytes 11010496 | tf_op jit(solution)/shard_map/tkc,tkd->kcd/dot_general | solution.py:50
  251.5 0.7 fusion.78
  252.1 6.1 %fusion.1 = bf16[1,112,128,128]{3,2,1,0:T(8,128)(2,1)} fusion(f32[112]{0:T(128)S(1)} %fusion.78, bf16[128,112,128]{0,2,1:T(8,128)(2,1)} %copy.64, bf16[128,112,128]{2,1,0:T(8,128)(2,1)} %convert_bitcast_fusion), kind=kOutput, calls=%fused_computation.10 | convolution fusion | flops 473432064 | bytes 11010496 | tf_op jit(solution)/shard_map/tkc,tkd->kcd/dot_general | solution.py:50
  258.4 0.7 fusion.76
  259.0 6.3 %fusion.2 = bf16[1,112,128,128]{3,2,1,0:T(8,128)(2,1)} fusion(f32[112]{0:T(128)S(1)} %fusion.76, bf16[128,112,128]{0,2,1:T(8,128)(2,1)} %copy.66, bf16[128,112,128]{2,1,0:T(8,128)(2,1)} %convert_bitcast_fusion.2), kind=kOutput, calls=%fused_computation.11 | convolution fusion | flops 473432064 | bytes 11010496 | tf_op jit(solution)/shard_map/tkc,tkd->kcd/dot_general | solution.py:50
  265.3 1.8 copy.69
  267.1 4.5 %reduce-scatter.6.cloned.1.call-done = bf16[128,1024]{0,1:T(8,128)(2,1)} async-done(((bf16[128,4096]{0,1:T(8,128)(2,1)}), bf16[128,1024]{0,1:T(8,128)(2,1)}) %reduce-scatter.6.cloned.1.call-update) | async-done | bytes 262160 | tf_op jit(solution)/shard_map/reduce_scatter | solution.py:96
  271.6 1.8 copy.68
  273.4 41.1 %reduce-scatter.10.cloned.1.call-done = bf16[1,28,128,128]{3,2,1,0:T(8,128)(2,1)} async-done(((bf16[1,112,128,128]{3,2,1,0:T(8,128)(2,1)}), bf16[1,28,128,128]{3,2,1,0:T(8,128)(2,1)}) %reduce-scatter.10.cloned.1.call-update) | async-done | bytes 917520 | tf_op jit(solution)/shard_map/reduce_scatter | solution.py:121
  314.5 44.5 %reduce-scatter.12.cloned.1.call-done = bf16[1,28,128,128]{3,2,1,0:T(8,128)(2,1)} async-done(((bf16[1,112,128,128]{3,2,1,0:T(8,128)(2,1)}), bf16[1,28,128,128]{3,2,1,0:T(8,128)(2,1)}) %reduce-scatter.12.cloned.1.call-update) | async-done | bytes 917520 | tf_op jit(solution)/shard_map/reduce_scatter | solution.py:124
  359.1 44.4 %reduce-scatter.14.cloned.1.call-done = bf16[1,28,128,128]{3,2,1,0:T(8,128)(2,1)} async-done(((bf16[1,112,128,128]{3,2,1,0:T(8,128)(2,1)}), bf16[1,28,128,128]{3,2,1,0:T(8,128)(2,1)}) %reduce-scatter.14.cloned.1.call-update) | async-done | bytes 917520 | tf_op jit(solution)/shard_map/reduce_scatter | solution.py:127
  (42 shorter events, 3.3 us)
Async XLA Ops:
  7.2 3.7 copy-start.4
  7.2 36.6 %all-gather.4.cloned.1.call-start = ((), (), s32[]{:S(2)}) async-start(), calls=%async_computation.5 | async-start | bytes 4587520 | tf_op jit(solution)/shard_map/all_gather | solution.py:79
  7.9 69.0 %all-gather.6.cloned.1.call-start = ((), (), s32[]{:S(2)}) async-start(), calls=%async_computation.6 | async-start | bytes 4587520 | tf_op jit(solution)/shard_map/all_gather | solution.py:80
  8.7 101.4 %all-gather.8.cloned.1.call-start = ((), (), s32[]{:S(2)}) async-start(), calls=%async_computation.7 | async-start | bytes 4587520 | tf_op jit(solution)/shard_map/all_gather | solution.py:81
  9.4 255.9 %reduce-scatter.8.cloned.1.call-start = ((), (), s32[]{:S(2)}) async-start(), calls=%async_computation.9 | async-start | bytes 1310720 | tf_op jit(solution)/shard_map/reduce_scatter | solution.py:115
  13.9 6.4 %copy-start.5 = (s32[2,1,112]{2,1,0:T(1,128)S(1)}, s32[2,1,112]{2,1,0:T(1,128)}, u32[]{:S(2)}) copy-start(s32[2,1,112]{2,1,0:T(1,128)} %param.15) | copy-start | bytes 2692
  23.2 6.4 %copy-start.2 = (bf16[128,4096]{1,0:T(8,128)(2,1)S(1)}, bf16[128,4096]{1,0:T(8,128)(2,1)}, u32[]{:S(2)}) copy-start(bf16[128,4096]{1,0:T(8,128)(2,1)} %param.10) | copy-start | bytes 3145732
  23.2 6.7 %copy-start.3 = (s32[3,1]{0,1:T(1,128)S(1)}, s32[3,1]{0,1:T(1,128)}, u32[]{:S(2)}) copy-start(s32[3,1]{0,1:T(1,128)} %param.17) | copy-start | bytes 40
  23.2 9.3 %copy-start.6 = (s32[2,1,112]{2,1,0:T(1,128)S(1)}, s32[2,1,112]{2,1,0:T(1,128)}, u32[]{:S(2)}) copy-start(s32[2,1,112]{2,1,0:T(1,128)} %param.16) | copy-start | bytes 2692
  146.6 4.2 %copy-start.1 = (bf16[1,112,128,128]{3,2,0,1:T(8,128)(2,1)S(1)}, bf16[1,112,128,128]{3,2,0,1:T(8,128)(2,1)}, u32[]{:S(2)}) copy-start(bf16[1,112,128,128]{3,2,0,1:T(8,128)(2,1)} %all-gather.4.cloned.1.call-done) | copy-start | bytes 11010052
  147.8 8.6 %copy-start = (bf16[128,112,128]{2,1,0:T(8,128)(2,1)}, bf16[128,112,128]{2,1,0:T(8,128)(2,1)S(1)}, u32[]{:S(2)}) copy-start(bf16[128,112,128]{2,1,0:T(8,128)(2,1)S(1)} %convert_bitcast_fusion.1) | copy-start | bytes 11010052
  210.4 61.2 %reduce-scatter.6.cloned.1.call-start = ((), (), s32[]{:S(2)}) async-start(), calls=%async_computation.8 | async-start | bytes 1310720 | tf_op jit(solution)/shard_map/reduce_scatter | solution.py:96
  244.5 70.0 %reduce-scatter.10.cloned.1.call-start = ((), (), s32[]{:S(2)}) async-start(), calls=%async_computation.10 | async-start | bytes 4587520 | tf_op jit(solution)/shard_map/reduce_scatter | solution.py:121
  251.4 107.6 %reduce-scatter.12.cloned.1.call-start = ((), (), s32[]{:S(2)}) async-start(), calls=%async_computation.11 | async-start | bytes 4587520 | tf_op jit(solution)/shard_map/reduce_scatter | solution.py:124
  258.3 145.1 %reduce-scatter.14.cloned.1.call-start = ((), (), s32[]{:S(2)}) async-start(), calls=%async_computation.12 | async-start | bytes 4587520 | tf_op jit(solution)/shard_map/reduce_scatter | solution.py:127
Sparse Core Ops, SparseCore 0:
  9.6 34.1 all-gather.3
  45.4 31.4 all-gather.5
  78.5 31.4 all-gather.7
  210.5 26.9 reduce-scatter.7
  244.6 26.9 reduce-scatter.5
  274.6 39.8 reduce-scatter.9
  317.8 41.2 reduce-scatter.11
  362.2 41.2 reduce-scatter.13
where the time goes:
time: 413 us; the launch traced here: 410 us
  waiting for transfers between devices  155 us (38%)
  other arithmetic  125 us (30%)
  matrix products  81.4 us (20%)
  local copies, waits for them, and re-layouts  33.8 us (8%)
  between operations  14.4 us (3%)
    scatter-add x6, other arithmetic, place_blocks(): placed = jnp.zeros((row_count, blocks_across, terms.shape[2]), jnp.float3...  115 us
    reduce_scatter x1, waiting for transfers between devices, per_device(): lax.psum_scatter(up_result.astype(jnp.bfloat16), 'dp', scatter_dimension=...  44.5 us
    reduce_scatter x1, waiting for transfers between devices, per_device(): lax.psum_scatter(down_result.astype(jnp.bfloat16), 'dp', scatter_dimensio...  44.4 us
    reduce_scatter x1, waiting for transfers between devices, per_device(): lax.psum_scatter(gate_result.astype(jnp.bfloat16), 'dp', scatter_dimensio...  41.1 us
    dot_general x3, matrix products, forward_product(): jnp.einsum('tkc,kcd->tkd', picked, weights, preferred_element_type=jnp.fl...  23.7 us
    dot_general x3, matrix products, backward_product(): jnp.einsum('tkd,kcd->tkc', picked, weights, preferred_element_type=jnp.fl...  23.2 us
    convert_element_type x3, local copies, waits for them, and re-layouts, choose_blocks(): return picked.astype(source.dtype)  19.2 us
    dot_general x3, matrix products, block_grads(): jnp.einsum('tkc,tkd->kcd', left_pick, right_pick, preferred_element_type=...  18.6 us
  transfers between devices with their start and end apart: 8, of which 7 were waited for; matrix products, arithmetic and copies ran while one was open for 34% of the time, Pallas kernels for 0%

commit v1 on v0

v1 whole, which is shorter than its diff:
```python
import functools

import jax
import jax.numpy as jnp
from jax import lax
from jax.experimental import pallas as pl
from jax.experimental.pallas import tpu as pltpu
from jax.sharding import PartitionSpec as P

FF = 14336
F32 = jnp.float32
BF16 = jnp.bfloat16
UNROLL = 4
NN = (((1,), (0,)), ((), ()))
NT = (((1,), (1,)), ((), ()))

VMEM = pl.BlockSpec(memory_space=pltpu.VMEM)
SMEM = pl.BlockSpec(memory_space=pltpu.SMEM)


def mm(left, right, dims=NN):
    return lax.dot_general(left, right, dims, preferred_element_type=F32)


def call(body, ints, arrays, outs, scratch=(), products=0, aliases=None):
    size = lambda a: a.size * a.dtype.itemsize
    total = sum(size(a) for a in arrays) + sum(size(o) for o in outs)
    held = total + sum(s.inner_aval.size * s.inner_aval.dtype.itemsize if hasattr(s, "inner_aval") else 0 for s in scratch)
    return pl.pallas_call(
        body,
        out_shape=outs,
        in_specs=[SMEM] * len(ints) + [VMEM] * len(arrays),
        out_specs=[VMEM] * len(outs),
        scratch_shapes=list(scratch),
        input_output_aliases=aliases or {},
        compiler_params=pltpu.CompilerParams(vmem_limit_bytes=held + (12 << 20)),
        cost_estimate=pl.CostEstimate(
            flops=products * 2 * 128**3 * 8, bytes_accessed=total, transcendentals=0
        ),
    )(*ints, *arrays)


class Place:
    def __init__(self, chips, parts, groups, shard):
        self.chips, self.parts, self.groups, self.shard = chips, parts, groups, shard

    def first(self, where, piece):
        chip, core, part = where[0], where[1], where[2]
        back, other, half = piece
        chip = lax.rem(chip + (self.chips - back), self.chips)
        core = 1 - core if other else core
        start = (chip * 2 + core) * self.shard
        if half is not None:
            start = start + (1 - part if half else part) * (self.shard // 2)
        return start


def over_live(live, terms, store):
    def several(step, _):
        slots = [step * UNROLL + u for u in range(UNROLL)]
        values = [terms(slot) for slot in slots]
        for slot, value in zip(slots, values):
            store(slot, value)
        return 0

    def single(slot, _):
        store(slot, terms(slot))
        return 0

    rounds = lax.div(live, UNROLL)
    lax.fori_loop(0, rounds, several, 0)
    lax.fori_loop(rounds * UNROLL, live, single, 0)


def live_in(count, first, extent):
    return jnp.clip(count - first, 0, extent)


def columns(block, size=128):
    return pl.ds(pl.multiple_of(block * size, size), size)


def zero(acc):
    acc[...] = jnp.zeros(acc.shape, acc.dtype)


def make(mesh):
    parts = mesh.shape["parts"]
    dp = mesh.shape["dp"]
    groups = mesh.shape["tensor"]
    chips = dp // 2

    def pair_swap(a):
        return lax.ppermute(a, "dp", [(i, i ^ 1) for i in range(dp)])

    def chip_shift(a, k):
        return lax.ppermute(
            a, "dp", [(i, ((i // 2 + k) % chips) * 2 + i % 2) for i in range(dp)]
        )

    def part_swap(a):
        return lax.ppermute(a, "parts", [(0, 1), (1, 0)])

    def group_shift(a, k):
        return lax.ppermute(a, "tensor", [(i, (i + k) % groups) for i in range(groups)])

    def per_device(
        tokens, cotangent, gate_blocks, up_blocks, down_blocks, gate_index, up_index, down_index, block_counts
    ):
        token_count, model_width = tokens.shape
        size = gate_blocks.shape[2]
        shard = gate_blocks.shape[1]
        model_blocks = model_width // size
        hidden_blocks = FF // size // groups
        halves = parts == 2 and shard % 2 == 0
        place = Place(chips, parts, groups, shard)
        at = lax.axis_index("dp")
        part = lax.axis_index("parts")
        where = jnp.stack([at // 2, at % 2, part, lax.axis_index("tensor")]).astype(jnp.int32)
        tables = [gate_index[:, 0], up_index[:, 0], down_index[:, 0]]
        counts = block_counts[:, 0]

        hidden_f32 = jax.ShapeDtypeStruct((hidden_blocks, token_count, size), F32)
        hidden_bf16 = jax.ShapeDtypeStruct((hidden_blocks, token_count, size), BF16)

        own = [gate_blocks[0], up_blocks[0], down_blocks[0]]
        keys = [(0, False, None), (0, True, None)]
        far_keys = []
        for k in range(1, chips):
            for half in (False, True) if halves else (None,):
                far_keys += [(k, False, half), (k, True, half)]
        sent = [
            lax.dynamic_slice_in_dim(w, part * (shard // 2), shard // 2, 0) if halves else w
            for w in own
        ]
        over_x = [[chip_shift(w, k) for k in range(1, chips)] for w in sent]
        near = [[w, pair_swap(w)] for w in own]
        far = []
        for arrived in over_x:
            pieces = []
            for w in arrived:
                pieces += [w, pair_swap(w)]
                if halves:
                    v = part_swap(w)
                    pieces += [v, pair_swap(v)]
            far.append(pieces)

        def turn(t_ref, o_ref):
            for j in range(model_blocks):
                o_ref[j] = t_ref[:, j * size : (j + 1) * size].T

        (tokens_t,) = call(
            turn, [], [tokens], [jax.ShapeDtypeStruct((model_blocks, size, token_count), BF16)]
        )
        tokens_t_pair = pair_swap(tokens_t)
        cotangent_pair = pair_swap(cotangent)

        def add_pieces(acc, x_ref, w_refs, piece_keys, table, count, where_ref):
            for w_ref, key in zip(w_refs, piece_keys):
                first = place.first(where_ref, key)

                def terms(s, w_ref=w_ref, first=first):
                    return mm(x_ref[:, columns(table[0, first + s])], w_ref[s])

                def store(s, value, first=first):
                    acc[table[1, first + s]] += value

                over_live(live_in(count, first, w_ref.shape[0]), terms, store)

        def near_body(where_ref, counts_ref, tg, tu, x_ref, g0, g1, u0, u1, acc_g, acc_u):
            zero(acc_g)
            zero(acc_u)
            add_pieces(acc_g, x_ref, [g0, g1], keys, tg, counts_ref[0], where_ref)
            add_pieces(acc_u, x_ref, [u0, u1], keys, tu, counts_ref[1], where_ref)

        acc_g, acc_u = call(
            near_body,
            [where, counts, tables[0], tables[1]],
            [tokens, *near[0], *near[1]],
            [hidden_f32, hidden_f32],
            products=4 * shard,
        )

        n_far = len(far_keys)

        def gate_body(where_ref, counts_ref, tg, acc_in, x_ref, *refs):
            w_refs, acc = refs[:n_far], refs[n_far]
            acc[...] = acc_in[...]
            add_pieces(acc, x_ref, w_refs, far_keys, tg, counts_ref[0], where_ref)

        (gate_value,) = call(
            gate_body,
            [where, counts, tables[0]],
            [acc_g, tokens, *far[0]],
            [hidden_f32],
            products=2 * shard,
        )

        def up_body(where_ref, counts_ref, tu, acc_in, gate_in, x_ref, *refs):
            w_refs = refs[:n_far]
            silu_ref, slope_ref, h_ref, ht_ref, acc = refs[n_far:]
            acc[...] = acc_in[...]
            add_pieces(acc, x_ref, w_refs, far_keys, tu, counts_ref[1], where_ref)

            def finish(b, _):
                gate, up = gate_in[b], acc[b]
                sigma = jax.nn.sigmoid(gate)
                silu = gate * sigma
                hidden = (silu * up).astype(BF16)
                silu_ref[b] = silu
                slope_ref[b] = up * sigma * (1.0 + gate * (1.0 - sigma))
                h_ref[b] = hidden
                ht_ref[b] = hidden.T
                return 0

            lax.fori_loop(0, hidden_blocks, finish, 0)

        silu, slope, hidden, hidden_t = call(
            up_body,
            [where, counts, tables[1]],
            [acc_u, gate_value, tokens, *far[1]],
            [
                hidden_f32,
                hidden_f32,
                hidden_bf16,
                jax.ShapeDtypeStruct((hidden_blocks, size, token_count), BF16),
            ],
            scratch=[pltpu.VMEM(hidden_f32.shape, F32)],
            products=2 * shard + 20,
        )
        hidden_t_pair = pair_swap(hidden_t)

        shard_out = jax.ShapeDtypeStruct((shard, size, size), BF16)

        def block_grads(m, ahead, left, right):
            def body(where_ref, counts_ref, table, l0, l1, r0, r1, *outs):
                for k, o_ref in zip(ahead, outs):
                    first = place.first(where_ref, ((chips - k) % chips, False, None))
                    live = live_in(counts_ref[m], first, shard)

                    def terms(s, first=first):
                        f, h = table[0, first + s], table[1, first + s]
                        if m == 2:
                            l, c = h, columns(f)
                            r = [r_ref[:, c] for r_ref in (r0, r1)]
                        else:
                            l = f
                            r = [r_ref[m, h] for r_ref in (r0, r1)]
                        return mm(
                            jnp.concatenate([l0[l], l1[l]], axis=1), jnp.concatenate(r, axis=0)
                        )

                    def store(s, value, o_ref=o_ref):
                        o_ref[s] = value.astype(BF16)

                    over_live(live, terms, store)

                    def clear(s, _, o_ref=o_ref):
                        o_ref[s] = jnp.zeros((size, size), BF16)
                        return 0

                    lax.fori_loop(live, shard, clear, 0)

            return call(
                body,
                [where, counts, tables[m]],
                [*left, *right],
                [shard_out] * len(ahead),
                products=len(ahead) * shard,
            )

        away = tuple(range(1, chips))

        def send(m, left, right):
            return [chip_shift(g, k) for g, k in zip(block_grads(m, away, left, right), away)]

        def total(kept, arrived):
            value = kept.astype(F32)
            for g in arrived:
                value = value + g.astype(F32)
            return value.astype(BF16)[None]

        down_operands = ([hidden_t, hidden_t_pair], [cotangent, cotangent_pair])
        down_far = send(2, *down_operands)

        def back_body(where_ref, counts_ref, td, c_ref, silu_ref, slope_ref, *refs):
            w_refs, o_ref, acc = refs[: 2 + n_far], refs[2 + n_far], refs[3 + n_far]
            zero(acc)
            for w_ref, key in zip(w_refs, keys + far_keys):
                first = place.first(where_ref, key)

                def terms(s, w_ref=w_ref, first=first):
                    return mm(c_ref[:, columns(td[0, first + s])], w_ref[s], NT)

                def store(s, value, first=first):
                    acc[td[1, first + s]] += value

                over_live(live_in(counts_ref[2], first, w_ref.shape[0]), terms, store)

            def finish(b, _):
                grad = acc[b]
                o_ref[0, b] = (grad * slope_ref[b]).astype(BF16)
                o_ref[1, b] = (grad * silu_ref[b]).astype(BF16)
                return 0

            lax.fori_loop(0, hidden_blocks, finish, 0)

        (grads,) = call(
            back_body,
            [where, counts, tables[2]],
            [cotangent, silu, slope, *near[2], *far[2]],
            [jax.ShapeDtypeStruct((2, hidden_blocks, token_count, size), BF16)],
            scratch=[pltpu.VMEM(hidden_f32.shape, F32)],
            products=4 * shard,
        )
        grads_pair = pair_swap(grads)
        token_operands = ([tokens_t, tokens_t_pair], [grads, grads_pair])
        gate_far = send(0, *token_operands)
        up_far = send(1, *token_operands)

        width = model_blocks // groups
        chunk = jax.ShapeDtypeStruct((token_count, width * size), BF16)

        def cut(where_ref, acc, outs):
            for k in range(groups):
                to = lax.rem(where_ref[3] + k, groups) * width
                for j in range(width):
                    outs[k][:, j * size : (j + 1) * size] = acc[to + j].astype(BF16)

        def out_body(where_ref, counts_ref, td, h_ref, *refs):
            w_refs, outs, acc = refs[: 2 + n_far], refs[2 + n_far : -1], refs[-1]
            zero(acc)
            for w_ref, key in zip(w_refs, keys + far_keys):
                first = place.first(where_ref, key)

                def terms(s, w_ref=w_ref, first=first):
                    return mm(h_ref[td[1, first + s]], w_ref[s])

                def store(s, value, first=first):
                    acc[td[0, first + s]] += value

                over_live(live_in(counts_ref[2], first, w_ref.shape[0]), terms, store)
            cut(where_ref, acc, outs)

        model_acc = pltpu.VMEM((model_blocks, token_count, size), F32)
        out_parts = call(
            out_body,
            [where, counts, tables[2]],
            [hidden, *near[2], *far[2]],
            [chunk] * groups,
            scratch=[model_acc],
            products=4 * shard,
        )

        def token_body(where_ref, counts_ref, tg, tu, y_ref, *refs):
            n = 2 + n_far
            outs, acc = refs[2 * n : -1], refs[-1]
            zero(acc)
            for m, table in ((0, tg), (1, tu)):
                for w_ref, key in zip(refs[m * n : (m + 1) * n], keys + far_keys):
                    first = place.first(where_ref, key)

                    def terms(s, m=m, table=table, w_ref=w_ref, first=first):
                        return mm(y_ref[m, table[1, first + s]], w_ref[s], NT)

                    def store(s, value, table=table, first=first):
                        acc[table[0, first + s]] += value

                    over_live(live_in(counts_ref[m], first, w_ref.shape[0]), terms, store)
            cut(where_ref, acc, outs)

        token_parts = call(
            token_body,
            [where, counts, tables[0], tables[1]],
            [grads, *near[0], *far[0], *near[1], *far[1]],
            [chunk] * groups,
            scratch=[model_acc],
            products=8 * shard,
        )

        def over_groups(chunks):
            value = chunks[0].astype(F32)
            for k in range(1, groups):
                value = value + group_shift(chunks[k], k).astype(F32)
            return value.astype(BF16)

        layer_out = over_groups(out_parts)
        token_grad = over_groups(token_parts)

        (down_kept,) = block_grads(2, (0,), *down_operands)
        (gate_kept,) = block_grads(0, (0,), *token_operands)
        (up_kept,) = block_grads(1, (0,), *token_operands)
        return (
            layer_out,
            token_grad,
            total(gate_kept, gate_far),
            total(up_kept, up_far),
            total(down_kept, down_far),
        )

    return per_device


def solution(mesh):
    return jax.shard_map(
        make(mesh),
        mesh=mesh,
        in_specs=(
            P(("parts", "dp"), None),
            P(("parts", "dp"), None),
            P("tensor", "dp", None, None),
            P("tensor", "dp", None, None),
            P("tensor", "dp", None, None),
            P(None, "tensor", None),
            P(None, "tensor", None),
            P(None, "tensor", None),
            P(None, "tensor"),
        ),
        out_specs=(
            P(("parts", "dp"), "tensor"),
            P(("parts", "dp"), "tensor"),
            P(("parts", "tensor"), "dp", None, None),
            P(("parts", "tensor"), "dp", None, None),
            P(("parts", "tensor"), "dp", None, None),
        ),
        check_vma=False,
    )
```

time: 413 us -> 178 us (0.43)
  other arithmetic: 125 us -> 5.56 us
  matrix products: 81.4 us -> 0 us
  waiting for transfers between devices: 155 us -> 82.6 us
  Pallas kernels: 0 us -> 53.6 us
  local copies, waits for them, and re-layouts: 33.8 us -> 6.69 us
  starting transfers between devices: 0.32 us -> 25.8 us
  between operations: 14.4 us -> 0.95 us
    reduce_scatter x5 -> x0, waiting for transfers between devices: 135 us -> none  [the longest x1 44.5 us: per_device(): lax.psum_scatter(up_result.astype(jnp.bfloat16), 'dp', scatter_dimension=...]
    scatter-add x6 -> x0, other arithmetic: 115 us -> none  [place_blocks(): placed = jnp.zeros((row_count, blocks_across, terms.shape[2]), jnp.float3...]
    ppermute x0 -> x28, waiting for transfers between devices: none -> 82.6 us  [the longest x6 49.3 us: chip_shift(): lax.ppermute(a, 'dp', [(i, (i // 2 + k) % chips * 2 + i % 2) for i in ran...]
    dot_general x15 -> x0, matrix products: 81.4 us -> none  [the longest x3 23.7 us: forward_product(): jnp.einsum('tkc,kcd->tkd', picked, weights, preferred_element_type=jnp.fl...]
    pallas_call x0 -> x13, Pallas kernels: none -> 53.6 us  [call(): pl.pallas_call(body, out_shape=outs, in_specs=[SMEM] * len(ints) + [VMEM]...]
    ppermute x0 -> x28, starting transfers between devices: none -> 25.8 us  [the longest x6 14.5 us: chip_shift(): lax.ppermute(a, 'dp', [(i, (i // 2 + k) % chips * 2 + i % 2) for i in ran...]
    convert_element_type x5 -> x0, local copies, waits for them, and re-layouts: 22.8 us -> none  [the longest x3 19.2 us: choose_blocks(): return picked.astype(source.dtype)]
    all_gather x3 -> x0, waiting for transfers between devices: 18.8 us -> none  [the longest x1 9.92 us: per_device(): lax.all_gather(up_blocks, 'dp', axis=1, tiled=True)]
  transfers between devices with their start and end apart: 8 -> 28, of which waited for: 7 -> 10; matrix products, arithmetic and copies ran while one was open for 34% -> 4% of each run, Pallas kernels for 0% -> 31%
where the time goes in v1:
time: 178 us; the launch traced here: 175 us
  waiting for transfers between devices  82.6 us (46%)
  Pallas kernels  53.6 us (30%)
  starting transfers between devices  25.8 us (14%)
  local copies, waits for them, and re-layouts  6.69 us (4%)
  other arithmetic  5.56 us (3%)
    pallas_call x13, Pallas kernels, call(): pl.pallas_call(body, out_shape=outs, in_specs=[SMEM] * len(ints) + [VMEM]...  53.6 us
    ppermute x6, waiting for transfers between devices, chip_shift(): lax.ppermute(a, 'dp', [(i, (i // 2 + k) % chips * 2 + i % 2) for i in ran...  49.3 us
    ppermute x3, waiting for transfers between devices, part_swap(): return lax.ppermute(a, 'parts', [(0, 1), (1, 0)])  18.8 us
    ppermute x6, starting transfers between devices, chip_shift(): lax.ppermute(a, 'dp', [(i, (i // 2 + k) % chips * 2 + i % 2) for i in ran...  14.5 us
    ppermute x6, waiting for transfers between devices, group_shift(): lax.ppermute(a, 'tensor', [(i, (i + k) % groups) for i in range(groups)])  14.4 us
    unnamed x28, local copies, waits for them, and re-layouts  4.49 us
    ppermute x6, starting transfers between devices, group_shift(): lax.ppermute(a, 'tensor', [(i, (i + k) % groups) for i in range(groups)])  4.38 us
    ppermute x3, starting transfers between devices, part_swap(): return lax.ppermute(a, 'parts', [(0, 1), (1, 0)])  4.04 us
  transfers between devices with their start and end apart: 28, of which 10 were waited for; matrix products, arithmetic and copies ran while one was open for 4% of the time, Pallas kernels for 31%

profile of v1, /device:TPU:0, one launch (start us, length us, event | category | flops | bytes accessed | tf_op | source)
XLA Modules:
  0.0 175.2 jit_solution(14695329797161585101)
XLA Ops:
  0.7 0.5 collective-permute-start
  1.2 1.1 dynamic-slice_bitcast_fusion.2
  2.3 2.6 %collective-permute-start.2 = (bf16[14,128,128]{2,1,0:T(8,128)(2,1)S(1)}, bf16[14,128,128]{2,1,0:T(8,128)(2,1)S(1)}, u32[]{:S(2)}, u32[]{:S(2)}) collective-permute-start(bf16[14,128,128]{2,1,0:T(8,128)(2,1)S(1)} %dynamic-slice_bitcast_fusion.2), channel_id=1, source_target_pairs={{0,8},{4,12},{8,0},{12,4},{1,9},{5,13},{9,1},{13,5},{2,10},{6,14},... | collective-permute-start | bytes 1376264 | tf_op jit(solution)/shard_map/ppermute | solution.py:97
  5.0 1.0 dynamic-slice_bitcast_fusion.1
  6.1 0.4 collective-permute-start.6
  6.6 1.7 collective-permute-start.11
  8.3 8.0 %collective-permute-done.2.refs_0_.refs_2_ = bf16[14,128,128]{2,1,0:T(8,128)(2,1)S(1)} collective-permute-done((bf16[14,128,128]{2,1,0:T(8,128)(2,1)S(1)}, bf16[14,128,128]{2,1,0:T(8,128)(2,1)S(1)}, u32[]{:S(2)}, u32[]{:S(2)}) %collective-permute-start.2) | collective-permute-done | bytes 458784 | tf_op jit(solution)/shard_map/ppermute | solution.py:97
  16.3 2.0 %collective-permute-start.4 = (bf16[14,128,128]{2,1,0:T(8,128)(2,1)S(1)}, bf16[14,128,128]{2,1,0:T(8,128)(2,1)}, u32[]{:S(2)}, u32[]{:S(2)}) collective-permute-start(bf16[14,128,128]{2,1,0:T(8,128)(2,1)S(1)} %collective-permute-done.2.refs_0_.refs_2_), channel_id=1, source_target_pairs={{0,16},{16,0},{1,17},{17,1},{2,18},{18,2},{3,19},{19,3},{4,20},{20... | collective-permute-start | bytes 1376264 | tf_op jit(solution)/shard_map/ppermute | solution.py:102
  18.3 7.9 %collective-permute-done.6.refs_0_.refs_8_ = bf16[14,128,128]{2,1,0:T(8,128)(2,1)} collective-permute-done((bf16[14,128,128]{2,1,0:T(8,128)(2,1)S(1)}, bf16[14,128,128]{2,1,0:T(8,128)(2,1)}, u32[]{:S(2)}, u32[]{:S(2)}) %collective-permute-start.6) | collective-permute-done | bytes 458784 | tf_op jit(solution)/shard_map/ppermute | solution.py:97
  26.3 9.5 %collective-permute-done.11.refs_2_ = bf16[14,128,128]{2,1,0:T(8,128)(2,1)} collective-permute-done((bf16[14,128,128]{2,1,0:T(8,128)(2,1)S(1)}, bf16[14,128,128]{2,1,0:T(8,128)(2,1)}, u32[]{:S(2)}, u32[]{:S(2)}) %collective-permute-start.11) | collective-permute-done | bytes 458784 | tf_op jit(solution)/shard_map/ppermute | solution.py:97
  35.8 1.8 %collective-permute-start.8 = (bf16[14,128,128]{2,1,0:T(8,128)(2,1)}, bf16[14,128,128]{2,1,0:T(8,128)(2,1)}, u32[]{:S(2)}, u32[]{:S(2)}) collective-permute-start(bf16[14,128,128]{2,1,0:T(8,128)(2,1)} %collective-permute-done.6.refs_0_.refs_8_), channel_id=1, source_target_pairs={{0,16},{16,0},{1,17},{17,1},{2,18},{18,2},{3,19},{19,3},{4,20},{20... | collective-permute-start | bytes 1376264 | tf_op jit(solution)/shard_map/ppermute | solution.py:102
  37.8 0.9 copy-done.11
  38.7 0.5 collective-permute-start.10
  39.3 10.2 %collective-permute-done.8.refs_2_.refs_10_ = bf16[14,128,128]{2,1,0:T(8,128)(2,1)} collective-permute-done((bf16[14,128,128]{2,1,0:T(8,128)(2,1)}, bf16[14,128,128]{2,1,0:T(8,128)(2,1)}, u32[]{:S(2)}, u32[]{:S(2)}) %collective-permute-start.8) | collective-permute-done | bytes 458784 | tf_op jit(solution)/shard_map/ppermute | solution.py:102
  49.5 8.6 %collective-permute-done.13.refs_4_ = bf16[14,128,128]{2,1,0:T(8,128)(2,1)} collective-permute-done((bf16[14,128,128]{2,1,0:T(8,128)(2,1)}, bf16[14,128,128]{2,1,0:T(8,128)(2,1)}, u32[]{:S(2)}, u32[]{:S(2)}) %collective-permute-start.13) | collective-permute-done | bytes 458784 | tf_op jit(solution)/shard_map/ppermute | solution.py:102
  58.1 0.5 collective-permute-start.14
  58.7 1.2 copy-done.3
  59.8 1.2 copy-done.5
  61.0 1.2 copy-done.12
  62.2 5.2 %shard_map.128 = (f32[28,128,128]{2,1,0:T(8,128)S(1)}, f32[28,128,128]{2,1,0:T(8,128)S(1)}) custom-call(s32[4]{0:T(128)S(1)} %pad_add_fusion.where_ref, s32[3]{0:T(128)S(1)} %bitcast.32, s32[2,112]{1,0:T(2,128)S(1)} %bitcast.48, s32[2,112]{1,0:T(2,128)S(1)} %bitcast.53, bf16[128,4096]{1,0:T(8,128)(2,1)S(1)} %copy-done.1, bf16[28,128,128]{2,1,0:T(8,128)(2,1)S(1)} %bitcast.27, ...), custom_call_target="tpu_custom_call" | custom-call | flops 3758096384 | bytes 8388608 | tf_op jit(solution)/shard_map/pallas_call | solution.py:29
  67.4 4.8 %shard_map.129.gate_in = f32[28,128,128]{2,1,0:T(8,128)S(1)} custom-call(s32[4]{0:T(128)S(1)} %pad_add_fusion.where_ref, s32[3]{0:T(128)S(1)} %bitcast.33, s32[2,112]{1,0:T(2,128)S(1)} %bitcast.49, f32[28,128,128]{2,1,0:T(8,128)S(1)} %get-tuple-element.20.acc_in, bf16[128,4096]{1,0:T(8,128)(2,1)S(1)} %copy-done.1, ...), custom_call_target="tpu_custom_call" | custom-call | flops 1879048192 | bytes 6553600 | tf_op jit(solution)/shard_map/pallas_call | solution.py:29
  72.4 3.8 %shard_map.130 = (f32[28,128,128]{2,1,0:T(8,128)S(1)}, f32[28,128,128]{2,1,0:T(8,128)S(1)}, bf16[28,128,128]{2,1,0:T(8,128)(2,1)S(1)}, bf16[28,128,128]{2,1,0:T(8,128)(2,1)S(1)}) custom-call(s32[4]{0:T(128)S(1)} %pad_add_fusion.where_ref, s32[3]{0:T(128)S(1)} %bitcast.34, s32[2,112]{1,0:T(2,128)S(1)} %bitcast.54, ...), custom_call_target="tpu_custom_call" | custom-call | flops 2550136832 | bytes 12058624 | tf_op jit(solution)/shard_map/pallas_call | solution.py:29
  76.2 8.8 %shard_map.132.y_ref.r0 = bf16[2,28,128,128]{3,2,1,0:T(8,128)(2,1)S(1)} custom-call(s32[4]{0:T(128)S(1)} %pad_add_fusion.where_ref, s32[3]{0:T(128)S(1)} %bitcast.35, s32[2,112]{1,0:T(2,128)S(1)} %bitcast.44, bf16[128,4096]{1,0:T(8,128)(2,1)S(1)} %copy-done, f32[28,128,128]{2,1,0:T(8,128)S(1)} %get-tuple-element.26.silu_ref, ...), custom_call_target="tpu_custom_call" | custom-call | flops 3758096384 | bytes 10223616 | tf_op jit(solution)/shard_map/pallas_call | solution.py:29
  85.1 0.5 collective-permute-start.22
  85.7 0.3 shard_map.134.l0
  86.0 0.5 collective-permute-start.21
  86.5 7.8 %shard_map.131 = (bf16[128,1024]{1,0:T(8,128)(2,1)S(1)}, bf16[128,1024]{1,0:T(8,128)(2,1)S(1)}, bf16[128,1024]{1,0:T(8,128)(2,1)S(1)}, bf16[128,1024]{1,0:T(8,128)(2,1)S(1)}) custom-call(s32[4]{0:T(128)S(1)} %pad_add_fusion.where_ref, s32[3]{0:T(128)S(1)} %bitcast.36, s32[2,112]{1,0:T(2,128)S(1)} %bitcast.45, ...), custom_call_target="tpu_custom_call" | custom-call | flops 3758096384 | bytes 5636096 | tf_op jit(solution)/shard_map/pallas_call | solution.py:29
  94.5 2.0 %collective-permute-start.15 = (bf16[128,1024]{1,0:T(8,128)(2,1)S(1)}, bf16[128,1024]{1,0:T(8,128)(2,1)S(1)}, u32[]{:S(2)}, u32[]{:S(2)}) collective-permute-start(bf16[128,1024]{1,0:T(8,128)(2,1)S(1)} %get-tuple-element.23), channel_id=1, source_target_pairs={{0,1},{1,2},{2,3},{3,0},{4,5},{5,6},{6,7},{7,4},{8,9},{9,10},{10,1... | collective-permute-start | bytes 786440 | tf_op jit(solution)/shard_map/ppermute | solution.py:105
  96.5 11.0 %shard_map.133 = (bf16[128,1024]{1,0:T(8,128)(2,1)S(1)}, bf16[128,1024]{1,0:T(8,128)(2,1)S(1)}, bf16[128,1024]{1,0:T(8,128)(2,1)S(1)}, bf16[128,1024]{1,0:T(8,128)(2,1)S(1)}) custom-call(s32[4]{0:T(128)S(1)} %pad_add_fusion.where_ref, s32[3]{0:T(128)S(1)} %bitcast.37, s32[2,112]{1,0:T(2,128)S(1)} %bitcast.50, s32[2,112]{1,0:T(2,128)S(1)} %bitcast.55, ...), custom_call_target="tpu_custom_call" | custom-call | flops 7516192768 | bytes 10223616 | tf_op jit(solution)/shard_map/pallas_call | solution.py:29
  107.5 2.4 %shard_map.140 = bf16[28,128,128]{2,1,0:T(8,128)(2,1)S(1)} custom-call(s32[4]{0:T(128)S(1)} %pad_add_fusion.where_ref, s32[3]{0:T(128)S(1)} %bitcast.38, s32[2,112]{1,0:T(2,128)S(1)} %bitcast.46, bf16[28,128,128]{2,1,0:T(8,128)(2,1)S(1)} %get-tuple-element.32.l0, bf16[28,128,128]{2,1,0:T(8,128)(2,1)S(1)} %collective-permute-done.25.l1, ...), custom_call_target="tpu_custom_call" | custom-call | flops 939524096 | bytes 4849664 | tf_op jit(solution)/shard_map/pallas_call | solution.py:29
  109.9 1.4 collective-permute-start.20
  111.3 4.8 %collective-permute-start.27 = (bf16[28,128,128]{2,1,0:T(8,128)(2,1)S(1)}, bf16[28,128,128]{2,1,0:T(8,128)(2,1)S(1)}, u32[]{:S(2)}, u32[]{:S(2)}) collective-permute-start(bf16[28,128,128]{2,1,0:T(8,128)(2,1)S(1)} %shard_map.140), channel_id=1, source_target_pairs={{0,8},{4,12},{8,0},{12,4},{1,9},{5,13},{9,1},{13,5},{2,10},{6,14},... | collective-permute-start | bytes 2752520 | tf_op jit(solution)/shard_map/ppermute | solution.py:97
  116.1 2.1 %shard_map.136 = bf16[28,128,128]{2,1,0:T(8,128)(2,1)S(1)} custom-call(s32[4]{0:T(128)S(1)} %pad_add_fusion.where_ref, s32[3]{0:T(128)S(1)} %bitcast.39, s32[2,112]{1,0:T(2,128)S(1)} %bitcast.51, bf16[32,128,128]{2,1,0:T(8,128)(2,1)S(1)} %shard_map.134.l0, bf16[32,128,128]{2,1,0:T(8,128)(2,1)S(1)} %collective-permute-done.21.l1, ...), custom_call_target="tpu_custom_call" | custom-call | flops 939524096 | bytes 6684672 | tf_op jit(solution)/shard_map/pallas_call | solution.py:29
  118.4 0.8 collective-permute-start.18
  119.2 2.1 %collective-permute-start.23 = (bf16[28,128,128]{2,1,0:T(8,128)(2,1)S(1)}, bf16[28,128,128]{2,1,0:T(8,128)(2,1)S(1)}, u32[]{:S(2)}, u32[]{:S(2)}) collective-permute-start(bf16[28,128,128]{2,1,0:T(8,128)(2,1)S(1)} %shard_map.136), channel_id=1, source_target_pairs={{0,8},{4,12},{8,0},{12,4},{1,9},{5,13},{9,1},{13,5},{2,10},{6,14},... | collective-permute-start | bytes 2752520 | tf_op jit(solution)/shard_map/ppermute | solution.py:97
  121.3 0.9 add_convert_fusion.4
  122.2 0.7 shard_map.138
  123.2 2.8 %collective-permute-start.24 = (bf16[28,128,128]{2,1,0:T(8,128)(2,1)S(1)}, bf16[28,128,128]{2,1,0:T(8,128)(2,1)S(1)}, u32[]{:S(2)}, u32[]{:S(2)}) collective-permute-start(bf16[28,128,128]{2,1,0:T(8,128)(2,1)S(1)} %shard_map.138), channel_id=1, source_target_pairs={{0,8},{4,12},{8,0},{12,4},{1,9},{5,13},{9,1},{13,5},{2,10},{6,14},... | collective-permute-start | bytes 2752520 | tf_op jit(solution)/shard_map/ppermute | solution.py:97
  126.1 14.0 %collective-permute-done.19 = bf16[128,1024]{1,0:T(8,128)(2,1)S(1)} collective-permute-done((bf16[128,1024]{1,0:T(8,128)(2,1)S(1)}, bf16[128,1024]{1,0:T(8,128)(2,1)S(1)}, u32[]{:S(2)}, u32[]{:S(2)}) %collective-permute-start.19) | collective-permute-done | bytes 262176 | tf_op jit(solution)/shard_map/ppermute | solution.py:105
  140.1 0.9 add_convert_fusion.3
  140.9 2.4 %shard_map.139 = bf16[28,128,128]{2,1,0:T(8,128)(2,1)S(1)} custom-call(s32[4]{0:T(128)S(1)} %pad_add_fusion.where_ref, s32[3]{0:T(128)S(1)} %bitcast.41, s32[2,112]{1,0:T(2,128)S(1)} %bitcast.47, bf16[28,128,128]{2,1,0:T(8,128)(2,1)S(1)} %get-tuple-element.32.l0, bf16[28,128,128]{2,1,0:T(8,128)(2,1)S(1)} %collective-permute-done.25.l1, ...), custom_call_target="tpu_custom_call" | custom-call | flops 939524096 | bytes 4849664 | tf_op jit(solution)/shard_map/pallas_call | solution.py:29
  143.3 2.1 %shard_map.135 = bf16[28,128,128]{2,1,0:T(8,128)(2,1)S(1)} custom-call(s32[4]{0:T(128)S(1)} %pad_add_fusion.where_ref, s32[3]{0:T(128)S(1)} %bitcast.42, s32[2,112]{1,0:T(2,128)S(1)} %bitcast.52, bf16[32,128,128]{2,1,0:T(8,128)(2,1)S(1)} %shard_map.134.l0, bf16[32,128,128]{2,1,0:T(8,128)(2,1)S(1)} %collective-permute-done.21.l1, ...), custom_call_target="tpu_custom_call" | custom-call | flops 939524096 | bytes 6684672 | tf_op jit(solution)/shard_map/pallas_call | solution.py:29
  145.4 2.1 %shard_map.137 = bf16[28,128,128]{2,1,0:T(8,128)(2,1)S(1)} custom-call(s32[4]{0:T(128)S(1)} %pad_add_fusion.where_ref, s32[3]{0:T(128)S(1)} %bitcast.43, s32[2,112]{1,0:T(2,128)S(1)} %bitcast.57, bf16[32,128,128]{2,1,0:T(8,128)(2,1)S(1)} %shard_map.134.l0, bf16[32,128,128]{2,1,0:T(8,128)(2,1)S(1)} %collective-permute-done.21.l1, ...), custom_call_target="tpu_custom_call" | custom-call | flops 939524096 | bytes 6684672 | tf_op jit(solution)/shard_map/pallas_call | solution.py:29
  147.6 1.2 fusion.2
  148.8 8.1 %collective-permute-done.23 = bf16[28,128,128]{2,1,0:T(8,128)(2,1)S(1)} collective-permute-done((bf16[28,128,128]{2,1,0:T(8,128)(2,1)S(1)}, bf16[28,128,128]{2,1,0:T(8,128)(2,1)S(1)}, u32[]{:S(2)}, u32[]{:S(2)}) %collective-permute-start.23) | collective-permute-done | bytes 917536 | tf_op jit(solution)/shard_map/ppermute | solution.py:97
  157.0 1.2 fusion
  158.2 15.7 %collective-permute-done.24 = bf16[28,128,128]{2,1,0:T(8,128)(2,1)S(1)} collective-permute-done((bf16[28,128,128]{2,1,0:T(8,128)(2,1)S(1)}, bf16[28,128,128]{2,1,0:T(8,128)(2,1)S(1)}, u32[]{:S(2)}, u32[]{:S(2)}) %collective-permute-start.24) | collective-permute-done | bytes 917536 | tf_op jit(solution)/shard_map/ppermute | solution.py:97
  173.9 1.2 fusion.1
  (58 shorter events, 1.4 us)
Async XLA Ops:
  0.6 5.9 %copy-start.2 = (bf16[1,28,128,128]{3,2,1,0:T(8,128)(2,1)S(1)}, bf16[1,28,128,128]{3,2,1,0:T(8,128)(2,1)}, u32[]{:S(2)}) copy-start(bf16[1,28,128,128]{3,2,1,0:T(8,128)(2,1)} %param.13) | copy-start | bytes 2752516
  0.6 58.0 %copy-start.7 = (s32[3,1]{0,1:T(1,128)S(1)}, s32[3,1]{0,1:T(1,128)}, u32[]{:S(2)}) copy-start(s32[3,1]{0,1:T(1,128)} %param.17) | copy-start | bytes 40
  0.7 58.0 %copy-start.10 = (s32[2,1,112]{2,1,0:T(1,128)S(1)}, s32[2,1,112]{2,1,0:T(1,128)}, u32[]{:S(2)}) copy-start(s32[2,1,112]{2,1,0:T(1,128)} %param.15) | copy-start | bytes 2692
  0.7 58.0 %copy-start.9 = (s32[2,1,112]{2,1,0:T(1,128)S(1)}, s32[2,1,112]{2,1,0:T(1,128)}, u32[]{:S(2)}) copy-start(s32[2,1,112]{2,1,0:T(1,128)} %param.14) | copy-start | bytes 2692
  0.7 58.0 %copy-start.1 = (bf16[128,4096]{1,0:T(8,128)(2,1)S(1)}, bf16[128,4096]{1,0:T(8,128)(2,1)}, u32[]{:S(2)}) copy-start(bf16[128,4096]{1,0:T(8,128)(2,1)} %t_ref.1) | copy-start | bytes 3145732
  0.7 36.9 %collective-permute-start = (bf16[28,128,128]{2,1,0:T(8,128)(2,1)}, bf16[28,128,128]{2,1,0:T(8,128)(2,1)S(1)}, u32[]{:S(2)}, u32[]{:S(2)}) collective-permute-start(bf16[28,128,128]{2,1,0:T(8,128)(2,1)} %bitcast.26), channel_id=1, source_target_pairs={{0,4},{4,0},{8,12},{12,8},{1,5},{5,1},{9,13},{13,9},{2,6},{6,2},{1... | collective-permute-start | bytes 2752520 | tf_op jit(solution)/shard_map/ppermute | solution.py:94
  2.3 14.0 %collective-permute-start.2 = (bf16[14,128,128]{2,1,0:T(8,128)(2,1)S(1)}, bf16[14,128,128]{2,1,0:T(8,128)(2,1)S(1)}, u32[]{:S(2)}, u32[]{:S(2)}) collective-permute-start(bf16[14,128,128]{2,1,0:T(8,128)(2,1)S(1)} %dynamic-slice_bitcast_fusion.2), channel_id=1, source_target_pairs={{0,8},{4,12},{8,0},{12,4},{1,9},{5,13},{9,1},{13,5},{2,10},{6,14},... | collective-permute-start | bytes 1376264 | tf_op jit(solution)/shard_map/ppermute | solution.py:97
  5.0 32.8 %collective-permute-start.1 = (bf16[28,128,128]{2,1,0:T(8,128)(2,1)}, bf16[28,128,128]{2,1,0:T(8,128)(2,1)S(1)}, u32[]{:S(2)}, u32[]{:S(2)}) collective-permute-start(bf16[28,128,128]{2,1,0:T(8,128)(2,1)} %bitcast.29), channel_id=1, source_target_pairs={{0,4},{4,0},{8,12},{12,8},{1,5},{5,1},{9,13},{13,9},{2,6},{6,2},{1... | collective-permute-start | bytes 2752520 | tf_op jit(solution)/shard_map/ppermute | solution.py:94
  6.1 20.2 %collective-permute-start.6 = (bf16[14,128,128]{2,1,0:T(8,128)(2,1)S(1)}, bf16[14,128,128]{2,1,0:T(8,128)(2,1)}, u32[]{:S(2)}, u32[]{:S(2)}) collective-permute-start(bf16[14,128,128]{2,1,0:T(8,128)(2,1)S(1)} %dynamic-slice_bitcast_fusion.1), channel_id=1, source_target_pairs={{0,8},{4,12},{8,0},{12,4},{1,9},{5,13},{9,1},{13,5},{2,10},{6,14},... | collective-permute-start | bytes 1376264 | tf_op jit(solution)/shard_map/ppermute | solution.py:97
  6.6 29.2 %collective-permute-start.11 = (bf16[14,128,128]{2,1,0:T(8,128)(2,1)S(1)}, bf16[14,128,128]{2,1,0:T(8,128)(2,1)}, u32[]{:S(2)}, u32[]{:S(2)}) collective-permute-start(bf16[14,128,128]{2,1,0:T(8,128)(2,1)S(1)} %dynamic-slice_bitcast_fusion), channel_id=1, source_target_pairs={{0,8},{4,12},{8,0},{12,4},{1,9},{5,13},{9,1},{13,5},{2,10},{6,14},... | collective-permute-start | bytes 1376264 | tf_op jit(solution)/shard_map/ppermute | solution.py:97
  16.3 21.5 %collective-permute-start.4 = (bf16[14,128,128]{2,1,0:T(8,128)(2,1)S(1)}, bf16[14,128,128]{2,1,0:T(8,128)(2,1)}, u32[]{:S(2)}, u32[]{:S(2)}) collective-permute-start(bf16[14,128,128]{2,1,0:T(8,128)(2,1)S(1)} %collective-permute-done.2.refs_0_.refs_2_), channel_id=1, source_target_pairs={{0,16},{16,0},{1,17},{17,1},{2,18},{18,2},{3,19},{19,3},{4,20},{20... | collective-permute-start | bytes 1376264 | tf_op jit(solution)/shard_map/ppermute | solution.py:102
  26.3 13.1 %collective-permute-start.3 = (bf16[14,128,128]{2,1,0:T(8,128)(2,1)S(1)}, bf16[14,128,128]{2,1,0:T(8,128)(2,1)}, u32[]{:S(2)}, u32[]{:S(2)}) collective-permute-start(bf16[14,128,128]{2,1,0:T(8,128)(2,1)S(1)} %collective-permute-done.2.refs_0_.refs_2_), channel_id=1, source_target_pairs={{0,4},{4,0},{8,12},{12,8},{1,5},{5,1},{9,13},{13,9},{2,6},{6,2},{1... | collective-permute-start | bytes 1376264 | tf_op jit(solution)/shard_map/ppermute | solution.py:94
  35.8 13.7 %collective-permute-start.8 = (bf16[14,128,128]{2,1,0:T(8,128)(2,1)}, bf16[14,128,128]{2,1,0:T(8,128)(2,1)}, u32[]{:S(2)}, u32[]{:S(2)}) collective-permute-start(bf16[14,128,128]{2,1,0:T(8,128)(2,1)} %collective-permute-done.6.refs_0_.refs_8_), channel_id=1, source_target_pairs={{0,16},{16,0},{1,17},{17,1},{2,18},{18,2},{3,19},{19,3},{4,20},{20... | collective-permute-start | bytes 1376264 | tf_op jit(solution)/shard_map/ppermute | solution.py:102
  37.5 20.6 %collective-permute-start.13 = (bf16[14,128,128]{2,1,0:T(8,128)(2,1)}, bf16[14,128,128]{2,1,0:T(8,128)(2,1)}, u32[]{:S(2)}, u32[]{:S(2)}) collective-permute-start(bf16[14,128,128]{2,1,0:T(8,128)(2,1)} %collective-permute-done.11.refs_2_), channel_id=1, source_target_pairs={{0,16},{16,0},{1,17},{17,1},{2,18},{18,2},{3,19},{19,3},{4,20},{20... | collective-permute-start | bytes 1376264 | tf_op jit(solution)/shard_map/ppermute | solution.py:102
  37.8 20.3 %collective-permute-start.5 = (bf16[14,128,128]{2,1,0:T(8,128)(2,1)}, bf16[14,128,128]{2,1,0:T(8,128)(2,1)}, u32[]{:S(2)}, u32[]{:S(2)}) collective-permute-start(bf16[14,128,128]{2,1,0:T(8,128)(2,1)} %collective-permute-done.4.refs_2_.refs_4_), channel_id=1, source_target_pairs={{0,4},{4,0},{8,12},{12,8},{1,5},{5,1},{9,13},{13,9},{2,6},{6,2},{1... | collective-permute-start | bytes 1376264 | tf_op jit(solution)/shard_map/ppermute | solution.py:94
  37.8 0.9 copy-start.11
  38.7 37.5 %collective-permute-start.10 = (bf16[28,128,128]{2,1,0:T(8,128)(2,1)S(1)}, bf16[28,128,128]{2,1,0:T(8,128)(2,1)}, u32[]{:S(2)}, u32[]{:S(2)}) collective-permute-start(bf16[28,128,128]{2,1,0:T(8,128)(2,1)S(1)} %bitcast.23), channel_id=1, source_target_pairs={{0,4},{4,0},{8,12},{12,8},{1,5},{5,1},{9,13},{13,9},{2,6},{6,2},{1... | collective-permute-start | bytes 2752520 | tf_op jit(solution)/shard_map/ppermute | solution.py:94
  39.3 32.9 %collective-permute-start.7 = (bf16[14,128,128]{2,1,0:T(8,128)(2,1)}, bf16[14,128,128]{2,1,0:T(8,128)(2,1)S(1)}, u32[]{:S(2)}, u32[]{:S(2)}) collective-permute-start(bf16[14,128,128]{2,1,0:T(8,128)(2,1)} %collective-permute-done.6.refs_0_.refs_8_), channel_id=1, source_target_pairs={{0,4},{4,0},{8,12},{12,8},{1,5},{5,1},{9,13},{13,9},{2,6},{6,2},{1... | collective-permute-start | bytes 1376264 | tf_op jit(solution)/shard_map/ppermute | solution.py:94
  49.5 26.7 %collective-permute-start.12 = (bf16[14,128,128]{2,1,0:T(8,128)(2,1)}, bf16[14,128,128]{2,1,0:T(8,128)(2,1)S(1)}, u32[]{:S(2)}, u32[]{:S(2)}) collective-permute-start(bf16[14,128,128]{2,1,0:T(8,128)(2,1)} %collective-permute-done.11.refs_2_), channel_id=1, source_target_pairs={{0,4},{4,0},{8,12},{12,8},{1,5},{5,1},{9,13},{13,9},{2,6},{6,2},{1... | collective-permute-start | bytes 1376264 | tf_op jit(solution)/shard_map/ppermute | solution.py:94
  58.1 14.2 %collective-permute-start.9 = (bf16[14,128,128]{2,1,0:T(8,128)(2,1)}, bf16[14,128,128]{2,1,0:T(8,128)(2,1)S(1)}, u32[]{:S(2)}, u32[]{:S(2)}) collective-permute-start(bf16[14,128,128]{2,1,0:T(8,128)(2,1)} %collective-permute-done.8.refs_2_.refs_10_), channel_id=1, source_target_pairs={{0,4},{4,0},{8,12},{12,8},{1,5},{5,1},{9,13},{13,9},{2,6},{6,2},{1... | collective-permute-start | bytes 1376264 | tf_op jit(solution)/shard_map/ppermute | solution.py:94
  58.1 18.1 %collective-permute-start.14 = (bf16[14,128,128]{2,1,0:T(8,128)(2,1)}, bf16[14,128,128]{2,1,0:T(8,128)(2,1)S(1)}, u32[]{:S(2)}, u32[]{:S(2)}) collective-permute-start(bf16[14,128,128]{2,1,0:T(8,128)(2,1)} %collective-permute-done.13.refs_4_), channel_id=1, source_target_pairs={{0,4},{4,0},{8,12},{12,8},{1,5},{5,1},{9,13},{13,9},{2,6},{6,2},{1... | collective-permute-start | bytes 1376264 | tf_op jit(solution)/shard_map/ppermute | solution.py:94
  58.7 1.2 copy-start.3
  59.8 1.2 copy-start.5
  61.0 1.2 copy-start.12
  67.4 4.8 %copy-start = (bf16[128,4096]{1,0:T(8,128)(2,1)S(1)}, bf16[128,4096]{1,0:T(8,128)(2,1)}, u32[]{:S(2)}) copy-start(bf16[128,4096]{1,0:T(8,128)(2,1)} %r0.3) | copy-start | bytes 3145732
  72.3 22.1 %collective-permute-start.26 = (bf16[128,4096]{1,0:T(8,128)(2,1)S(1)}, bf16[128,4096]{1,0:T(8,128)(2,1)S(1)}, u32[]{:S(2)}, u32[]{:S(2)}) collective-permute-start(bf16[128,4096]{1,0:T(8,128)(2,1)S(1)} %copy-done), channel_id=1, source_target_pairs={{0,4},{4,0},{8,12},{12,8},{1,5},{5,1},{9,13},{13,9},{2,6},{6,2},{1... | collective-permute-start | bytes 3145736 | tf_op jit(solution)/shard_map/ppermute | solution.py:94
  72.4 3.8 %copy-start.8 = (s32[2,1,112]{2,1,0:T(1,128)S(1)}, s32[2,1,112]{2,1,0:T(1,128)}, u32[]{:S(2)}) copy-start(s32[2,1,112]{2,1,0:T(1,128)} %param.16) | copy-start | bytes 2692
  85.1 26.2 %collective-permute-start.22 = (bf16[2,28,128,128]{3,2,1,0:T(8,128)(2,1)S(1)}, bf16[2,28,128,128]{3,2,1,0:T(8,128)(2,1)S(1)}, u32[]{:S(2)}, u32[]{:S(2)}) collective-permute-start(bf16[2,28,128,128]{3,2,1,0:T(8,128)(2,1)S(1)} %shard_map.132.y_ref.r0), channel_id=1, source_target_pairs={{0,4},{4,0},{8,12},{12,8},{1,5},{5,1},{9,13},{13,9},{2,6},{6,2},{1... | collective-permute-start | bytes 5505032 | tf_op jit(solution)/shard_map/ppermute | solution.py:94
  85.6 8.9 %collective-permute-start.25 = (bf16[28,128,128]{2,1,0:T(8,128)(2,1)S(1)}, bf16[28,128,128]{2,1,0:T(8,128)(2,1)S(1)}, u32[]{:S(2)}, u32[]{:S(2)}) collective-permute-start(bf16[28,128,128]{2,1,0:T(8,128)(2,1)S(1)} %get-tuple-element.32.l0), channel_id=1, source_target_pairs={{0,4},{4,0},{8,12},{12,8},{1,5},{5,1},{9,13},{13,9},{2,6},{6,2},{1... | collective-permute-start | bytes 2752520 | tf_op jit(solution)/shard_map/ppermute | solution.py:94
  86.0 23.8 %collective-permute-start.21 = (bf16[32,128,128]{2,1,0:T(8,128)(2,1)S(1)}, bf16[32,128,128]{2,1,0:T(8,128)(2,1)S(1)}, u32[]{:S(2)}, u32[]{:S(2)}) collective-permute-start(bf16[32,128,128]{2,1,0:T(8,128)(2,1)S(1)} %shard_map.134.l0), channel_id=1, source_target_pairs={{0,4},{4,0},{8,12},{12,8},{1,5},{5,1},{9,13},{13,9},{2,6},{6,2},{1... | collective-permute-start | bytes 3145736 | tf_op jit(solution)/shard_map/ppermute | solution.py:94
  86.5 10.0 %copy-start.4 = (bf16[1,28,128,128]{3,2,1,0:T(8,128)(2,1)S(1)}, bf16[1,28,128,128]{3,2,1,0:T(8,128)(2,1)}, u32[]{:S(2)}) copy-start(bf16[1,28,128,128]{3,2,1,0:T(8,128)(2,1)} %param.11) | copy-start | bytes 2752516
  86.5 10.0 %copy-start.6 = (bf16[1,28,128,128]{3,2,1,0:T(8,128)(2,1)S(1)}, bf16[1,28,128,128]{3,2,1,0:T(8,128)(2,1)}, u32[]{:S(2)}) copy-start(bf16[1,28,128,128]{3,2,1,0:T(8,128)(2,1)} %param.12) | copy-start | bytes 2752516
  86.5 10.0 %copy-start.13 = (bf16[28,128,128]{2,1,0:T(8,128)(2,1)S(1)}, bf16[28,128,128]{2,1,0:T(8,128)(2,1)}, u32[]{:S(2)}) copy-start(bf16[28,128,128]{2,1,0:T(8,128)(2,1)} %copy-done.11) | copy-start | bytes 2752516
  94.4 23.8 %collective-permute-start.17 = (bf16[128,1024]{1,0:T(8,128)(2,1)S(1)}, bf16[128,1024]{1,0:T(8,128)(2,1)S(1)}, u32[]{:S(2)}, u32[]{:S(2)}) collective-permute-start(bf16[128,1024]{1,0:T(8,128)(2,1)S(1)} %get-tuple-element.25), channel_id=1, source_target_pairs={{0,3},{1,0},{2,1},{3,2},{4,7},{5,4},{6,5},{7,6},{8,11},{9,8},{10,9... | collective-permute-start | bytes 786440 | tf_op jit(solution)/shard_map/ppermute | solution.py:105
  94.4 24.0 %collective-permute-start.16 = (bf16[128,1024]{1,0:T(8,128)(2,1)S(1)}, bf16[128,1024]{1,0:T(8,128)(2,1)S(1)}, u32[]{:S(2)}, u32[]{:S(2)}) collective-permute-start(bf16[128,1024]{1,0:T(8,128)(2,1)S(1)} %get-tuple-element.24), channel_id=1, source_target_pairs={{0,2},{1,3},{2,0},{3,1},{4,6},{5,7},{6,4},{7,5},{8,10},{9,11},{10,... | collective-permute-start | bytes 786440 | tf_op jit(solution)/shard_map/ppermute | solution.py:105
  94.5 24.7 %collective-permute-start.15 = (bf16[128,1024]{1,0:T(8,128)(2,1)S(1)}, bf16[128,1024]{1,0:T(8,128)(2,1)S(1)}, u32[]{:S(2)}, u32[]{:S(2)}) collective-permute-start(bf16[128,1024]{1,0:T(8,128)(2,1)S(1)} %get-tuple-element.23), channel_id=1, source_target_pairs={{0,1},{1,2},{2,3},{3,0},{4,5},{5,6},{6,7},{7,4},{8,9},{9,10},{10,1... | collective-permute-start | bytes 786440 | tf_op jit(solution)/shard_map/ppermute | solution.py:105
  109.9 13.4 %collective-permute-start.20 = (bf16[128,1024]{1,0:T(8,128)(2,1)S(1)}, bf16[128,1024]{1,0:T(8,128)(2,1)S(1)}, u32[]{:S(2)}, u32[]{:S(2)}) collective-permute-start(bf16[128,1024]{1,0:T(8,128)(2,1)S(1)} %get-tuple-element.31), channel_id=1, source_target_pairs={{0,3},{1,0},{2,1},{3,2},{4,7},{5,4},{6,5},{7,6},{8,11},{9,8},{10,9... | collective-permute-start | bytes 786440 | tf_op jit(solution)/shard_map/ppermute | solution.py:105
  111.3 36.3 %collective-permute-start.27 = (bf16[28,128,128]{2,1,0:T(8,128)(2,1)S(1)}, bf16[28,128,128]{2,1,0:T(8,128)(2,1)S(1)}, u32[]{:S(2)}, u32[]{:S(2)}) collective-permute-start(bf16[28,128,128]{2,1,0:T(8,128)(2,1)S(1)} %shard_map.140), channel_id=1, source_target_pairs={{0,8},{4,12},{8,0},{12,4},{1,9},{5,13},{9,1},{13,5},{2,10},{6,14},... | collective-permute-start | bytes 2752520 | tf_op jit(solution)/shard_map/ppermute | solution.py:97
  118.2 21.9 %collective-permute-start.19 = (bf16[128,1024]{1,0:T(8,128)(2,1)S(1)}, bf16[128,1024]{1,0:T(8,128)(2,1)S(1)}, u32[]{:S(2)}, u32[]{:S(2)}) collective-permute-start(bf16[128,1024]{1,0:T(8,128)(2,1)S(1)} %get-tuple-element.30), channel_id=1, source_target_pairs={{0,2},{1,3},{2,0},{3,1},{4,6},{5,7},{6,4},{7,5},{8,10},{9,11},{10,... | collective-permute-start | bytes 786440 | tf_op jit(solution)/shard_map/ppermute | solution.py:105
  118.4 21.6 %collective-permute-start.18 = (bf16[128,1024]{1,0:T(8,128)(2,1)S(1)}, bf16[128,1024]{1,0:T(8,128)(2,1)S(1)}, u32[]{:S(2)}, u32[]{:S(2)}) collective-permute-start(bf16[128,1024]{1,0:T(8,128)(2,1)S(1)} %get-tuple-element.29), channel_id=1, source_target_pairs={{0,1},{1,2},{2,3},{3,0},{4,5},{5,6},{6,7},{7,4},{8,9},{9,10},{10,1... | collective-permute-start | bytes 786440 | tf_op jit(solution)/shard_map/ppermute | solution.py:105
  119.2 37.8 %collective-permute-start.23 = (bf16[28,128,128]{2,1,0:T(8,128)(2,1)S(1)}, bf16[28,128,128]{2,1,0:T(8,128)(2,1)S(1)}, u32[]{:S(2)}, u32[]{:S(2)}) collective-permute-start(bf16[28,128,128]{2,1,0:T(8,128)(2,1)S(1)} %shard_map.136), channel_id=1, source_target_pairs={{0,8},{4,12},{8,0},{12,4},{1,9},{5,13},{9,1},{13,5},{2,10},{6,14},... | collective-permute-start | bytes 2752520 | tf_op jit(solution)/shard_map/ppermute | solution.py:97
  123.2 50.7 %collective-permute-start.24 = (bf16[28,128,128]{2,1,0:T(8,128)(2,1)S(1)}, bf16[28,128,128]{2,1,0:T(8,128)(2,1)S(1)}, u32[]{:S(2)}, u32[]{:S(2)}) collective-permute-start(bf16[28,128,128]{2,1,0:T(8,128)(2,1)S(1)} %shard_map.138), channel_id=1, source_target_pairs={{0,8},{4,12},{8,0},{12,4},{1,9},{5,13},{9,1},{13,5},{2,10},{6,14},... | collective-permute-start | bytes 2752520 | tf_op jit(solution)/shard_map/ppermute | solution.py:97

commit v2 on v1

v2 whole, which is shorter than its diff:
```python
import functools

import jax
import jax.numpy as jnp
from jax import lax
from jax.experimental import pallas as pl
from jax.experimental.pallas import tpu as pltpu
from jax.sharding import PartitionSpec as P

FF = 14336
F32 = jnp.float32
BF16 = jnp.bfloat16
UNROLL = 4
NN = (((1,), (0,)), ((), ()))
NT = (((1,), (1,)), ((), ()))
TN = (((0,), (0,)), ((), ()))

VMEM = pl.BlockSpec(memory_space=pltpu.VMEM)
SMEM = pl.BlockSpec(memory_space=pltpu.SMEM)


def mm(left, right, dims=NN):
    return lax.dot_general(left, right, dims, preferred_element_type=F32)


def call(body, ints, arrays, outs, scratch=(), products=0, aliases=None):
    size = lambda a: a.size * a.dtype.itemsize
    total = sum(size(a) for a in arrays) + sum(size(o) for o in outs)
    held = total + sum(s.inner_aval.size * s.inner_aval.dtype.itemsize if hasattr(s, "inner_aval") else 0 for s in scratch)
    return pl.pallas_call(
        body,
        out_shape=outs,
        in_specs=[SMEM] * len(ints) + [VMEM] * len(arrays),
        out_specs=[VMEM] * len(outs),
        scratch_shapes=list(scratch),
        input_output_aliases=aliases or {},
        compiler_params=pltpu.CompilerParams(vmem_limit_bytes=held + (12 << 20)),
        cost_estimate=pl.CostEstimate(
            flops=products, bytes_accessed=products, transcendentals=0
        ),
    )(*ints, *arrays)


class Place:
    def __init__(self, chips, parts, groups, shard):
        self.chips, self.parts, self.groups, self.shard = chips, parts, groups, shard

    def first(self, where, piece):
        chip, core, part = where[0], where[1], where[2]
        back, other, half = piece
        chip = lax.rem(chip + (self.chips - back), self.chips)
        core = 1 - core if other else core
        start = (chip * 2 + core) * self.shard
        if half is not None:
            start = start + (1 - part if half else part) * (self.shard // 2)
        return start


def over_live(live, terms, store):
    def several(step, _):
        slots = [step * UNROLL + u for u in range(UNROLL)]
        values = [terms(slot) for slot in slots]
        for slot, value in zip(slots, values):
            store(slot, value)
        return 0

    def single(slot, _):
        store(slot, terms(slot))
        return 0

    rounds = lax.div(live, UNROLL)
    lax.fori_loop(0, rounds, several, 0)
    lax.fori_loop(rounds * UNROLL, live, single, 0)


def live_in(count, first, extent):
    return jnp.clip(count - first, 0, extent)


def columns(block, size=128):
    return pl.ds(pl.multiple_of(block * size, size), size)


def after(value, *others):
    return lax.optimization_barrier((value, others))[0]


def zero(acc):
    acc[...] = jnp.zeros(acc.shape, acc.dtype)


def make(mesh):
    parts = mesh.shape["parts"]
    dp = mesh.shape["dp"]
    groups = mesh.shape["tensor"]
    chips = dp // 2

    def pair_swap(a, name):
        with jax.named_scope(name + "_core"):
            return lax.ppermute(a, "dp", [(i, i ^ 1) for i in range(dp)])

    def chip_shift(a, k, name):
        with jax.named_scope(name + "_chip"):
            return lax.ppermute(
                a, "dp", [(i, ((i // 2 + k) % chips) * 2 + i % 2) for i in range(dp)]
            )

    def part_swap(a, name):
        with jax.named_scope(name + "_part"):
            return lax.ppermute(a, "parts", [(0, 1), (1, 0)])

    def group_swap(a, bit, name):
        with jax.named_scope(name + "_group"):
            return lax.ppermute(a, "tensor", [(i, i ^ bit) for i in range(groups)])

    def per_device(
        tokens, cotangent, gate_blocks, up_blocks, down_blocks, gate_index, up_index, down_index, block_counts
    ):
        token_count, model_width = tokens.shape
        size = gate_blocks.shape[2]
        shard = gate_blocks.shape[1]
        model_blocks = model_width // size
        hidden_blocks = FF // size // groups
        halves = parts == 2 and shard % 2 == 0
        place = Place(chips, parts, groups, shard)
        at = lax.axis_index("dp")
        part = lax.axis_index("parts")
        where = jnp.stack([at // 2, at % 2, part, lax.axis_index("tensor")]).astype(jnp.int32)
        tables = [gate_index[:, 0], up_index[:, 0], down_index[:, 0]]
        counts = block_counts[:, 0]

        hidden_f32 = jax.ShapeDtypeStruct((hidden_blocks, token_count, size), F32)
        hidden_bf16 = jax.ShapeDtypeStruct((hidden_blocks, token_count, size), BF16)

        own = [gate_blocks[0], up_blocks[0], down_blocks[0]]
        near_keys = [(0, False, None), (0, True, None)]
        away = tuple(range(1, chips))
        near_half, far_half = (False, True) if halves else (None, None)
        direct_keys = [(k, other, near_half) for k in away for other in (False, True)]
        relay_keys = [(k, other, far_half) for k in away for other in (False, True)] if halves else []
        all_keys = near_keys + direct_keys + relay_keys
        cut = own
        if halves:
            cut = [
                lax.dynamic_slice_in_dim(w, part * (shard // 2), shard // 2, 0) for w in own
            ]

        def shift_all(name, blocks, *others):
            arrived = []
            for k in away:
                arrived.append(chip_shift(after(blocks, *others), k, name))
                others = arrived[-1:]
            return arrived

        names = ("gate", "up", "down")
        near = [[w, pair_swap(w, name)] for w, name in zip(own[:2], names)]

        def both(name, pieces):
            return [q for w in pieces for q in (w, pair_swap(w, name))]

        def add_pieces(acc, m, x_ref, w_refs, piece_keys, table, counts_ref, where_ref):
            for w_ref, key in zip(w_refs, piece_keys):
                first = place.first(where_ref, key)

                def terms(s, w_ref=w_ref, first=first):
                    return mm(x_ref[:, columns(table[0, first + s])], w_ref[s], NT if m == 2 else NN)

                def store(s, value, first=first):
                    acc[table[1, first + s]] += value

                over_live(live_in(counts_ref[m], first, w_ref.shape[0]), terms, store)

        def begin(m, x, pieces, piece_keys):
            def body(where_ref, counts_ref, table, x_ref, *refs):
                zero(refs[-1])
                add_pieces(refs[-1], m, x_ref, refs[:-1], piece_keys, table, counts_ref, where_ref)

            (acc,) = call(
                body, [where, counts, tables[m]], [x, *pieces], [hidden_f32],
                products=sum(p.shape[0] for p in pieces),
            )
            return acc

        def go_on(m, acc, x, pieces, piece_keys):
            if not pieces:
                return acc

            def body(where_ref, counts_ref, table, acc_in, x_ref, *refs):
                add_pieces(refs[-1], m, x_ref, refs[:-1], piece_keys, table, counts_ref, where_ref)

            (acc,) = call(
                body, [where, counts, tables[m]], [acc, x, *pieces], [hidden_f32],
                products=sum(p.shape[0] for p in pieces), aliases={3: 0},
            )
            return acc

        def relayed(name, pieces, *others):
            out = []
            for w in pieces if halves else []:
                out.append(part_swap(after(w, *others), name))
                others = out[-1:]
            return out

        acc_g = begin(0, tokens, near[0], near_keys)
        acc_u = begin(1, tokens, near[1], near_keys)
        tokens_pair = pair_swap(tokens, "tokens")
        cotangent_pair = pair_swap(cotangent, "cotangent")

        x_g = shift_all("gate", cut[0])
        x_g = after(x_g, acc_g, tokens_pair, cotangent_pair)
        x_u = shift_all("up", cut[1], *x_g)
        y_g = relayed("gate", x_g)

        near.append([own[2], pair_swap(after(own[2], *x_g), "down")])
        direct = [both("gate_x", after(x_g, acc_u))]
        x_u, y_g = after((x_u, y_g), acc_u)
        x_d = shift_all("down", cut[2], *x_u)
        acc_g = go_on(0, after(acc_g, *x_u), tokens, direct[0], direct_keys)
        y_u = relayed("up", x_u)
        direct.append(both("up_x", after(x_u, acc_g)))
        acc_h = begin(2, cotangent, near[2], near_keys)
        relay = [both("gate_y", after(y_g, acc_g))]

        acc_u = go_on(1, acc_u, tokens, direct[1], direct_keys)

        def gate_body(where_ref, counts_ref, tg, acc_in, x_ref, *refs):
            w_refs, silu_ref, slope_ref, acc = refs[:-3], *refs[-3:]
            acc[...] = acc_in[...]
            add_pieces(acc, 0, x_ref, w_refs, relay_keys, tg, counts_ref, where_ref)

            def finish(b, _):
                gate = acc[b]
                sigma = jax.nn.sigmoid(gate)
                silu_ref[b] = gate * sigma
                slope_ref[b] = sigma * (1.0 + gate * (1.0 - sigma))
                return 0

            lax.fori_loop(0, hidden_blocks, finish, 0)

        silu, slope = call(
            gate_body,
            [where, counts, tables[0]],
            [acc_g, tokens, *relay[0]],
            [hidden_f32, hidden_f32],
            scratch=[pltpu.VMEM(hidden_f32.shape, F32)],
            products=shard,
        )
        x_d = after(x_d, acc_u, silu, acc_h)
        y_u = after(y_u, *x_d)
        y_d = relayed("down", x_d, *y_u)
        direct.append(both("down_x", x_d))
        relay.append(both("up_y", y_u))

        quarter = token_count // 4

        def up_body(where_ref, counts_ref, tu, acc_in, silu_ref, x_ref, *refs):
            w_refs, acc, h_refs = refs[:-5], refs[-5], refs[-4:]
            add_pieces(acc, 1, x_ref, w_refs, relay_keys, tu, counts_ref, where_ref)

            def finish(b, _):
                hidden = (silu_ref[b] * acc[b]).astype(BF16)
                for i, h_ref in enumerate(h_refs):
                    h_ref[b] = hidden[i * quarter : (i + 1) * quarter]
                return 0

            lax.fori_loop(0, hidden_blocks, finish, 0)

        up_value, *hidden = call(
            up_body,
            [where, counts, tables[1]],
            [acc_u, silu, tokens, *relay[1]],
            [
                hidden_f32,
                *[jax.ShapeDtypeStruct((hidden_blocks, quarter, size), BF16)] * 4,
            ],
            aliases={3: 0},
            products=shard + 20,
        )
        hidden_pair = after([pair_swap(h, "hidden") for h in hidden], *y_d)

        def block_grads(m, ahead, left, right, cuts=(0, shard)):
            spans = [(k, low, high) for k in ahead for low, high in zip(cuts, cuts[1:])]

            n_left, n_both = len(left), len(left) + len(right)

            def body(where_ref, counts_ref, table, *refs):
                ls, rs, outs = refs[:n_left], refs[n_left:n_both], refs[n_both:]
                for (k, low, high), o_ref in zip(spans, outs):
                    first = place.first(where_ref, ((chips - k) % chips, False, None)) + low
                    live = live_in(counts_ref[m], first, high - low)

                    def terms(s, first=first):
                        f, h = table[0, first + s], table[1, first + s]
                        wide, deep = (rs, ls) if m == 2 else (ls, rs)
                        model = jnp.concatenate([ref[:, columns(f)] for ref in wide], axis=0)
                        inner = jnp.concatenate([ref[h] for ref in deep], axis=0)
                        return mm(inner, model, TN) if m == 2 else mm(model, inner, TN)

                    def store(s, value, o_ref=o_ref):
                        o_ref[s] = value.astype(BF16)

                    over_live(live, terms, store)

                    def clear(s, _, o_ref=o_ref):
                        o_ref[s] = jnp.zeros((size, size), BF16)
                        return 0

                    lax.fori_loop(live, high - low, clear, 0)

            return call(
                body,
                [where, counts, tables[m]],
                [*left, *right],
                [jax.ShapeDtypeStruct((high - low, size, size), BF16) for _, low, high in spans],
                products=len(ahead) * shard,
            )

        def total(kept, arrived):
            value = kept.astype(F32)
            for g in arrived:
                value = value + g.astype(F32)
            return value.astype(BF16)[None]

        down_operands = ([*hidden, *hidden_pair], [cotangent, cotangent_pair])
        cuts = tuple(sorted({0, max(shard // 4, 1), shard}))
        down_away = [block_grads(2, away, *down_operands, cuts=cuts[:2])]
        held = [*after(hidden, *down_away[0]), *hidden_pair]
        rest = block_grads(2, away, held, down_operands[1], cuts=cuts[1:])
        steps = len(cuts) - 2
        down_away += [rest[i::steps] for i in range(steps)]
        hurry = [g for grads in down_away[1:] for g in grads]
        down_far = []
        for grads in down_away:
            grads = after(grads, *(down_far[-1] if down_far else []))
            down_far.append([chip_shift(g, k, "down_grad") for g, k in zip(grads, away)])
            if hurry:
                down_far[0], hurry = after(down_far[0], *hurry), []
        down_lead, down_last = down_far[0], down_far[-1]

        relay.append(both("down_y", after(y_d, *down_lead)))
        acc_h = go_on(2, after(acc_h, *down_lead), cotangent, direct[2], direct_keys)

        half_tokens = token_count // 2

        def back_body(where_ref, counts_ref, td, acc_in, c_ref, silu_ref, slope_ref, up_ref, *refs):
            outs, acc = refs[-4:-1], refs[-1]
            acc[...] = acc_in[...]
            add_pieces(acc, 2, c_ref, refs[:-4], relay_keys, td, counts_ref, where_ref)

            def finish(b, _):
                grad = acc[b]
                gate = (grad * up_ref[b] * slope_ref[b]).astype(BF16)
                up = (grad * silu_ref[b]).astype(BF16)
                for i in range(2):
                    rows = slice(i * half_tokens, (i + 1) * half_tokens)
                    outs[i][b] = gate[rows]
                outs[2][b] = up
                return 0

            lax.fori_loop(0, hidden_blocks, finish, 0)

        grads = call(
            back_body,
            [where, counts, tables[2]],
            [acc_h, cotangent, silu, slope, up_value, *relay[2]],
            [jax.ShapeDtypeStruct((hidden_blocks, half_tokens, size), BF16)] * 2 + [hidden_bf16],
            scratch=[pltpu.VMEM(hidden_f32.shape, F32)],
            products=shard + 10,
        )
        pieces = [near[m] + direct[m] + relay[m] for m in range(3)]

        width = model_blocks // groups
        chunk = jax.ShapeDtypeStruct((groups // 2, token_count, width * size), BF16)

        def deal(where_ref, acc, outs):
            for i in range(groups):
                to = lax.bitwise_xor(where_ref[3], i) * width
                for j in range(width):
                    outs[i % 2][i // 2, :, j * size : (j + 1) * size] = acc[to + j].astype(BF16)

        def out_body(where_ref, counts_ref, td, *refs):
            h_refs, refs = refs[:4], refs[4:]
            w_refs, outs, acc = refs[: len(all_keys)], refs[len(all_keys) : -1], refs[-1]
            zero(acc)
            for w_ref, key in zip(w_refs, all_keys):
                first = place.first(where_ref, key)

                def terms(s, w_ref=w_ref, first=first):
                    h = td[1, first + s]
                    return mm(jnp.concatenate([h_ref[h] for h_ref in h_refs], axis=0), w_ref[s])

                def store(s, value, first=first):
                    acc[td[0, first + s]] += value

                over_live(live_in(counts_ref[2], first, w_ref.shape[0]), terms, store)
            deal(where_ref, acc, outs)

        model_acc = pltpu.VMEM((model_blocks, token_count, size), F32)
        out_parts = call(
            out_body,
            [where, counts, tables[2]],
            [*after(hidden, *grads), *pieces[2]],
            [chunk] * 2,
            scratch=[model_acc],
            products=4 * shard,
        )

        grads_pair = [pair_swap(g, "grads") for g in grads]
        grads_pair[:2] = after(grads_pair[:2], *out_parts)
        gate_operands = ([tokens, tokens_pair], [*grads[:2], *grads_pair[:2]])
        up_operands = ([tokens, tokens_pair], [grads[2], after(grads_pair[2], *down_last)])
        gate_away = block_grads(0, away, *gate_operands)

        def token_body(where_ref, counts_ref, tg, tu, *refs):
            ys, refs = refs[:3], refs[3:]
            n = len(all_keys)
            outs, acc = refs[2 * n : -1], refs[-1]
            zero(acc)
            for m, table in ((0, tg), (1, tu)):
                for w_ref, key in zip(refs[m * n : (m + 1) * n], all_keys):
                    first = place.first(where_ref, key)

                    def terms(s, m=m, table=table, w_ref=w_ref, first=first):
                        h = table[1, first + s]
                        y = ys[2][h] if m else jnp.concatenate([ys[0][h], ys[1][h]], axis=0)
                        return mm(y, w_ref[s], NT)

                    def store(s, value, table=table, first=first):
                        acc[table[0, first + s]] += value

                    over_live(live_in(counts_ref[m], first, w_ref.shape[0]), terms, store)
            deal(where_ref, acc, outs)

        token_parts = call(
            token_body,
            [where, counts, tables[0], tables[1]],
            [*after(grads, *gate_away), *pieces[0], *pieces[1]],
            [chunk] * 2,
            scratch=[model_acc],
            products=8 * shard,
        )

        def swap_groups(name, chunks, *others):
            kept, sent = chunks
            bit, first = 1, None
            while True:
                arrived = group_swap(sent, bit, name)
                first = arrived if first is None else first
                bit *= 2
                if bit == groups:
                    return first, kept, arrived
                value = (kept.astype(F32) + after(arrived, *others).astype(F32)).astype(BF16)
                kept, sent = value[0::2], value[1::2]

        def last_sum(kept, arrived, *others):
            value = kept.astype(F32) + after(arrived, *others).astype(F32)
            return value[0].astype(BF16)

        up_away = block_grads(1, away, *up_operands)
        down_last = down_far[-1] = after(down_last, *gate_away)
        gate_far = [chip_shift(g, k, "gate_grad") for g, k in zip(after(gate_away, *down_last), away)]
        kept_t, kept_h = after((tokens, hidden), *down_last)
        (down_kept,) = block_grads(2, (0,), [*kept_h, *hidden_pair], down_operands[1])
        (gate_kept,) = block_grads(0, (0,), [kept_t, tokens_pair], gate_operands[1])
        (up_kept,) = block_grads(1, (0,), [kept_t, tokens_pair], up_operands[1])
        joined = [jnp.concatenate(steps, axis=0) for steps in zip(*down_far)]
        down_grad = total(down_kept, joined)
        out_first, *out_terms = swap_groups("out", out_parts, *token_parts)
        gate_far = after(gate_far, down_grad, gate_kept, up_kept, out_first, *up_away)
        up_far = [chip_shift(g, k, "up_grad") for g, k in zip(after(up_away, *gate_far), away)]
        gate_grad = total(gate_kept, gate_far)
        layer_out = last_sum(*out_terms, gate_grad)
        _, *token_terms = swap_groups("token", token_parts, gate_grad)
        token_grad = last_sum(*token_terms, layer_out)
        up_grad = total(up_kept, after(up_far, token_grad))
        return layer_out, token_grad, gate_grad, up_grad, down_grad

    return per_device


def solution(mesh):
    return jax.shard_map(
        make(mesh),
        mesh=mesh,
        in_specs=(
            P(("parts", "dp"), None),
            P(("parts", "dp"), None),
            P("tensor", "dp", None, None),
            P("tensor", "dp", None, None),
            P("tensor", "dp", None, None),
            P(None, "tensor", None),
            P(None, "tensor", None),
            P(None, "tensor", None),
            P(None, "tensor"),
        ),
        out_specs=(
            P(("parts", "dp"), "tensor"),
            P(("parts", "dp"), "tensor"),
            P(("parts", "tensor"), "dp", None, None),
            P(("parts", "tensor"), "dp", None, None),
            P(("parts", "tensor"), "dp", None, None),
        ),
        check_vma=False,
    )
```

time: 178 us -> 139 us (0.78); the launches traced: 175 us -> 139 us
  waiting for transfers between devices: 82.6 us -> 47.4 us
  local copies, waits for them, and re-layouts: 6.69 us -> 4.16 us
    ppermute x6 -> x7, waiting for transfers between devices: 49.3 us -> 21.5 us  [chip_shift(): lax.ppermute(a, 'dp', [(i, (i // 2 + k) % chips * 2 + i % 2) for i in ran...]
    ppermute x3, waiting for transfers between devices: 18.8 us -> 10.8 us  [part_swap(): return lax.ppermute(a, 'parts', [(0, 1), (1, 0)])]
    unnamed x28 -> x20, local copies, waits for them, and re-layouts: 4.49 us -> 1.22 us
    ppermute x6 -> x7, starting transfers between devices: 14.5 us -> 11.5 us  [chip_shift(): lax.ppermute(a, 'dp', [(i, (i // 2 + k) % chips * 2 + i % 2) for i in ran...]
    ppermute x13 -> x18, starting transfers between devices: 2.83 us -> 4.15 us  [pair_swap(): return lax.ppermute(a, 'dp', [(i, i ^ 1) for i in range(dp)])]
    pallas_call x13 -> x18, Pallas kernels: 53.6 us -> 54.9 us  [call(): pl.pallas_call(body, out_shape=outs, in_specs=[SMEM] * len(ints) + [VMEM]...]
    ppermute x6 -> x4, starting transfers between devices: 4.38 us -> 5.34 us  [group_swap(): return lax.ppermute(a, 'tensor', [(i, i ^ bit) for i in range(groups)])]
    ppermute x6 -> x4, waiting for transfers between devices: 14.4 us -> 14.6 us  [group_swap(): return lax.ppermute(a, 'tensor', [(i, i ^ bit) for i in range(groups)])]
  transfers between devices with their start and end apart: 28 -> 32, of which waited for: 10 -> 12; matrix products, arithmetic and copies ran while one was open for 4% -> 5% of each run, Pallas kernels for 31% -> 38%
where the time goes in v2:
time: 139 us
  Pallas kernels  54.9 us (39%)
  waiting for transfers between devices  47.4 us (34%)
  starting transfers between devices  25.4 us (18%)
  other arithmetic  5.81 us (4%)
  local copies, waits for them, and re-layouts  4.16 us (3%)
    pallas_call x18, Pallas kernels, call(): pl.pallas_call(body, out_shape=outs, in_specs=[SMEM] * len(ints) + [VMEM]...  54.9 us
    ppermute x7, waiting for transfers between devices, chip_shift(): lax.ppermute(a, 'dp', [(i, (i // 2 + k) % chips * 2 + i % 2) for i in ran...  21.5 us
    ppermute x4, waiting for transfers between devices, group_swap(): return lax.ppermute(a, 'tensor', [(i, i ^ bit) for i in range(groups)])  14.6 us
    ppermute x7, starting transfers between devices, chip_shift(): lax.ppermute(a, 'dp', [(i, (i // 2 + k) % chips * 2 + i % 2) for i in ran...  11.5 us
    ppermute x3, waiting for transfers between devices, part_swap(): return lax.ppermute(a, 'parts', [(0, 1), (1, 0)])  10.8 us
    ppermute x4, starting transfers between devices, group_swap(): return lax.ppermute(a, 'tensor', [(i, i ^ bit) for i in range(groups)])  5.34 us
    ppermute x3, starting transfers between devices, part_swap(): return lax.ppermute(a, 'parts', [(0, 1), (1, 0)])  4.43 us
    ppermute x18, starting transfers between devices, pair_swap(): return lax.ppermute(a, 'dp', [(i, i ^ 1) for i in range(dp)])  4.15 us
  transfers between devices with their start and end apart: 32, of which 12 were waited for; matrix products, arithmetic and copies ran while one was open for 5% of the time, Pallas kernels for 38%

profile of v2, /device:TPU:0, one launch (start us, length us, event | category | flops | bytes accessed | tf_op | source)
XLA Modules:
  0.0 138.7 jit_solution(12060221993119634097)
XLA Ops:
  1.8 1.8 %dynamic-slice_bitcast_fusion.1 = bf16[14,128,128]{2,1,0:T(8,128)(2,1)} fusion(bf16[1,28,128,128]{3,2,1,0:T(8,128)(2,1)} %param.11, s32[]{:T(128)S(6)} %select_n.18), kind=kLoop, calls=%fused_computation.11 | loop fusion | bytes 917508 | tf_op jit(solution)/shard_map/dynamic_slice | solution.py:145
  3.6 2.9 %collective-permute-start.1 = (bf16[14,128,128]{2,1,0:T(8,128)(2,1)}, bf16[14,128,128]{2,1,0:T(8,128)(2,1)}, u32[]{:S(2)}, u32[]{:S(2)}) collective-permute-start(bf16[14,128,128]{2,1,0:T(8,128)(2,1)} %dynamic-slice_bitcast_fusion.1), channel_id=1, source_target_pairs={{0,8},{4,12},{8,0},{12,4},{1,9},{5,13},{9,1},{13,5},{2,10},{6,14},... | collective-permute-start | bytes 1376264 | tf_op jit(solution)/shard_map/gate_chip/ppermute | solution.py:104
  6.6 1.1 dynamic-slice_bitcast_fusion.2
  7.7 1.2 copy-done.4
  8.9 4.0 %shard_map.129.acc_in = f32[28,128,128]{2,1,0:T(8,128)S(1)} custom-call(s32[4]{0:T(128)S(1)} %pad_add_fusion.where_ref, s32[3]{0:T(128)S(1)} %bitcast.36, s32[2,112]{1,0:T(2,128)S(1)} %bitcast.61, bf16[128,4096]{1,0:T(8,128)(2,1)S(1)} %copy-done, bf16[28,128,128]{2,1,0:T(8,128)(2,1)S(1)} %bitcast.34, bf16[28,128,128]{2,1,0:T(8,128)(2,1)} %collective-permute-done.2.refs_1_.refs_4_), custom_call_target="tpu_custom_call" | custom-call | flops 56 | bytes 56 | tf_op jit(solution)/shard_map/pallas_call | solution.py:30
  12.9 4.7 %collective-permute-done.1.refs_0_.refs_5_ = bf16[14,128,128]{2,1,0:T(8,128)(2,1)} collective-permute-done((bf16[14,128,128]{2,1,0:T(8,128)(2,1)}, bf16[14,128,128]{2,1,0:T(8,128)(2,1)}, u32[]{:S(2)}, u32[]{:S(2)}) %collective-permute-start.1) | collective-permute-done | bytes 458784 | tf_op jit(solution)/shard_map/gate_chip/ppermute | solution.py:104
  17.6 1.7 %collective-permute-start.5 = (bf16[14,128,128]{2,1,0:T(8,128)(2,1)S(1)}, bf16[14,128,128]{2,1,0:T(8,128)(2,1)S(1)}, u32[]{:S(2)}, u32[]{:S(2)}) collective-permute-start(bf16[14,128,128]{2,1,0:T(8,128)(2,1)S(1)} %dynamic-slice_bitcast_fusion.2), channel_id=1, source_target_pairs={{0,8},{4,12},{8,0},{12,4},{1,9},{5,13},{9,1},{13,5},{2,10},{6,14},... | collective-permute-start | bytes 1376264 | tf_op jit(solution)/shard_map/up_chip/ppermute | solution.py:104
  19.3 1.5 %collective-permute-start.6 = (bf16[14,128,128]{2,1,0:T(8,128)(2,1)}, bf16[14,128,128]{2,1,0:T(8,128)(2,1)S(1)}, u32[]{:S(2)}, u32[]{:S(2)}) collective-permute-start(bf16[14,128,128]{2,1,0:T(8,128)(2,1)} %collective-permute-done.1.refs_0_.refs_5_), channel_id=1, source_target_pairs={{0,16},{16,0},{1,17},{17,1},{2,18},{18,2},{3,19},{19,3},{4,20},{20... | collective-permute-start | bytes 1376264 | tf_op jit(solution)/shard_map/gate_part/ppermute | solution.py:110
  20.9 4.0 %shard_map.128.acc_in = f32[28,128,128]{2,1,0:T(8,128)S(1)} custom-call(s32[4]{0:T(128)S(1)} %pad_add_fusion.where_ref, s32[3]{0:T(128)S(1)} %bitcast.37, s32[2,112]{1,0:T(2,128)S(1)} %bitcast.67, bf16[128,4096]{1,0:T(8,128)(2,1)S(1)} %copy-done, bf16[28,128,128]{2,1,0:T(8,128)(2,1)S(1)} %bitcast.31, bf16[28,128,128]{2,1,0:T(8,128)(2,1)} %collective-permute-done.refs_1_.refs_10_), custom_call_target="tpu_custom_call" | custom-call | flops 56 | bytes 56 | tf_op jit(solution)/shard_map/pallas_call | solution.py:30
  25.5 4.1 %collective-permute-done.5.refs_0_.refs_11_ = bf16[14,128,128]{2,1,0:T(8,128)(2,1)S(1)} collective-permute-done((bf16[14,128,128]{2,1,0:T(8,128)(2,1)S(1)}, bf16[14,128,128]{2,1,0:T(8,128)(2,1)S(1)}, u32[]{:S(2)}, u32[]{:S(2)}) %collective-permute-start.5) | collective-permute-done | bytes 458784 | tf_op jit(solution)/shard_map/up_chip/ppermute | solution.py:104
  29.6 1.4 collective-permute-done.6.refs_0_.refs_7_
  30.9 2.7 %shard_map.130.acc_in = f32[28,128,128]{2,1,0:T(8,128)S(1)} custom-call(s32[4]{0:T(128)S(1)} %pad_add_fusion.where_ref, s32[3]{0:T(128)S(1)} %bitcast.38, s32[2,112]{1,0:T(2,128)S(1)} %bitcast.62, f32[28,128,128]{2,1,0:T(8,128)S(1)} %shard_map.129.acc_in, bf16[128,4096]{1,0:T(8,128)(2,1)S(1)} %copy-done, ...), custom_call_target="tpu_custom_call", output_to_operand_aliasing={{}: (3, {})} | custom-call | flops 28 | bytes 28 | tf_op jit(solution)/shard_map/pallas_call | solution.py:30
  34.2 0.7 collective-permute-start.11
  34.9 1.5 %collective-permute-start.10 = (bf16[14,128,128]{2,1,0:T(8,128)(2,1)S(1)}, bf16[14,128,128]{2,1,0:T(8,128)(2,1)S(1)}, u32[]{:S(2)}, u32[]{:S(2)}) collective-permute-start(bf16[14,128,128]{2,1,0:T(8,128)(2,1)S(1)} %collective-permute-done.5.refs_0_.refs_11_), channel_id=1, source_target_pairs={{0,16},{16,0},{1,17},{17,1},{2,18},{18,2},{3,19},{19,3},{4,20},{20... | collective-permute-start | bytes 1376264 | tf_op jit(solution)/shard_map/up_part/ppermute | solution.py:110
  36.3 1.2 shard_map.131.acc_in
  37.6 3.0 %shard_map.132 = (f32[28,128,128]{2,1,0:T(8,128)S(1)}, f32[28,128,128]{2,1,0:T(8,128)S(1)}) custom-call(s32[4]{0:T(128)S(1)} %pad_add_fusion.where_ref, s32[3]{0:T(128)S(1)} %bitcast.40, s32[2,112]{1,0:T(2,128)S(1)} %bitcast.63, f32[28,128,128]{2,1,0:T(8,128)S(1)} %shard_map.130.acc_in, bf16[128,4096]{1,0:T(8,128)(2,1)S(1)} %copy-done, ...), custom_call_target="tpu_custom_call" | custom-call | flops 28 | bytes 28 | tf_op jit(solution)/shard_map/pallas_call | solution.py:30
  40.7 3.7 %shard_map.133.acc_in = f32[28,128,128]{2,1,0:T(8,128)S(1)} custom-call(s32[4]{0:T(128)S(1)} %pad_add_fusion.where_ref, s32[3]{0:T(128)S(1)} %bitcast.41, s32[2,112]{1,0:T(2,128)S(1)} %bitcast.54, bf16[128,4096]{1,0:T(8,128)(2,1)S(1)} %copy-done.1, bf16[28,128,128]{2,1,0:T(8,128)(2,1)S(1)} %bitcast.28, ...), custom_call_target="tpu_custom_call" | custom-call | flops 56 | bytes 56 | tf_op jit(solution)/shard_map/pallas_call | solution.py:30
  44.4 2.4 %collective-permute-done.11.refs_0_.refs_6_ = bf16[14,128,128]{2,1,0:T(8,128)(2,1)S(1)} collective-permute-done((bf16[14,128,128]{2,1,0:T(8,128)(2,1)S(1)}, bf16[14,128,128]{2,1,0:T(8,128)(2,1)S(1)}, u32[]{:S(2)}, u32[]{:S(2)}) %collective-permute-start.11) | collective-permute-done | bytes 458784 | tf_op jit(solution)/shard_map/down_chip/ppermute | solution.py:104
  47.1 1.5 %collective-permute-start.18 = (bf16[14,128,128]{2,1,0:T(8,128)(2,1)S(1)}, bf16[14,128,128]{2,1,0:T(8,128)(2,1)S(1)}, u32[]{:S(2)}, u32[]{:S(2)}) collective-permute-start(bf16[14,128,128]{2,1,0:T(8,128)(2,1)S(1)} %collective-permute-done.11.refs_0_.refs_6_), channel_id=1, source_target_pairs={{0,16},{16,0},{1,17},{17,1},{2,18},{18,2},{3,19},{19,3},{4,20},{20... | collective-permute-start | bytes 1376264 | tf_op jit(solution)/shard_map/down_part/ppermute | solution.py:110
  48.9 0.9 shard_map.134
  50.9 9.1 %collective-permute-done.18.refs_0_.refs_8_ = bf16[14,128,128]{2,1,0:T(8,128)(2,1)S(1)} collective-permute-done((bf16[14,128,128]{2,1,0:T(8,128)(2,1)S(1)}, bf16[14,128,128]{2,1,0:T(8,128)(2,1)S(1)}, u32[]{:S(2)}, u32[]{:S(2)}) %collective-permute-start.18) | collective-permute-done | bytes 458784 | tf_op jit(solution)/shard_map/down_part/ppermute | solution.py:110
  60.1 1.5 %shard_map.135 = bf16[7,128,128]{2,1,0:T(8,128)(2,1)S(1)} custom-call(s32[4]{0:T(128)S(1)} %pad_add_fusion.where_ref, s32[3]{0:T(128)S(1)} %bitcast.43, s32[2,112]{1,0:T(2,128)S(1)} %bitcast.55, bf16[28,32,128]{2,1,0:T(8,128)(2,1)S(1)} %get-tuple-element.120.refs_0_, bf16[28,32,128]{2,1,0:T(8,128)(2,1)S(1)} %get-tuple-element.121.refs_1_, ...), custom_call_target="tpu_custom_call" | custom-call | flops 28 | bytes 28 | tf_op jit(solution)/shard_map/pallas_call | solution.py:30
  61.6 1.5 %collective-permute-start.19 = (bf16[7,128,128]{2,1,0:T(8,128)(2,1)S(1)}, bf16[7,128,128]{2,1,0:T(8,128)(2,1)S(1)}, u32[]{:S(2)}, u32[]{:S(2)}) collective-permute-start(bf16[7,128,128]{2,1,0:T(8,128)(2,1)S(1)} %shard_map.135), channel_id=1, source_target_pairs={{0,8},{4,12},{8,0},{12,4},{1,9},{5,13},{9,1},{13,5},{2,10},{6,14},... | collective-permute-start | bytes 688136 | tf_op jit(solution)/shard_map/down_grad_chip/ppermute | solution.py:104
  63.1 1.5 %shard_map.136 = bf16[21,128,128]{2,1,0:T(8,128)(2,1)S(1)} custom-call(s32[4]{0:T(128)S(1)} %pad_add_fusion.where_ref, s32[3]{0:T(128)S(1)} %bitcast.44, s32[2,112]{1,0:T(2,128)S(1)} %bitcast.56, bf16[28,32,128]{2,1,0:T(8,128)(2,1)S(1)} %get-tuple-element.120.refs_0_, bf16[28,32,128]{2,1,0:T(8,128)(2,1)S(1)} %get-tuple-element.121.refs_1_, ...), custom_call_target="tpu_custom_call" | custom-call | flops 28 | bytes 28 | tf_op jit(solution)/shard_map/pallas_call | solution.py:30
  64.5 4.0 %collective-permute-done.19 = bf16[7,128,128]{2,1,0:T(8,128)(2,1)S(1)} collective-permute-done((bf16[7,128,128]{2,1,0:T(8,128)(2,1)S(1)}, bf16[7,128,128]{2,1,0:T(8,128)(2,1)S(1)}, u32[]{:S(2)}, u32[]{:S(2)}) %collective-permute-start.19) | collective-permute-done | bytes 229408 | tf_op jit(solution)/shard_map/down_grad_chip/ppermute | solution.py:104
  68.6 1.7 %collective-permute-start.26 = (bf16[21,128,128]{2,1,0:T(8,128)(2,1)S(1)}, bf16[21,128,128]{2,1,0:T(8,128)(2,1)S(1)}, u32[]{:S(2)}, u32[]{:S(2)}) collective-permute-start(bf16[21,128,128]{2,1,0:T(8,128)(2,1)S(1)} %shard_map.136), channel_id=1, source_target_pairs={{0,8},{4,12},{8,0},{12,4},{1,9},{5,13},{9,1},{13,5},{2,10},{6,14},... | collective-permute-start | bytes 2064392 | tf_op jit(solution)/shard_map/down_grad_chip/ppermute | solution.py:104
  70.3 1.5 %shard_map.137.acc_in = f32[28,128,128]{2,1,0:T(8,128)S(1)} custom-call(s32[4]{0:T(128)S(1)} %pad_add_fusion.where_ref, s32[3]{0:T(128)S(1)} %bitcast.45, s32[2,112]{1,0:T(2,128)S(1)} %bitcast.57, f32[28,128,128]{2,1,0:T(8,128)S(1)} %shard_map.133.acc_in, bf16[128,4096]{1,0:T(8,128)(2,1)S(1)} %copy-done.1, ...), custom_call_target="tpu_custom_call", output_to_operand_aliasing={{}: (3, {})} | custom-call | flops 28 | bytes 28 | tf_op jit(solution)/shard_map/pallas_call | solution.py:30
  71.8 1.4 %shard_map.138 = (bf16[28,64,128]{2,1,0:T(8,128)(2,1)S(1)}, bf16[28,64,128]{2,1,0:T(8,128)(2,1)S(1)}, bf16[28,128,128]{2,1,0:T(8,128)(2,1)S(1)}) custom-call(s32[4]{0:T(128)S(1)} %pad_add_fusion.where_ref, s32[3]{0:T(128)S(1)} %bitcast.46, s32[2,112]{1,0:T(2,128)S(1)} %bitcast.58, f32[28,128,128]{2,1,0:T(8,128)S(1)} %shard_map.137.acc_in, ...), custom_call_target="tpu_custom_call" | custom-call | flops 38 | bytes 38 | tf_op jit(solution)/shard_map/pallas_call | solution.py:30
  74.1 4.6 %shard_map.139 = (bf16[2,128,1024]{2,1,0:T(8,128)(2,1)S(1)}, bf16[2,128,1024]{2,1,0:T(8,128)(2,1)S(1)}) custom-call(s32[4]{0:T(128)S(1)} %pad_add_fusion.where_ref, s32[3]{0:T(128)S(1)} %bitcast.47, s32[2,112]{1,0:T(2,128)S(1)} %bitcast.59, bf16[28,32,128]{2,1,0:T(8,128)(2,1)S(1)} %get-tuple-element.120.refs_0_, ...), custom_call_target="tpu_custom_call" | custom-call | flops 112 | bytes 112 | tf_op jit(solution)/shard_map/pallas_call | solution.py:30
  78.8 2.6 %shard_map.140 = bf16[28,128,128]{2,1,0:T(8,128)(2,1)S(1)} custom-call(s32[4]{0:T(128)S(1)} %pad_add_fusion.where_ref, s32[3]{0:T(128)S(1)} %bitcast.48, s32[2,112]{1,0:T(2,128)S(1)} %bitcast.64, bf16[128,4096]{1,0:T(8,128)(2,1)S(1)} %copy-done, bf16[128,4096]{1,0:T(8,128)(2,1)S(1)} %collective-permute-done.3.refs_1_, ...), custom_call_target="tpu_custom_call" | custom-call | flops 28 | bytes 28 | tf_op jit(solution)/shard_map/pallas_call | solution.py:30
  81.4 5.0 %collective-permute-done.26 = bf16[21,128,128]{2,1,0:T(8,128)(2,1)S(1)} collective-permute-done((bf16[21,128,128]{2,1,0:T(8,128)(2,1)S(1)}, bf16[21,128,128]{2,1,0:T(8,128)(2,1)S(1)}, u32[]{:S(2)}, u32[]{:S(2)}) %collective-permute-start.26) | collective-permute-done | bytes 688160 | tf_op jit(solution)/shard_map/down_grad_chip/ppermute | solution.py:104
  86.4 1.7 %collective-permute-start.27 = (bf16[28,128,128]{2,1,0:T(8,128)(2,1)S(1)}, bf16[28,128,128]{2,1,0:T(8,128)(2,1)S(1)}, u32[]{:S(2)}, u32[]{:S(2)}) collective-permute-start(bf16[28,128,128]{2,1,0:T(8,128)(2,1)S(1)} %shard_map.140), channel_id=1, source_target_pairs={{0,8},{4,12},{8,0},{12,4},{1,9},{5,13},{9,1},{13,5},{2,10},{6,14},... | collective-permute-start | bytes 2752520 | tf_op jit(solution)/shard_map/gate_grad_chip/ppermute | solution.py:104
  88.1 1.3 collective-permute-start.22
  89.5 12.6 %shard_map.141 = (bf16[2,128,1024]{2,1,0:T(8,128)(2,1)S(1)}, bf16[2,128,1024]{2,1,0:T(8,128)(2,1)S(1)}) custom-call(s32[4]{0:T(128)S(1)} %pad_add_fusion.where_ref, s32[3]{0:T(128)S(1)} %bitcast.49, s32[2,112]{1,0:T(2,128)S(1)} %bitcast.65, s32[2,112]{1,0:T(2,128)S(1)} %bitcast.70, bf16[28,64,128]{2,1,0:T(8,128)(2,1)S(1)} %get-tuple-element.110.refs_2_.refs_0_, ...), custom_call_target="tpu_custom_call" | custom-call | flops 224 | bytes 224 | tf_op jit(solution)/shard_map/pallas_call | solution.py:30
  102.2 2.6 %shard_map.142 = bf16[28,128,128]{2,1,0:T(8,128)(2,1)S(1)} custom-call(s32[4]{0:T(128)S(1)} %pad_add_fusion.where_ref, s32[3]{0:T(128)S(1)} %bitcast.50, s32[2,112]{1,0:T(2,128)S(1)} %bitcast.66, bf16[128,4096]{1,0:T(8,128)(2,1)S(1)} %copy-done, bf16[128,4096]{1,0:T(8,128)(2,1)S(1)} %collective-permute-done.3.refs_1_, ...), custom_call_target="tpu_custom_call" | custom-call | flops 28 | bytes 28 | tf_op jit(solution)/shard_map/pallas_call | solution.py:30
  104.8 2.6 %shard_map.143 = bf16[28,128,128]{2,1,0:T(8,128)(2,1)S(1)} custom-call(s32[4]{0:T(128)S(1)} %pad_add_fusion.where_ref, s32[3]{0:T(128)S(1)} %bitcast.51, s32[2,112]{1,0:T(2,128)S(1)} %bitcast.60, bf16[28,32,128]{2,1,0:T(8,128)(2,1)S(1)} %get-tuple-element.120.refs_0_, bf16[28,32,128]{2,1,0:T(8,128)(2,1)S(1)} %get-tuple-element.121.refs_1_, ...), custom_call_target="tpu_custom_call" | custom-call | flops 28 | bytes 28 | tf_op jit(solution)/shard_map/pallas_call | solution.py:30
  107.5 1.2 fusion
  109.0 3.9 %collective-permute-start.25 = (bf16[1,128,1024]{2,1,0:T(8,128)(2,1)S(1)}, bf16[1,128,1024]{2,1,0:T(8,128)(2,1)S(1)}, u32[]{:S(2)}, u32[]{:S(2)}) collective-permute-start(bf16[1,128,1024]{2,1,0:T(8,128)(2,1)S(1)} %slice.21), channel_id=1, source_target_pairs={{0,2},{1,3},{2,0},{3,1},{4,6},{5,7},{6,4},{7,5},{8,10},{9,11},{10,... | collective-permute-start | bytes 786440 | tf_op jit(solution)/shard_map/out_group/ppermute | solution.py:114
  112.8 1.7 %shard_map.145 = bf16[28,128,128]{2,1,0:T(8,128)(2,1)S(1)} custom-call(s32[4]{0:T(128)S(1)} %pad_add_fusion.where_ref, s32[3]{0:T(128)S(1)} %bitcast.52, s32[2,112]{1,0:T(2,128)S(1)} %bitcast.71, bf16[128,4096]{1,0:T(8,128)(2,1)S(1)} %copy-done, bf16[128,4096]{1,0:T(8,128)(2,1)S(1)} %collective-permute-done.3.refs_1_, ...), custom_call_target="tpu_custom_call" | custom-call | flops 28 | bytes 28 | tf_op jit(solution)/shard_map/pallas_call | solution.py:30
  114.5 2.6 %shard_map.144 = bf16[28,128,128]{2,1,0:T(8,128)(2,1)S(1)} custom-call(s32[4]{0:T(128)S(1)} %pad_add_fusion.where_ref, s32[3]{0:T(128)S(1)} %bitcast.53, s32[2,112]{1,0:T(2,128)S(1)} %bitcast.72, bf16[128,4096]{1,0:T(8,128)(2,1)S(1)} %copy-done, bf16[128,4096]{1,0:T(8,128)(2,1)S(1)} %collective-permute-done.3.refs_1_, ...), custom_call_target="tpu_custom_call" | custom-call | flops 28 | bytes 28 | tf_op jit(solution)/shard_map/pallas_call | solution.py:30
  117.2 1.2 collective-permute-start.31
  118.4 1.2 fusion.1
  119.6 1.3 collective-permute-done.29
  121.2 0.8 fusion.3
  122.0 13.4 %collective-permute-done.30 = bf16[1,128,1024]{2,1,0:T(8,128)(2,1)S(1)} collective-permute-done((bf16[1,128,1024]{2,1,0:T(8,128)(2,1)S(1)}, bf16[1,128,1024]{2,1,0:T(8,128)(2,1)S(1)}, u32[]{:S(2)}, u32[]{:S(2)}) %collective-permute-start.30) | collective-permute-done | bytes 262176 | tf_op jit(solution)/shard_map/token_group/ppermute | solution.py:114
  135.3 0.8 fusion.4
  136.1 1.3 collective-permute-done.31
  137.4 1.3 fusion.2
  (67 shorter events, 5.6 us)
Async XLA Ops:
  0.6 7.0 %copy-start = (bf16[128,4096]{1,0:T(8,128)(2,1)S(1)}, bf16[128,4096]{1,0:T(8,128)(2,1)}, u32[]{:S(2)}) copy-start(bf16[128,4096]{1,0:T(8,128)(2,1)} %refs_0_.5) | copy-start | bytes 3145732
  0.6 7.0 %copy-start.6 = (s32[3,1]{0,1:T(1,128)S(1)}, s32[3,1]{0,1:T(1,128)}, u32[]{:S(2)}) copy-start(s32[3,1]{0,1:T(1,128)} %param.17) | copy-start | bytes 40
  0.7 7.0 %copy-start.8 = (s32[2,1,112]{2,1,0:T(1,128)S(1)}, s32[2,1,112]{2,1,0:T(1,128)}, u32[]{:S(2)}) copy-start(s32[2,1,112]{2,1,0:T(1,128)} %param.14) | copy-start | bytes 2692
  0.7 16.9 %collective-permute-start.4 = (bf16[128,4096]{1,0:T(8,128)(2,1)}, bf16[128,4096]{1,0:T(8,128)(2,1)S(1)}, u32[]{:S(2)}, u32[]{:S(2)}) collective-permute-start(bf16[128,4096]{1,0:T(8,128)(2,1)} %refs_8_.5), channel_id=1, source_target_pairs={{0,4},{4,0},{8,12},{12,8},{1,5},{5,1},{9,13},{13,9},{2,6},{6,2},{1... | collective-permute-start | bytes 3145736 | tf_op jit(solution)/shard_map/cotangent_core/ppermute | solution.py:100
  1.2 16.4 %collective-permute-start.3 = (bf16[128,4096]{1,0:T(8,128)(2,1)}, bf16[128,4096]{1,0:T(8,128)(2,1)S(1)}, u32[]{:S(2)}, u32[]{:S(2)}) collective-permute-start(bf16[128,4096]{1,0:T(8,128)(2,1)} %refs_0_.5), channel_id=1, source_target_pairs={{0,4},{4,0},{8,12},{12,8},{1,5},{5,1},{9,13},{13,9},{2,6},{6,2},{1... | collective-permute-start | bytes 3145736 | tf_op jit(solution)/shard_map/tokens_core/ppermute | solution.py:100
  1.3 6.4 %collective-permute-start.2 = (bf16[28,128,128]{2,1,0:T(8,128)(2,1)}, bf16[28,128,128]{2,1,0:T(8,128)(2,1)}, u32[]{:S(2)}, u32[]{:S(2)}) collective-permute-start(bf16[28,128,128]{2,1,0:T(8,128)(2,1)} %bitcast.33), channel_id=1, source_target_pairs={{0,4},{4,0},{8,12},{12,8},{1,5},{5,1},{9,13},{13,9},{2,6},{6,2},{1... | collective-permute-start | bytes 2752520 | tf_op jit(solution)/shard_map/gate_core/ppermute | solution.py:100
  1.7 19.2 %collective-permute-start = (bf16[28,128,128]{2,1,0:T(8,128)(2,1)}, bf16[28,128,128]{2,1,0:T(8,128)(2,1)}, u32[]{:S(2)}, u32[]{:S(2)}) collective-permute-start(bf16[28,128,128]{2,1,0:T(8,128)(2,1)} %bitcast.30), channel_id=1, source_target_pairs={{0,4},{4,0},{8,12},{12,8},{1,5},{5,1},{9,13},{13,9},{2,6},{6,2},{1... | collective-permute-start | bytes 2752520 | tf_op jit(solution)/shard_map/up_core/ppermute | solution.py:100
  3.6 14.0 %collective-permute-start.1 = (bf16[14,128,128]{2,1,0:T(8,128)(2,1)}, bf16[14,128,128]{2,1,0:T(8,128)(2,1)}, u32[]{:S(2)}, u32[]{:S(2)}) collective-permute-start(bf16[14,128,128]{2,1,0:T(8,128)(2,1)} %dynamic-slice_bitcast_fusion.1), channel_id=1, source_target_pairs={{0,8},{4,12},{8,0},{12,4},{1,9},{5,13},{9,1},{13,5},{2,10},{6,14},... | collective-permute-start | bytes 1376264 | tf_op jit(solution)/shard_map/gate_chip/ppermute | solution.py:104
  7.7 1.2 copy-start.4
  8.9 12.0 %copy-start.3 = (bf16[1,28,128,128]{3,2,1,0:T(8,128)(2,1)S(1)}, bf16[1,28,128,128]{3,2,1,0:T(8,128)(2,1)}, u32[]{:S(2)}) copy-start(bf16[1,28,128,128]{3,2,1,0:T(8,128)(2,1)} %param.12) | copy-start | bytes 2752516
  8.9 12.0 %copy-start.9 = (s32[2,1,112]{2,1,0:T(1,128)S(1)}, s32[2,1,112]{2,1,0:T(1,128)}, u32[]{:S(2)}) copy-start(s32[2,1,112]{2,1,0:T(1,128)} %param.15) | copy-start | bytes 2692
  17.6 12.0 %collective-permute-start.5 = (bf16[14,128,128]{2,1,0:T(8,128)(2,1)S(1)}, bf16[14,128,128]{2,1,0:T(8,128)(2,1)S(1)}, u32[]{:S(2)}, u32[]{:S(2)}) collective-permute-start(bf16[14,128,128]{2,1,0:T(8,128)(2,1)S(1)} %dynamic-slice_bitcast_fusion.2), channel_id=1, source_target_pairs={{0,8},{4,12},{8,0},{12,4},{1,9},{5,13},{9,1},{13,5},{2,10},{6,14},... | collective-permute-start | bytes 1376264 | tf_op jit(solution)/shard_map/up_chip/ppermute | solution.py:104
  19.3 11.6 %collective-permute-start.6 = (bf16[14,128,128]{2,1,0:T(8,128)(2,1)}, bf16[14,128,128]{2,1,0:T(8,128)(2,1)S(1)}, u32[]{:S(2)}, u32[]{:S(2)}) collective-permute-start(bf16[14,128,128]{2,1,0:T(8,128)(2,1)} %collective-permute-done.1.refs_0_.refs_5_), channel_id=1, source_target_pairs={{0,16},{16,0},{1,17},{17,1},{2,18},{18,2},{3,19},{19,3},{4,20},{20... | collective-permute-start | bytes 1376264 | tf_op jit(solution)/shard_map/gate_part/ppermute | solution.py:110
  20.9 4.1 %copy-start.2 = (bf16[1,28,128,128]{3,2,1,0:T(8,128)(2,1)S(1)}, bf16[1,28,128,128]{3,2,1,0:T(8,128)(2,1)}, u32[]{:S(2)}) copy-start(bf16[1,28,128,128]{3,2,1,0:T(8,128)(2,1)} %param.13) | copy-start | bytes 2752516
  24.9 6.1 %collective-permute-start.7 = (bf16[14,128,128]{2,1,0:T(8,128)(2,1)}, bf16[14,128,128]{2,1,0:T(8,128)(2,1)S(1)}, u32[]{:S(2)}, u32[]{:S(2)}) collective-permute-start(bf16[14,128,128]{2,1,0:T(8,128)(2,1)} %collective-permute-done.1.refs_0_.refs_5_), channel_id=1, source_target_pairs={{0,4},{4,0},{8,12},{12,8},{1,5},{5,1},{9,13},{13,9},{2,6},{6,2},{1... | collective-permute-start | bytes 1376264 | tf_op jit(solution)/shard_map/gate_x_core/ppermute | solution.py:100
  25.0 15.7 %collective-permute-start.12 = (bf16[28,128,128]{2,1,0:T(8,128)(2,1)S(1)}, bf16[28,128,128]{2,1,0:T(8,128)(2,1)S(1)}, u32[]{:S(2)}, u32[]{:S(2)}) collective-permute-start(bf16[28,128,128]{2,1,0:T(8,128)(2,1)S(1)} %bitcast.27), channel_id=1, source_target_pairs={{0,4},{4,0},{8,12},{12,8},{1,5},{5,1},{9,13},{13,9},{2,6},{6,2},{1... | collective-permute-start | bytes 2752520 | tf_op jit(solution)/shard_map/down_core/ppermute | solution.py:100
  33.6 2.7 %collective-permute-start.8 = (bf16[14,128,128]{2,1,0:T(8,128)(2,1)S(1)}, bf16[14,128,128]{2,1,0:T(8,128)(2,1)S(1)}, u32[]{:S(2)}, u32[]{:S(2)}) collective-permute-start(bf16[14,128,128]{2,1,0:T(8,128)(2,1)S(1)} %collective-permute-done.5.refs_0_.refs_11_), channel_id=1, source_target_pairs={{0,4},{4,0},{8,12},{12,8},{1,5},{5,1},{9,13},{13,9},{2,6},{6,2},{1... | collective-permute-start | bytes 1376264 | tf_op jit(solution)/shard_map/up_x_core/ppermute | solution.py:100
  33.7 3.9 %collective-permute-start.9 = (bf16[14,128,128]{2,1,0:T(8,128)(2,1)S(1)}, bf16[14,128,128]{2,1,0:T(8,128)(2,1)S(1)}, u32[]{:S(2)}, u32[]{:S(2)}) collective-permute-start(bf16[14,128,128]{2,1,0:T(8,128)(2,1)S(1)} %collective-permute-done.6.refs_0_.refs_7_), channel_id=1, source_target_pairs={{0,4},{4,0},{8,12},{12,8},{1,5},{5,1},{9,13},{13,9},{2,6},{6,2},{1... | collective-permute-start | bytes 1376264 | tf_op jit(solution)/shard_map/gate_y_core/ppermute | solution.py:100
  34.2 12.6 %collective-permute-start.11 = (bf16[14,128,128]{2,1,0:T(8,128)(2,1)S(1)}, bf16[14,128,128]{2,1,0:T(8,128)(2,1)S(1)}, u32[]{:S(2)}, u32[]{:S(2)}) collective-permute-start(bf16[14,128,128]{2,1,0:T(8,128)(2,1)S(1)} %dynamic-slice_bitcast_fusion), channel_id=1, source_target_pairs={{0,8},{4,12},{8,0},{12,4},{1,9},{5,13},{9,1},{13,5},{2,10},{6,14},... | collective-permute-start | bytes 1376264 | tf_op jit(solution)/shard_map/down_chip/ppermute | solution.py:104
  34.9 12.2 %collective-permute-start.10 = (bf16[14,128,128]{2,1,0:T(8,128)(2,1)S(1)}, bf16[14,128,128]{2,1,0:T(8,128)(2,1)S(1)}, u32[]{:S(2)}, u32[]{:S(2)}) collective-permute-start(bf16[14,128,128]{2,1,0:T(8,128)(2,1)S(1)} %collective-permute-done.5.refs_0_.refs_11_), channel_id=1, source_target_pairs={{0,16},{16,0},{1,17},{17,1},{2,18},{18,2},{3,19},{19,3},{4,20},{20... | collective-permute-start | bytes 1376264 | tf_op jit(solution)/shard_map/up_part/ppermute | solution.py:110
  37.6 3.1 %copy-start.1 = (bf16[128,4096]{1,0:T(8,128)(2,1)S(1)}, bf16[128,4096]{1,0:T(8,128)(2,1)}, u32[]{:S(2)}) copy-start(bf16[128,4096]{1,0:T(8,128)(2,1)} %refs_8_.5) | copy-start | bytes 3145732
  37.6 3.1 %copy-start.7 = (s32[2,1,112]{2,1,0:T(1,128)S(1)}, s32[2,1,112]{2,1,0:T(1,128)}, u32[]{:S(2)}) copy-start(s32[2,1,112]{2,1,0:T(1,128)} %param.16) | copy-start | bytes 2692
  47.1 1.8 %collective-permute-start.13 = (bf16[14,128,128]{2,1,0:T(8,128)(2,1)S(1)}, bf16[14,128,128]{2,1,0:T(8,128)(2,1)S(1)}, u32[]{:S(2)}, u32[]{:S(2)}) collective-permute-start(bf16[14,128,128]{2,1,0:T(8,128)(2,1)S(1)} %collective-permute-done.10.refs_0_.refs_13_), channel_id=1, source_target_pairs={{0,4},{4,0},{8,12},{12,8},{1,5},{5,1},{9,13},{13,9},{2,6},{6,2},{1... | collective-permute-start | bytes 1376264 | tf_op jit(solution)/shard_map/up_y_core/ppermute | solution.py:100
  47.1 12.9 %collective-permute-start.18 = (bf16[14,128,128]{2,1,0:T(8,128)(2,1)S(1)}, bf16[14,128,128]{2,1,0:T(8,128)(2,1)S(1)}, u32[]{:S(2)}, u32[]{:S(2)}) collective-permute-start(bf16[14,128,128]{2,1,0:T(8,128)(2,1)S(1)} %collective-permute-done.11.refs_0_.refs_6_), channel_id=1, source_target_pairs={{0,16},{16,0},{1,17},{17,1},{2,18},{18,2},{3,19},{19,3},{4,20},{20... | collective-permute-start | bytes 1376264 | tf_op jit(solution)/shard_map/down_part/ppermute | solution.py:110
  49.8 10.2 %collective-permute-start.14 = (bf16[28,32,128]{2,1,0:T(8,128)(2,1)S(1)}, bf16[28,32,128]{2,1,0:T(8,128)(2,1)S(1)}, u32[]{:S(2)}, u32[]{:S(2)}) collective-permute-start(bf16[28,32,128]{2,1,0:T(8,128)(2,1)S(1)} %get-tuple-element.120.refs_0_), channel_id=1, source_target_pairs={{0,4},{4,0},{8,12},{12,8},{1,5},{5,1},{9,13},{13,9},{2,6},{6,2},{1... | collective-permute-start | bytes 688136 | tf_op jit(solution)/shard_map/hidden_core/ppermute | solution.py:100
  50.0 10.0 %collective-permute-start.15 = (bf16[28,32,128]{2,1,0:T(8,128)(2,1)S(1)}, bf16[28,32,128]{2,1,0:T(8,128)(2,1)S(1)}, u32[]{:S(2)}, u32[]{:S(2)}) collective-permute-start(bf16[28,32,128]{2,1,0:T(8,128)(2,1)S(1)} %get-tuple-element.121.refs_1_), channel_id=1, source_target_pairs={{0,4},{4,0},{8,12},{12,8},{1,5},{5,1},{9,13},{13,9},{2,6},{6,2},{1... | collective-permute-start | bytes 688136 | tf_op jit(solution)/shard_map/hidden_core/ppermute | solution.py:100
  50.4 9.7 %collective-permute-start.16 = (bf16[28,32,128]{2,1,0:T(8,128)(2,1)S(1)}, bf16[28,32,128]{2,1,0:T(8,128)(2,1)S(1)}, u32[]{:S(2)}, u32[]{:S(2)}) collective-permute-start(bf16[28,32,128]{2,1,0:T(8,128)(2,1)S(1)} %get-tuple-element.122.refs_2_), channel_id=1, source_target_pairs={{0,4},{4,0},{8,12},{12,8},{1,5},{5,1},{9,13},{13,9},{2,6},{6,2},{1... | collective-permute-start | bytes 688136 | tf_op jit(solution)/shard_map/hidden_core/ppermute | solution.py:100
  50.5 9.5 %collective-permute-start.17 = (bf16[28,32,128]{2,1,0:T(8,128)(2,1)S(1)}, bf16[28,32,128]{2,1,0:T(8,128)(2,1)S(1)}, u32[]{:S(2)}, u32[]{:S(2)}) collective-permute-start(bf16[28,32,128]{2,1,0:T(8,128)(2,1)S(1)} %get-tuple-element.123.refs_3_), channel_id=1, source_target_pairs={{0,4},{4,0},{8,12},{12,8},{1,5},{5,1},{9,13},{13,9},{2,6},{6,2},{1... | collective-permute-start | bytes 688136 | tf_op jit(solution)/shard_map/hidden_core/ppermute | solution.py:100
  61.6 7.0 %collective-permute-start.19 = (bf16[7,128,128]{2,1,0:T(8,128)(2,1)S(1)}, bf16[7,128,128]{2,1,0:T(8,128)(2,1)S(1)}, u32[]{:S(2)}, u32[]{:S(2)}) collective-permute-start(bf16[7,128,128]{2,1,0:T(8,128)(2,1)S(1)} %shard_map.135), channel_id=1, source_target_pairs={{0,8},{4,12},{8,0},{12,4},{1,9},{5,13},{9,1},{13,5},{2,10},{6,14},... | collective-permute-start | bytes 688136 | tf_op jit(solution)/shard_map/down_grad_chip/ppermute | solution.py:104
  63.1 7.2 %collective-permute-start.20 = (bf16[14,128,128]{2,1,0:T(8,128)(2,1)S(1)}, bf16[14,128,128]{2,1,0:T(8,128)(2,1)S(1)}, u32[]{:S(2)}, u32[]{:S(2)}) collective-permute-start(bf16[14,128,128]{2,1,0:T(8,128)(2,1)S(1)} %collective-permute-done.11.refs_0_.refs_6_), channel_id=1, source_target_pairs={{0,4},{4,0},{8,12},{12,8},{1,5},{5,1},{9,13},{13,9},{2,6},{6,2},{1... | collective-permute-start | bytes 1376264 | tf_op jit(solution)/shard_map/down_x_core/ppermute | solution.py:100
  68.5 3.3 %collective-permute-start.21 = (bf16[14,128,128]{2,1,0:T(8,128)(2,1)S(1)}, bf16[14,128,128]{2,1,0:T(8,128)(2,1)S(1)}, u32[]{:S(2)}, u32[]{:S(2)}) collective-permute-start(bf16[14,128,128]{2,1,0:T(8,128)(2,1)S(1)} %collective-permute-done.18.refs_0_.refs_8_), channel_id=1, source_target_pairs={{0,4},{4,0},{8,12},{12,8},{1,5},{5,1},{9,13},{13,9},{2,6},{6,2},{1... | collective-permute-start | bytes 1376264 | tf_op jit(solution)/shard_map/down_y_core/ppermute | solution.py:100
  68.6 17.8 %collective-permute-start.26 = (bf16[21,128,128]{2,1,0:T(8,128)(2,1)S(1)}, bf16[21,128,128]{2,1,0:T(8,128)(2,1)S(1)}, u32[]{:S(2)}, u32[]{:S(2)}) collective-permute-start(bf16[21,128,128]{2,1,0:T(8,128)(2,1)S(1)} %shard_map.136), channel_id=1, source_target_pairs={{0,8},{4,12},{8,0},{12,4},{1,9},{5,13},{9,1},{13,5},{2,10},{6,14},... | collective-permute-start | bytes 2064392 | tf_op jit(solution)/shard_map/down_grad_chip/ppermute | solution.py:104
  73.3 5.5 %collective-permute-start.23 = (bf16[28,64,128]{2,1,0:T(8,128)(2,1)S(1)}, bf16[28,64,128]{2,1,0:T(8,128)(2,1)S(1)}, u32[]{:S(2)}, u32[]{:S(2)}) collective-permute-start(bf16[28,64,128]{2,1,0:T(8,128)(2,1)S(1)} %get-tuple-element.110.refs_2_.refs_0_), channel_id=1, source_target_pairs={{0,4},{4,0},{8,12},{12,8},{1,5},{5,1},{9,13},{13,9},{2,6},{6,2},{1... | collective-permute-start | bytes 1376264 | tf_op jit(solution)/shard_map/grads_core/ppermute | solution.py:100
  73.6 5.1 %collective-permute-start.24 = (bf16[28,64,128]{2,1,0:T(8,128)(2,1)S(1)}, bf16[28,64,128]{2,1,0:T(8,128)(2,1)S(1)}, u32[]{:S(2)}, u32[]{:S(2)}) collective-permute-start(bf16[28,64,128]{2,1,0:T(8,128)(2,1)S(1)} %get-tuple-element.111.refs_3_.refs_1_), channel_id=1, source_target_pairs={{0,4},{4,0},{8,12},{12,8},{1,5},{5,1},{9,13},{13,9},{2,6},{6,2},{1... | collective-permute-start | bytes 1376264 | tf_op jit(solution)/shard_map/grads_core/ppermute | solution.py:100
  73.9 39.0 %collective-permute-start.28 = (bf16[28,128,128]{2,1,0:T(8,128)(2,1)S(1)}, bf16[28,128,128]{2,1,0:T(8,128)(2,1)S(1)}, u32[]{:S(2)}, u32[]{:S(2)}) collective-permute-start(bf16[28,128,128]{2,1,0:T(8,128)(2,1)S(1)} %get-tuple-element.112.refs_2_), channel_id=1, source_target_pairs={{0,4},{4,0},{8,12},{12,8},{1,5},{5,1},{9,13},{13,9},{2,6},{6,2},{1... | collective-permute-start | bytes 2752520 | tf_op jit(solution)/shard_map/grads_core/ppermute | solution.py:100
  78.8 10.7 %copy-start.5 = (bf16[1,28,128,128]{3,2,1,0:T(8,128)(2,1)S(1)}, bf16[1,28,128,128]{3,2,1,0:T(8,128)(2,1)}, u32[]{:S(2)}) copy-start(bf16[1,28,128,128]{3,2,1,0:T(8,128)(2,1)} %param.11) | copy-start | bytes 2752516
  86.4 30.7 %collective-permute-start.27 = (bf16[28,128,128]{2,1,0:T(8,128)(2,1)S(1)}, bf16[28,128,128]{2,1,0:T(8,128)(2,1)S(1)}, u32[]{:S(2)}, u32[]{:S(2)}) collective-permute-start(bf16[28,128,128]{2,1,0:T(8,128)(2,1)S(1)} %shard_map.140), channel_id=1, source_target_pairs={{0,8},{4,12},{8,0},{12,4},{1,9},{5,13},{9,1},{13,5},{2,10},{6,14},... | collective-permute-start | bytes 2752520 | tf_op jit(solution)/shard_map/gate_grad_chip/ppermute | solution.py:104
  88.1 20.6 %collective-permute-start.22 = (bf16[2,128,1024]{2,1,0:T(8,128)(2,1)S(1)}, bf16[2,128,1024]{2,1,0:T(8,128)(2,1)S(1)}, u32[]{:S(2)}, u32[]{:S(2)}) collective-permute-start(bf16[2,128,1024]{2,1,0:T(8,128)(2,1)S(1)} %get-tuple-element.107), channel_id=1, source_target_pairs={{0,1},{1,0},{2,3},{3,2},{4,5},{5,4},{6,7},{7,6},{8,9},{9,8},{10,11... | collective-permute-start | bytes 1572872 | tf_op jit(solution)/shard_map/out_group/ppermute | solution.py:114
  102.1 18.8 %collective-permute-start.29 = (bf16[2,128,1024]{2,1,0:T(8,128)(2,1)S(1)}, bf16[2,128,1024]{2,1,0:T(8,128)(2,1)S(1)}, u32[]{:S(2)}, u32[]{:S(2)}) collective-permute-start(bf16[2,128,1024]{2,1,0:T(8,128)(2,1)S(1)} %get-tuple-element.114), channel_id=1, source_target_pairs={{0,1},{1,0},{2,3},{3,2},{4,5},{5,4},{6,7},{7,6},{8,9},{9,8},{10,11... | collective-permute-start | bytes 1572872 | tf_op jit(solution)/shard_map/token_group/ppermute | solution.py:114
  109.0 12.2 %collective-permute-start.25 = (bf16[1,128,1024]{2,1,0:T(8,128)(2,1)S(1)}, bf16[1,128,1024]{2,1,0:T(8,128)(2,1)S(1)}, u32[]{:S(2)}, u32[]{:S(2)}) collective-permute-start(bf16[1,128,1024]{2,1,0:T(8,128)(2,1)S(1)} %slice.21), channel_id=1, source_target_pairs={{0,2},{1,3},{2,0},{3,1},{4,6},{5,7},{6,4},{7,5},{8,10},{9,11},{10,... | collective-permute-start | bytes 786440 | tf_op jit(solution)/shard_map/out_group/ppermute | solution.py:114
  117.2 20.2 %collective-permute-start.31 = (bf16[28,128,128]{2,1,0:T(8,128)(2,1)S(1)}, bf16[28,128,128]{2,1,0:T(8,128)(2,1)S(1)}, u32[]{:S(2)}, u32[]{:S(2)}) collective-permute-start(bf16[28,128,128]{2,1,0:T(8,128)(2,1)S(1)} %shard_map.145), channel_id=1, source_target_pairs={{0,8},{4,12},{8,0},{12,4},{1,9},{5,13},{9,1},{13,5},{2,10},{6,14},... | collective-permute-start | bytes 2752520 | tf_op jit(solution)/shard_map/up_grad_chip/ppermute | solution.py:104
  121.1 14.2 %collective-permute-start.30 = (bf16[1,128,1024]{2,1,0:T(8,128)(2,1)S(1)}, bf16[1,128,1024]{2,1,0:T(8,128)(2,1)S(1)}, u32[]{:S(2)}, u32[]{:S(2)}) collective-permute-start(bf16[1,128,1024]{2,1,0:T(8,128)(2,1)S(1)} %slice.23), channel_id=1, source_target_pairs={{0,2},{1,3},{2,0},{3,1},{4,6},{5,7},{6,4},{7,5},{8,10},{9,11},{10,... | collective-permute-start | bytes 786440 | tf_op jit(solution)/shard_map/token_group/ppermute | solution.py:114

commit v3 on v2

--- a/solution.py
+++ b/solution.py
@@ -47,13 +47,13 @@
 
     def first(self, where, piece):
         chip, core, part = where[0], where[1], where[2]
-        back, other, half = piece
+        back, other, half, offset = piece
         chip = lax.rem(chip + (self.chips - back), self.chips)
         core = 1 - core if other else core
         start = (chip * 2 + core) * self.shard
         if half is not None:
             start = start + (1 - part if half else part) * (self.shard // 2)
-        return start
+        return start + offset
 
 
 def over_live(live, terms, store):
@@ -133,12 +133,13 @@
         hidden_bf16 = jax.ShapeDtypeStruct((hidden_blocks, token_count, size), BF16)
 
         own = [gate_blocks[0], up_blocks[0], down_blocks[0]]
-        near_keys = [(0, False, None), (0, True, None)]
+        near_keys = [(0, False, None, 0), (0, True, None, 0)]
         away = tuple(range(1, chips))
         near_half, far_half = (False, True) if halves else (None, None)
-        direct_keys = [(k, other, near_half) for k in away for other in (False, True)]
-        relay_keys = [(k, other, far_half) for k in away for other in (False, True)] if halves else []
-        all_keys = near_keys + direct_keys + relay_keys
+        direct_keys = [(k, other, near_half, 0) for k in away for other in (False, True)]
+        relay_keys = [(k, other, far_half, 0) for k in away for other in (False, True)] if halves else []
+        every = near_keys + direct_keys + relay_keys
+        all_keys = [every, every, every]
         cut = own
         if halves:
             cut = [
@@ -153,7 +154,7 @@
             return arrived
 
         names = ("gate", "up", "down")
-        near = [[w, pair_swap(w, name)] for w, name in zip(own[:2], names)]
+        near = [[w, pair_swap(w, name)] for w, name in zip(own, names)]
 
         def both(name, pieces):
             return [q for w in pieces for q in (w, pair_swap(w, name))]
@@ -207,21 +208,54 @@
         cotangent_pair = pair_swap(cotangent, "cotangent")
 
         x_g = shift_all("gate", cut[0])
-        x_g = after(x_g, acc_g, tokens_pair, cotangent_pair)
+        x_g = after(x_g, acc_g, cotangent_pair)
         x_u = shift_all("up", cut[1], *x_g)
         y_g = relayed("gate", x_g)
 
-        near.append([own[2], pair_swap(after(own[2], *x_g), "down")])
+        acc_h = begin(2, cotangent, near[2], near_keys)
         direct = [both("gate_x", after(x_g, acc_u))]
-        x_u, y_g = after((x_u, y_g), acc_u)
+        x_u, y_g = after((x_u, y_g), acc_u, acc_h)
         x_d = shift_all("down", cut[2], *x_u)
-        acc_g = go_on(0, after(acc_g, *x_u), tokens, direct[0], direct_keys)
+
+        low = cut[1].shape[0] // 2
+        sizes = (low, cut[1].shape[0] - low)
+        n_fresh, n_direct = len(x_u), len(direct_keys)
+
+        def direct_body(where_ref, counts_ref, tg, acc_in, x_ref, *refs):
+            w_refs, refs = refs[:n_direct], refs[n_direct:]
+            fresh, acc, outs = refs[:n_fresh], refs[n_fresh], refs[n_fresh + 1 :]
+            for i, w_ref in enumerate(fresh):
+                outs[2 * i][...] = w_ref[:low]
+                outs[2 * i + 1][...] = w_ref[low:]
+            add_pieces(acc, 0, x_ref, w_refs, direct_keys, tg, counts_ref, where_ref)
+
+        acc_g, *split = call(
+            direct_body,
+            [where, counts, tables[0]],
+            [acc_g, tokens, *direct[0], *x_u],
+            [hidden_f32] + [jax.ShapeDtypeStruct((n, size, size), BF16) for n in sizes] * n_fresh,
+            products=2 * shard,
+            aliases={3: 0},
+        )
+
+        def split_swap(name, pieces, halved, half):
+            blocks, its_keys = [], []
+            for k, w in enumerate(pieces):
+                blocks += [w] + [pair_swap(h, name) for h in halved[2 * k : 2 * k + 2]]
+                its_keys += [(k + 1, other, half, o) for other, o in ((False, 0), (True, 0), (True, low))]
+            return blocks, its_keys
+
+        up_direct, up_keys = split_swap("up_x", x_u, split, near_half)
+        all_keys[1] = near_keys + up_keys + relay_keys
         y_u = relayed("up", x_u)
-        direct.append(both("up_x", after(x_u, acc_g)))
-        acc_h = begin(2, cotangent, near[2], near_keys)
-        relay = [both("gate_y", after(y_g, acc_g))]
-
-        acc_u = go_on(1, acc_u, tokens, direct[1], direct_keys)
+        direct.append(up_direct)
+        acc_u = go_on(1, acc_u, tokens, up_direct, up_keys)
+
+        x_d = after(x_d, acc_u)
+        y_u = after(y_u, *x_d)
+        y_d = relayed("down", x_d, *y_u)
+        direct.append(both("down_x", x_d))
+        relay = [both("gate_y", after(y_g, *x_d)), both("up_y", y_u)]
 
         def gate_body(where_ref, counts_ref, tg, acc_in, x_ref, *refs):
             w_refs, silu_ref, slope_ref, acc = refs[:-3], *refs[-3:]
@@ -245,12 +279,6 @@
             scratch=[pltpu.VMEM(hidden_f32.shape, F32)],
             products=shard,
         )
-        x_d = after(x_d, acc_u, silu, acc_h)
-        y_u = after(y_u, *x_d)
-        y_d = relayed("down", x_d, *y_u)
-        direct.append(both("down_x", x_d))
-        relay.append(both("up_y", y_u))
-
         quarter = token_count // 4
 
         def up_body(where_ref, counts_ref, tu, acc_in, silu_ref, x_ref, *refs):
@@ -276,7 +304,7 @@
             aliases={3: 0},
             products=shard + 20,
         )
-        hidden_pair = after([pair_swap(h, "hidden") for h in hidden], *y_d)
+        hidden_pair = [pair_swap(h, "hidden") for h in hidden]
 
         def block_grads(m, ahead, left, right, cuts=(0, shard)):
             spans = [(k, low, high) for k in ahead for low, high in zip(cuts, cuts[1:])]
@@ -286,7 +314,7 @@
             def body(where_ref, counts_ref, table, *refs):
                 ls, rs, outs = refs[:n_left], refs[n_left:n_both], refs[n_both:]
                 for (k, low, high), o_ref in zip(spans, outs):
-                    first = place.first(where_ref, ((chips - k) % chips, False, None)) + low
+                    first = place.first(where_ref, ((chips - k) % chips, False, None, 0)) + low
                     live = live_in(counts_ref[m], first, high - low)
 
                     def terms(s, first=first):
@@ -322,23 +350,11 @@
             return value.astype(BF16)[None]
 
         down_operands = ([*hidden, *hidden_pair], [cotangent, cotangent_pair])
-        cuts = tuple(sorted({0, max(shard // 4, 1), shard}))
-        down_away = [block_grads(2, away, *down_operands, cuts=cuts[:2])]
-        held = [*after(hidden, *down_away[0]), *hidden_pair]
-        rest = block_grads(2, away, held, down_operands[1], cuts=cuts[1:])
-        steps = len(cuts) - 2
-        down_away += [rest[i::steps] for i in range(steps)]
-        hurry = [g for grads in down_away[1:] for g in grads]
-        down_far = []
-        for grads in down_away:
-            grads = after(grads, *(down_far[-1] if down_far else []))
-            down_far.append([chip_shift(g, k, "down_grad") for g, k in zip(grads, away)])
-            if hurry:
-                down_far[0], hurry = after(down_far[0], *hurry), []
-        down_lead, down_last = down_far[0], down_far[-1]
-
-        relay.append(both("down_y", after(y_d, *down_lead)))
-        acc_h = go_on(2, after(acc_h, *down_lead), cotangent, direct[2], direct_keys)
+        down_away = block_grads(2, away, *down_operands)
+        down_far = [chip_shift(g, k, "down_grad") for g, k in zip(down_away, away)]
+
+        relay.append(both("down_y", after(y_d, *down_away)))
+        acc_h = go_on(2, after(acc_h, *down_away), cotangent, direct[2], direct_keys)
 
         half_tokens = token_count // 2
 
@@ -380,9 +396,9 @@
 
         def out_body(where_ref, counts_ref, td, *refs):
             h_refs, refs = refs[:4], refs[4:]
-            w_refs, outs, acc = refs[: len(all_keys)], refs[len(all_keys) : -1], refs[-1]
+            w_refs, outs, acc = refs[: len(every)], refs[len(every) : -1], refs[-1]
             zero(acc)
-            for w_ref, key in zip(w_refs, all_keys):
+            for w_ref, key in zip(w_refs, every):
                 first = place.first(where_ref, key)
 
                 def terms(s, w_ref=w_ref, first=first):
@@ -408,36 +424,48 @@
         grads_pair = [pair_swap(g, "grads") for g in grads]
         grads_pair[:2] = after(grads_pair[:2], *out_parts)
         gate_operands = ([tokens, tokens_pair], [*grads[:2], *grads_pair[:2]])
-        up_operands = ([tokens, tokens_pair], [grads[2], after(grads_pair[2], *down_last)])
+        up_operands = ([tokens, tokens_pair], [grads[2], grads_pair[2]])
         gate_away = block_grads(0, away, *gate_operands)
-
-        def token_body(where_ref, counts_ref, tg, tu, *refs):
-            ys, refs = refs[:3], refs[3:]
-            n = len(all_keys)
-            outs, acc = refs[2 * n : -1], refs[-1]
-            zero(acc)
-            for m, table in ((0, tg), (1, tu)):
-                for w_ref, key in zip(refs[m * n : (m + 1) * n], all_keys):
-                    first = place.first(where_ref, key)
-
-                    def terms(s, m=m, table=table, w_ref=w_ref, first=first):
-                        h = table[1, first + s]
-                        y = ys[2][h] if m else jnp.concatenate([ys[0][h], ys[1][h]], axis=0)
-                        return mm(y, w_ref[s], NT)
-
-                    def store(s, value, table=table, first=first):
-                        acc[table[0, first + s]] += value
-
-                    over_live(live_in(counts_ref[m], first, w_ref.shape[0]), terms, store)
-            deal(where_ref, acc, outs)
-
-        token_parts = call(
-            token_body,
-            [where, counts, tables[0], tables[1]],
-            [*after(grads, *gate_away), *pieces[0], *pieces[1]],
-            [chunk] * 2,
-            scratch=[model_acc],
-            products=8 * shard,
+        up_away = block_grads(1, away, *up_operands)
+        down_far = after(down_far, *gate_away)
+
+        def token_body(m, last, where_ref, counts_ref, table, *refs):
+            n, n_y = len(all_keys[m]), 1 if m else 2
+            ys, w_refs, acc = refs[:n_y], refs[n_y : n_y + n], refs[-1]
+            if not last:
+                zero(acc)
+            for w_ref, key in zip(w_refs, all_keys[m]):
+                first = place.first(where_ref, key)
+
+                def terms(s, w_ref=w_ref, first=first):
+                    h = table[1, first + s]
+                    y = jnp.concatenate([y_ref[h] for y_ref in ys], axis=0)
+                    return mm(y, w_ref[s], NT)
+
+                def store(s, value, first=first):
+                    acc[table[0, first + s]] += value
+
+                over_live(live_in(counts_ref[m], first, w_ref.shape[0]), terms, store)
+            if last:
+                deal(where_ref, acc, refs[-3:-1])
+
+        model_f32 = jax.ShapeDtypeStruct((model_blocks, token_count, size), F32)
+        (token_acc,) = call(
+            functools.partial(token_body, 0, False),
+            [where, counts, tables[0]],
+            [*after(grads[:2], *gate_away), *pieces[0]],
+            [model_f32],
+            products=4 * shard,
+        )
+        down_far = after(down_far, token_acc)
+        y_up = after(grads[2], *down_far)
+        *token_parts, _ = call(
+            functools.partial(token_body, 1, True),
+            [where, counts, tables[1]],
+            [y_up, *pieces[1], token_acc],
+            [chunk] * 2 + [model_f32],
+            products=4 * shard,
+            aliases={4 + len(pieces[1]): 2},
         )
 
         def swap_groups(name, chunks, *others):
@@ -456,22 +484,21 @@
             value = kept.astype(F32) + after(arrived, *others).astype(F32)
             return value[0].astype(BF16)
 
-        up_away = block_grads(1, away, *up_operands)
-        down_last = down_far[-1] = after(down_last, *gate_away)
-        gate_far = [chip_shift(g, k, "gate_grad") for g, k in zip(after(gate_away, *down_last), away)]
-        kept_t, kept_h = after((tokens, hidden), *down_last)
-        (down_kept,) = block_grads(2, (0,), [*kept_h, *hidden_pair], down_operands[1])
-        (gate_kept,) = block_grads(0, (0,), [kept_t, tokens_pair], gate_operands[1])
-        (up_kept,) = block_grads(1, (0,), [kept_t, tokens_pair], up_operands[1])
-        joined = [jnp.concatenate(steps, axis=0) for steps in zip(*down_far)]
-        down_grad = total(down_kept, joined)
+        gate_sent = after(gate_away, *down_far)
+        gate_far = [chip_shift(g, k, "gate_grad") for g, k in zip(gate_sent, away)]
         out_first, *out_terms = swap_groups("out", out_parts, *token_parts)
-        gate_far = after(gate_far, down_grad, gate_kept, up_kept, out_first, *up_away)
-        up_far = [chip_shift(g, k, "up_grad") for g, k in zip(after(up_away, *gate_far), away)]
+        up_sent = after(up_away, out_first)
+        up_far = [chip_shift(g, k, "up_grad") for g, k in zip(up_sent, away)]
+        late_h, late_t = after(hidden, out_first), after(tokens, *gate_far)
+        (down_kept,) = block_grads(2, (0,), [*late_h, *hidden_pair], down_operands[1])
+        (gate_kept,) = block_grads(0, (0,), [late_t, tokens_pair], gate_operands[1])
+        (up_kept,) = block_grads(1, (0,), [late_t, tokens_pair], up_operands[1])
+        down_grad = total(down_kept, down_far)
+        gate_far = after(gate_far, down_grad)
+        layer_out = last_sum(*out_terms, *gate_far)
+        _, *token_terms = swap_groups("token", token_parts, *gate_far)
         gate_grad = total(gate_kept, gate_far)
-        layer_out = last_sum(*out_terms, gate_grad)
-        _, *token_terms = swap_groups("token", token_parts, gate_grad)
-        token_grad = last_sum(*token_terms, layer_out)
+        token_grad = last_sum(*token_terms, layer_out, gate_grad)
         up_grad = total(up_kept, after(up_far, token_grad))
         return layer_out, token_grad, gate_grad, up_grad, down_grad
 

time: 139 us -> 125 us (0.90); the launches traced: 139 us -> 123 us
  waiting for transfers between devices: 47.4 us -> 29.4 us
  starting transfers between devices: 25.4 us -> 29.8 us
  Pallas kernels: 54.9 us -> 52.9 us
    ppermute x3, waiting for transfers between devices: 10.8 us -> 3.84 us  [part_swap(): return lax.ppermute(a, 'parts', [(0, 1), (1, 0)])]
    ppermute x4, waiting for transfers between devices: 14.6 us -> 7.73 us  [group_swap(): return lax.ppermute(a, 'tensor', [(i, i ^ bit) for i in range(groups)])]
    ppermute x7 -> x6, waiting for transfers between devices: 21.5 us -> 15.3 us  [chip_shift(): lax.ppermute(a, 'dp', [(i, (i // 2 + k) % chips * 2 + i % 2) for i in ran...]
    ppermute x4, starting transfers between devices: 5.34 us -> 9.57 us  [group_swap(): return lax.ppermute(a, 'tensor', [(i, i ^ bit) for i in range(groups)])]
    ppermute x18 -> x19, waiting for transfers between devices: 0.42 us -> 2.48 us  [pair_swap(): return lax.ppermute(a, 'dp', [(i, i ^ 1) for i in range(dp)])]
    pallas_call x18, Pallas kernels: 54.9 us -> 52.9 us  [call(): pl.pallas_call(body, out_shape=outs, in_specs=[SMEM] * len(ints) + [VMEM]...]
    ppermute x7 -> x6, starting transfers between devices: 11.5 us -> 11.4 us  [chip_shift(): lax.ppermute(a, 'dp', [(i, (i // 2 + k) % chips * 2 + i % 2) for i in ran...]
    ppermute x18 -> x19, starting transfers between devices: 4.15 us -> 4.2 us  [pair_swap(): return lax.ppermute(a, 'dp', [(i, i ^ 1) for i in range(dp)])]
  transfers between devices with their start and end apart: 32 -> 32, of which waited for: 12 -> 16; matrix products, arithmetic and copies ran while one was open for 5% -> 6% of each run, Pallas kernels for 38% -> 43%
where the time goes in v3:
time: 125 us; the launch traced here: 123 us
  Pallas kernels  52.9 us (42%)
  starting transfers between devices  29.8 us (24%)
  waiting for transfers between devices  29.4 us (24%)
  other arithmetic  5.75 us (5%)
  local copies, waits for them, and re-layouts  4.16 us (3%)
    pallas_call x18, Pallas kernels, call(): pl.pallas_call(body, out_shape=outs, in_specs=[SMEM] * len(ints) + [VMEM]...  52.9 us
    ppermute x6, waiting for transfers between devices, chip_shift(): lax.ppermute(a, 'dp', [(i, (i // 2 + k) % chips * 2 + i % 2) for i in ran...  15.3 us
    ppermute x6, starting transfers between devices, chip_shift(): lax.ppermute(a, 'dp', [(i, (i // 2 + k) % chips * 2 + i % 2) for i in ran...  11.4 us
    ppermute x4, starting transfers between devices, group_swap(): return lax.ppermute(a, 'tensor', [(i, i ^ bit) for i in range(groups)])  9.57 us
    ppermute x4, waiting for transfers between devices, group_swap(): return lax.ppermute(a, 'tensor', [(i, i ^ bit) for i in range(groups)])  7.73 us
    ppermute x3, starting transfers between devices, part_swap(): return lax.ppermute(a, 'parts', [(0, 1), (1, 0)])  4.63 us
    ppermute x19, starting transfers between devices, pair_swap(): return lax.ppermute(a, 'dp', [(i, i ^ 1) for i in range(dp)])  4.2 us
    ppermute x3, waiting for transfers between devices, part_swap(): return lax.ppermute(a, 'parts', [(0, 1), (1, 0)])  3.84 us
  transfers between devices with their start and end apart: 32, of which 16 were waited for; matrix products, arithmetic and copies ran while one was open for 6% of the time, Pallas kernels for 43%

profile of v3, /device:TPU:0, one launch (start us, length us, event | category | flops | bytes accessed | tf_op | source)
XLA Modules:
  0.0 123.0 jit_solution(11643405008524599988)
XLA Ops:
  0.7 0.5 collective-permute-start.3
  1.7 1.8 %dynamic-slice_bitcast_fusion.1 = bf16[14,128,128]{2,1,0:T(8,128)(2,1)} fusion(bf16[1,28,128,128]{3,2,1,0:T(8,128)(2,1)} %param.11, s32[]{:T(128)S(6)} %select_n.18), kind=kLoop, calls=%fused_computation.11 | loop fusion | bytes 917508 | tf_op jit(solution)/shard_map/dynamic_slice | solution.py:146
  3.5 2.6 %collective-permute-start.1 = (bf16[14,128,128]{2,1,0:T(8,128)(2,1)}, bf16[14,128,128]{2,1,0:T(8,128)(2,1)S(1)}, u32[]{:S(2)}, u32[]{:S(2)}) collective-permute-start(bf16[14,128,128]{2,1,0:T(8,128)(2,1)} %dynamic-slice_bitcast_fusion.1), channel_id=1, source_target_pairs={{0,8},{4,12},{8,0},{12,4},{1,9},{5,13},{9,1},{13,5},{2,10},{6,14},... | collective-permute-start | bytes 1376264 | tf_op jit(solution)/shard_map/gate_chip/ppermute | solution.py:104
  6.3 1.1 dynamic-slice_bitcast_fusion.2
  7.4 1.2 copy-done.2
  8.6 4.0 %shard_map.129.acc_in = f32[28,128,128]{2,1,0:T(8,128)S(1)} custom-call(s32[4]{0:T(128)S(1)} %pad_add_fusion.where_ref, s32[3]{0:T(128)S(1)} %bitcast.36, s32[2,112]{1,0:T(2,128)S(1)} %bitcast.66, bf16[128,4096]{1,0:T(8,128)(2,1)S(1)} %copy-done, bf16[28,128,128]{2,1,0:T(8,128)(2,1)S(1)} %bitcast.28, bf16[28,128,128]{2,1,0:T(8,128)(2,1)} %collective-permute-done.2.refs_1_.refs_3_), custom_call_target="tpu_custom_call" | custom-call | flops 56 | bytes 56 | tf_op jit(solution)/shard_map/pallas_call | solution.py:30
  12.6 4.8 %collective-permute-done.1.refs_0_.refs_4_ = bf16[14,128,128]{2,1,0:T(8,128)(2,1)S(1)} collective-permute-done((bf16[14,128,128]{2,1,0:T(8,128)(2,1)}, bf16[14,128,128]{2,1,0:T(8,128)(2,1)S(1)}, u32[]{:S(2)}, u32[]{:S(2)}) %collective-permute-start.1) | collective-permute-done | bytes 458784 | tf_op jit(solution)/shard_map/gate_chip/ppermute | solution.py:104
  17.4 1.8 %collective-permute-start.4 = (bf16[14,128,128]{2,1,0:T(8,128)(2,1)S(1)}, bf16[14,128,128]{2,1,0:T(8,128)(2,1)S(1)}, u32[]{:S(2)}, u32[]{:S(2)}) collective-permute-start(bf16[14,128,128]{2,1,0:T(8,128)(2,1)S(1)} %dynamic-slice_bitcast_fusion.2), channel_id=1, source_target_pairs={{0,8},{4,12},{8,0},{12,4},{1,9},{5,13},{9,1},{13,5},{2,10},{6,14},... | collective-permute-start | bytes 1376264 | tf_op jit(solution)/shard_map/up_chip/ppermute | solution.py:104
  19.2 1.5 %collective-permute-start.5 = (bf16[14,128,128]{2,1,0:T(8,128)(2,1)S(1)}, bf16[14,128,128]{2,1,0:T(8,128)(2,1)S(1)}, u32[]{:S(2)}, u32[]{:S(2)}) collective-permute-start(bf16[14,128,128]{2,1,0:T(8,128)(2,1)S(1)} %collective-permute-done.1.refs_0_.refs_4_), channel_id=1, source_target_pairs={{0,16},{16,0},{1,17},{17,1},{2,18},{18,2},{3,19},{19,3},{4,20},{20... | collective-permute-start | bytes 1376264 | tf_op jit(solution)/shard_map/gate_part/ppermute | solution.py:110
  20.7 2.6 %shard_map.128.acc_in = f32[28,128,128]{2,1,0:T(8,128)S(1)} custom-call(s32[4]{0:T(128)S(1)} %pad_add_fusion.where_ref, s32[3]{0:T(128)S(1)} %bitcast.37, s32[2,112]{1,0:T(2,128)S(1)} %bitcast.54, bf16[128,4096]{1,0:T(8,128)(2,1)S(1)} %copy-done, bf16[28,128,128]{2,1,0:T(8,128)(2,1)S(1)} %bitcast.31, ...), custom_call_target="tpu_custom_call" | custom-call | flops 56 | bytes 56 | tf_op jit(solution)/shard_map/pallas_call | solution.py:30
  23.4 4.3 %shard_map.130.acc_in = f32[28,128,128]{2,1,0:T(8,128)S(1)} custom-call(s32[4]{0:T(128)S(1)} %pad_add_fusion.where_ref, s32[3]{0:T(128)S(1)} %bitcast.38, s32[2,112]{1,0:T(2,128)S(1)} %bitcast.60, bf16[128,4096]{1,0:T(8,128)(2,1)S(1)} %copy-done.1, bf16[28,128,128]{2,1,0:T(8,128)(2,1)S(1)} %bitcast.34, ...), custom_call_target="tpu_custom_call" | custom-call | flops 56 | bytes 56 | tf_op jit(solution)/shard_map/pallas_call | solution.py:30
  27.8 1.9 %collective-permute-done.4.refs_2_.refs_0_.refs_3_ = bf16[14,128,128]{2,1,0:T(8,128)(2,1)S(1)} collective-permute-done((bf16[14,128,128]{2,1,0:T(8,128)(2,1)S(1)}, bf16[14,128,128]{2,1,0:T(8,128)(2,1)S(1)}, u32[]{:S(2)}, u32[]{:S(2)}) %collective-permute-start.4) | collective-permute-done | bytes 458784 | tf_op jit(solution)/shard_map/up_chip/ppermute | solution.py:104
  29.7 1.3 %collective-permute-done.5.refs_0_.refs_6_ = bf16[14,128,128]{2,1,0:T(8,128)(2,1)S(1)} collective-permute-done((bf16[14,128,128]{2,1,0:T(8,128)(2,1)S(1)}, bf16[14,128,128]{2,1,0:T(8,128)(2,1)S(1)}, u32[]{:S(2)}, u32[]{:S(2)}) %collective-permute-start.5) | collective-permute-done | bytes 458784 | tf_op jit(solution)/shard_map/gate_part/ppermute | solution.py:110
  31.4 1.6 %collective-permute-start.12 = (bf16[14,128,128]{2,1,0:T(8,128)(2,1)S(1)}, bf16[14,128,128]{2,1,0:T(8,128)(2,1)S(1)}, u32[]{:S(2)}, u32[]{:S(2)}) collective-permute-start(bf16[14,128,128]{2,1,0:T(8,128)(2,1)S(1)} %collective-permute-done.4.refs_2_.refs_0_.refs_3_), channel_id=1, source_target_pairs={{0,16},{16,0},{1,17},{17,1},{2,18},{18,2},{3,19},{19,3},{4,20},{20... | collective-permute-start | bytes 1376264 | tf_op jit(solution)/shard_map/up_part/ppermute | solution.py:110
  33.0 2.2 %shard_map.131 = (f32[28,128,128]{2,1,0:T(8,128)S(1)}, bf16[7,128,128]{2,1,0:T(8,128)(2,1)S(1)}, bf16[7,128,128]{2,1,0:T(8,128)(2,1)S(1)}) custom-call(s32[4]{0:T(128)S(1)} %pad_add_fusion.where_ref, s32[3]{0:T(128)S(1)} %bitcast.39, s32[2,112]{1,0:T(2,128)S(1)} %bitcast.67, f32[28,128,128]{2,1,0:T(8,128)S(1)} %shard_map.129.acc_in, ...), custom_call_target="tpu_custom_call", output_to_operand_aliasing={{0}: (3, {})} | custom-call | flops 56 | bytes 56 | tf_op jit(solution)/shard_map/pallas_call | solution.py:30
  35.8 1.0 collective-permute-done.8.refs_1_.refs_4_
  37.1 0.6 shard_map.132.acc_in
  37.7 4.1 %collective-permute-done.10.refs_0_.refs_6_ = bf16[14,128,128]{2,1,0:T(8,128)(2,1)S(1)} collective-permute-done((bf16[14,128,128]{2,1,0:T(8,128)(2,1)S(1)}, bf16[14,128,128]{2,1,0:T(8,128)(2,1)S(1)}, u32[]{:S(2)}, u32[]{:S(2)}) %collective-permute-start.10) | collective-permute-done | bytes 458784 | tf_op jit(solution)/shard_map/down_chip/ppermute | solution.py:104
  42.4 1.5 %collective-permute-start.19 = (bf16[14,128,128]{2,1,0:T(8,128)(2,1)S(1)}, bf16[14,128,128]{2,1,0:T(8,128)(2,1)S(1)}, u32[]{:S(2)}, u32[]{:S(2)}) collective-permute-start(bf16[14,128,128]{2,1,0:T(8,128)(2,1)S(1)} %collective-permute-done.10.refs_0_.refs_6_), channel_id=1, source_target_pairs={{0,16},{16,0},{1,17},{17,1},{2,18},{18,2},{3,19},{19,3},{4,20},{20... | collective-permute-start | bytes 1376264 | tf_op jit(solution)/shard_map/down_part/ppermute | solution.py:110
  43.9 3.0 %shard_map.133 = (f32[28,128,128]{2,1,0:T(8,128)S(1)}, f32[28,128,128]{2,1,0:T(8,128)S(1)}) custom-call(s32[4]{0:T(128)S(1)} %pad_add_fusion.where_ref, s32[3]{0:T(128)S(1)} %bitcast.41, s32[2,112]{1,0:T(2,128)S(1)} %bitcast.68, f32[28,128,128]{2,1,0:T(8,128)S(1)} %get-tuple-element.64.acc_in, bf16[128,4096]{1,0:T(8,128)(2,1)S(1)} %copy-done, ...), custom_call_target="tpu_custom_call" | custom-call | flops 28 | bytes 28 | tf_op jit(solution)/shard_map/pallas_call | solution.py:30
  46.9 0.9 shard_map.134
  50.4 2.6 %shard_map.135 = bf16[28,128,128]{2,1,0:T(8,128)(2,1)S(1)} custom-call(s32[4]{0:T(128)S(1)} %pad_add_fusion.where_ref, s32[3]{0:T(128)S(1)} %bitcast.43, s32[2,112]{1,0:T(2,128)S(1)} %bitcast.61, bf16[28,32,128]{2,1,0:T(8,128)(2,1)S(1)} %get-tuple-element.100.refs_0_, bf16[28,32,128]{2,1,0:T(8,128)(2,1)S(1)} %get-tuple-element.101.refs_1_, ...), custom_call_target="tpu_custom_call" | custom-call | flops 28 | bytes 28 | tf_op jit(solution)/shard_map/pallas_call | solution.py:30
  53.0 2.2 %collective-permute-done.19.refs_0_.refs_8_ = bf16[14,128,128]{2,1,0:T(8,128)(2,1)S(1)} collective-permute-done((bf16[14,128,128]{2,1,0:T(8,128)(2,1)S(1)}, bf16[14,128,128]{2,1,0:T(8,128)(2,1)S(1)}, u32[]{:S(2)}, u32[]{:S(2)}) %collective-permute-start.19) | collective-permute-done | bytes 458784 | tf_op jit(solution)/shard_map/down_part/ppermute | solution.py:110
  55.2 1.4 %collective-permute-start.22 = (bf16[28,128,128]{2,1,0:T(8,128)(2,1)S(1)}, bf16[28,128,128]{2,1,0:T(8,128)(2,1)S(1)}, u32[]{:S(2)}, u32[]{:S(2)}) collective-permute-start(bf16[28,128,128]{2,1,0:T(8,128)(2,1)S(1)} %shard_map.135), channel_id=1, source_target_pairs={{0,8},{4,12},{8,0},{12,4},{1,9},{5,13},{9,1},{13,5},{2,10},{6,14},... | collective-permute-start | bytes 2752520 | tf_op jit(solution)/shard_map/down_grad_chip/ppermute | solution.py:104
  56.5 1.8 %shard_map.136.acc_in = f32[28,128,128]{2,1,0:T(8,128)S(1)} custom-call(s32[4]{0:T(128)S(1)} %pad_add_fusion.where_ref, s32[3]{0:T(128)S(1)} %bitcast.44, s32[2,112]{1,0:T(2,128)S(1)} %bitcast.62, f32[28,128,128]{2,1,0:T(8,128)S(1)} %shard_map.130.acc_in, bf16[128,4096]{1,0:T(8,128)(2,1)S(1)} %copy-done.1, ...), custom_call_target="tpu_custom_call", output_to_operand_aliasing={{}: (3, {})} | custom-call | flops 28 | bytes 28 | tf_op jit(solution)/shard_map/pallas_call | solution.py:30
  58.4 2.2 %shard_map.137 = (bf16[28,64,128]{2,1,0:T(8,128)(2,1)S(1)}, bf16[28,64,128]{2,1,0:T(8,128)(2,1)S(1)}, bf16[28,128,128]{2,1,0:T(8,128)(2,1)S(1)}) custom-call(s32[4]{0:T(128)S(1)} %pad_add_fusion.where_ref, s32[3]{0:T(128)S(1)} %bitcast.45, s32[2,112]{1,0:T(2,128)S(1)} %bitcast.63, f32[28,128,128]{2,1,0:T(8,128)S(1)} %shard_map.136.acc_in, ...), custom_call_target="tpu_custom_call" | custom-call | flops 38 | bytes 38 | tf_op jit(solution)/shard_map/pallas_call | solution.py:30
  61.2 6.1 %shard_map.138 = (bf16[2,128,1024]{2,1,0:T(8,128)(2,1)S(1)}, bf16[2,128,1024]{2,1,0:T(8,128)(2,1)S(1)}) custom-call(s32[4]{0:T(128)S(1)} %pad_add_fusion.where_ref, s32[3]{0:T(128)S(1)} %bitcast.46, s32[2,112]{1,0:T(2,128)S(1)} %bitcast.64, bf16[28,32,128]{2,1,0:T(8,128)(2,1)S(1)} %get-tuple-element.100.refs_0_, ...), custom_call_target="tpu_custom_call" | custom-call | flops 112 | bytes 112 | tf_op jit(solution)/shard_map/pallas_call | solution.py:30
  67.7 2.6 %shard_map.139 = bf16[28,128,128]{2,1,0:T(8,128)(2,1)S(1)} custom-call(s32[4]{0:T(128)S(1)} %pad_add_fusion.where_ref, s32[3]{0:T(128)S(1)} %bitcast.47, s32[2,112]{1,0:T(2,128)S(1)} %bitcast.69, bf16[128,4096]{1,0:T(8,128)(2,1)S(1)} %copy-done, bf16[128,4096]{1,0:T(8,128)(2,1)S(1)} %collective-permute-done.23.refs_1_, ...), custom_call_target="tpu_custom_call" | custom-call | flops 28 | bytes 28 | tf_op jit(solution)/shard_map/pallas_call | solution.py:30
  70.4 8.2 %shard_map.140.refs_8_ = f32[32,128,128]{2,1,0:T(8,128)S(1)} custom-call(s32[4]{0:T(128)S(1)} %pad_add_fusion.where_ref, s32[3]{0:T(128)S(1)} %bitcast.48, s32[2,112]{1,0:T(2,128)S(1)} %bitcast.70, bf16[28,64,128]{2,1,0:T(8,128)(2,1)S(1)} %get-tuple-element.92.refs_2_.refs_0_, bf16[28,64,128]{2,1,0:T(8,128)(2,1)S(1)} %get-tuple-element.93.refs_3_.refs_1_, ...), custom_call_target="tpu_custom_call" | custom-call | flops 112 | bytes 112 | tf_op jit(solution)/shard_map/pallas_call | solution.py:30
  78.6 2.7 %collective-permute-start.27 = (bf16[28,128,128]{2,1,0:T(8,128)(2,1)S(1)}, bf16[28,128,128]{2,1,0:T(8,128)(2,1)S(1)}, u32[]{:S(2)}, u32[]{:S(2)}) collective-permute-start(bf16[28,128,128]{2,1,0:T(8,128)(2,1)S(1)} %shard_map.139), channel_id=1, source_target_pairs={{0,8},{4,12},{8,0},{12,4},{1,9},{5,13},{9,1},{13,5},{2,10},{6,14},... | collective-permute-start | bytes 2752520 | tf_op jit(solution)/shard_map/gate_grad_chip/ppermute | solution.py:104
  81.3 3.0 %shard_map.141 = (bf16[2,128,1024]{2,1,0:T(8,128)(2,1)S(1)}, bf16[2,128,1024]{2,1,0:T(8,128)(2,1)S(1)}, f32[32,128,128]{2,1,0:T(8,128)S(1)}) custom-call(s32[4]{0:T(128)S(1)} %pad_add_fusion.where_ref, s32[3]{0:T(128)S(1)} %bitcast.49, s32[2,112]{1,0:T(2,128)S(1)} %bitcast.57, ...), custom_call_target="tpu_custom_call", output_to_operand_aliasing={{2}: (11, {})} | custom-call | flops 112 | bytes 112 | tf_op jit(solution)/shard_map/pallas_call | solution.py:30
  84.3 4.7 %collective-permute-start.28 = (bf16[2,128,1024]{2,1,0:T(8,128)(2,1)S(1)}, bf16[2,128,1024]{2,1,0:T(8,128)(2,1)S(1)}, u32[]{:S(2)}, u32[]{:S(2)}) collective-permute-start(bf16[2,128,1024]{2,1,0:T(8,128)(2,1)S(1)} %get-tuple-element.97), channel_id=1, source_target_pairs={{0,1},{1,0},{2,3},{3,2},{4,5},{5,4},{6,7},{7,6},{8,9},{9,8},{10,11... | collective-permute-start | bytes 1572872 | tf_op jit(solution)/shard_map/token_group/ppermute | solution.py:114
  89.3 2.4 %collective-permute-start.26 = (bf16[1,128,1024]{2,1,0:T(8,128)(2,1)S(1)}, bf16[1,128,1024]{2,1,0:T(8,128)(2,1)S(1)}, u32[]{:S(2)}, u32[]{:S(2)}) collective-permute-start(bf16[1,128,1024]{2,1,0:T(8,128)(2,1)S(1)} %slice.21), channel_id=1, source_target_pairs={{0,2},{1,3},{2,0},{3,1},{4,6},{5,7},{6,4},{7,5},{8,10},{9,11},{10,... | collective-permute-start | bytes 786440 | tf_op jit(solution)/shard_map/out_group/ppermute | solution.py:114
  91.7 2.6 %shard_map.142 = bf16[28,128,128]{2,1,0:T(8,128)(2,1)S(1)} custom-call(s32[4]{0:T(128)S(1)} %pad_add_fusion.where_ref, s32[3]{0:T(128)S(1)} %bitcast.50, s32[2,112]{1,0:T(2,128)S(1)} %bitcast.65, bf16[28,32,128]{2,1,0:T(8,128)(2,1)S(1)} %get-tuple-element.100.refs_0_, bf16[28,32,128]{2,1,0:T(8,128)(2,1)S(1)} %get-tuple-element.101.refs_1_, ...), custom_call_target="tpu_custom_call" | custom-call | flops 28 | bytes 28 | tf_op jit(solution)/shard_map/pallas_call | solution.py:30
  94.3 1.2 %fusion = bf16[1,28,128,128]{3,2,1,0:T(8,128)(2,1)} fusion(bf16[28,128,128]{2,1,0:T(8,128)(2,1)S(1)} %collective-permute-done.22, bf16[28,128,128]{2,1,0:T(8,128)(2,1)S(1)} %shard_map.142), kind=kLoop, calls=%fused_computation.5 | loop fusion | flops 1835008 | bytes 2752512 | tf_op jit(solution)/shard_map/broadcast_in_dim | solution.py:350
  95.6 0.7 shard_map.145
  96.3 2.5 %collective-permute-start.31 = (bf16[28,128,128]{2,1,0:T(8,128)(2,1)S(1)}, bf16[28,128,128]{2,1,0:T(8,128)(2,1)S(1)}, u32[]{:S(2)}, u32[]{:S(2)}) collective-permute-start(bf16[28,128,128]{2,1,0:T(8,128)(2,1)S(1)} %shard_map.145), channel_id=1, source_target_pairs={{0,8},{4,12},{8,0},{12,4},{1,9},{5,13},{9,1},{13,5},{2,10},{6,14},... | collective-permute-start | bytes 2752520 | tf_op jit(solution)/shard_map/up_grad_chip/ppermute | solution.py:104
  98.9 3.5 %collective-permute-done.27 = bf16[28,128,128]{2,1,0:T(8,128)(2,1)S(1)} collective-permute-done((bf16[28,128,128]{2,1,0:T(8,128)(2,1)S(1)}, bf16[28,128,128]{2,1,0:T(8,128)(2,1)S(1)}, u32[]{:S(2)}, u32[]{:S(2)}) %collective-permute-start.27) | collective-permute-done | bytes 917536 | tf_op jit(solution)/shard_map/gate_grad_chip/ppermute | solution.py:104
  102.4 3.7 %collective-permute-done.28 = bf16[2,128,1024]{2,1,0:T(8,128)(2,1)S(1)} collective-permute-done((bf16[2,128,1024]{2,1,0:T(8,128)(2,1)S(1)}, bf16[2,128,1024]{2,1,0:T(8,128)(2,1)S(1)}, u32[]{:S(2)}, u32[]{:S(2)}) %collective-permute-start.28) | collective-permute-done | bytes 524320 | tf_op jit(solution)/shard_map/token_group/ppermute | solution.py:114
  106.4 2.3 %collective-permute-start.29 = (bf16[1,128,1024]{2,1,0:T(8,128)(2,1)S(1)}, bf16[1,128,1024]{2,1,0:T(8,128)(2,1)S(1)}, u32[]{:S(2)}, u32[]{:S(2)}) collective-permute-start(bf16[1,128,1024]{2,1,0:T(8,128)(2,1)S(1)} %slice.23), channel_id=1, source_target_pairs={{0,2},{1,3},{2,0},{3,1},{4,6},{5,7},{6,4},{7,5},{8,10},{9,11},{10,... | collective-permute-start | bytes 786440 | tf_op jit(solution)/shard_map/token_group/ppermute | solution.py:114
  108.7 2.6 %shard_map.143 = bf16[28,128,128]{2,1,0:T(8,128)(2,1)S(1)} custom-call(s32[4]{0:T(128)S(1)} %pad_add_fusion.where_ref, s32[3]{0:T(128)S(1)} %bitcast.52, s32[2,112]{1,0:T(2,128)S(1)} %bitcast.71, bf16[128,4096]{1,0:T(8,128)(2,1)S(1)} %copy-done, bf16[128,4096]{1,0:T(8,128)(2,1)S(1)} %collective-permute-done.23.refs_1_, ...), custom_call_target="tpu_custom_call" | custom-call | flops 28 | bytes 28 | tf_op jit(solution)/shard_map/pallas_call | solution.py:30
  111.4 1.3 %fusion.1 = bf16[1,28,128,128]{3,2,1,0:T(8,128)(2,1)} fusion(bf16[28,128,128]{2,1,0:T(8,128)(2,1)S(1)} %collective-permute-done.27, bf16[28,128,128]{2,1,0:T(8,128)(2,1)S(1)} %shard_map.143), kind=kLoop, calls=%fused_computation.6 | loop fusion | flops 1835008 | bytes 2752512 | tf_op jit(solution)/shard_map/broadcast_in_dim | solution.py:350
  112.6 2.6 %shard_map.144 = bf16[28,128,128]{2,1,0:T(8,128)(2,1)S(1)} custom-call(s32[4]{0:T(128)S(1)} %pad_add_fusion.where_ref, s32[3]{0:T(128)S(1)} %bitcast.53, s32[2,112]{1,0:T(2,128)S(1)} %bitcast.59, bf16[128,4096]{1,0:T(8,128)(2,1)S(1)} %copy-done, bf16[128,4096]{1,0:T(8,128)(2,1)S(1)} %collective-permute-done.23.refs_1_, ...), custom_call_target="tpu_custom_call" | custom-call | flops 28 | bytes 28 | tf_op jit(solution)/shard_map/pallas_call | solution.py:30
  115.3 0.8 fusion.3
  116.1 4.0 %collective-permute-done.29 = bf16[1,128,1024]{2,1,0:T(8,128)(2,1)S(1)} collective-permute-done((bf16[1,128,1024]{2,1,0:T(8,128)(2,1)S(1)}, bf16[1,128,1024]{2,1,0:T(8,128)(2,1)S(1)}, u32[]{:S(2)}, u32[]{:S(2)}) %collective-permute-start.29) | collective-permute-done | bytes 262176 | tf_op jit(solution)/shard_map/token_group/ppermute | solution.py:114
  120.0 0.8 fusion.4
  120.8 0.9 collective-permute-done.31
  121.8 1.2 %fusion.2 = bf16[1,28,128,128]{3,2,1,0:T(8,128)(2,1)} fusion(bf16[28,128,128]{2,1,0:T(8,128)(2,1)S(1)} %collective-permute-done.31, bf16[28,128,128]{2,1,0:T(8,128)(2,1)S(1)} %shard_map.144), kind=kLoop, calls=%fused_computation.7 | loop fusion | flops 1835008 | bytes 2752512 | tf_op jit(solution)/shard_map/broadcast_in_dim | solution.py:350
  (67 shorter events, 6.7 us)
Async XLA Ops:
  0.6 6.8 %copy-start.6 = (s32[3,1]{0,1:T(1,128)S(1)}, s32[3,1]{0,1:T(1,128)}, u32[]{:S(2)}) copy-start(s32[3,1]{0,1:T(1,128)} %param.17) | copy-start | bytes 40
  0.6 6.8 %copy-start = (bf16[128,4096]{1,0:T(8,128)(2,1)S(1)}, bf16[128,4096]{1,0:T(8,128)(2,1)}, u32[]{:S(2)}) copy-start(bf16[128,4096]{1,0:T(8,128)(2,1)} %refs_0_.5) | copy-start | bytes 3145732
  0.7 6.8 %copy-start.9 = (s32[2,1,112]{2,1,0:T(1,128)S(1)}, s32[2,1,112]{2,1,0:T(1,128)}, u32[]{:S(2)}) copy-start(s32[2,1,112]{2,1,0:T(1,128)} %param.14) | copy-start | bytes 2692
  0.7 16.7 %collective-permute-start.3 = (bf16[128,4096]{1,0:T(8,128)(2,1)}, bf16[128,4096]{1,0:T(8,128)(2,1)S(1)}, u32[]{:S(2)}, u32[]{:S(2)}) collective-permute-start(bf16[128,4096]{1,0:T(8,128)(2,1)} %refs_8_.3), channel_id=1, source_target_pairs={{0,4},{4,0},{8,12},{12,8},{1,5},{5,1},{9,13},{13,9},{2,6},{6,2},{1... | collective-permute-start | bytes 3145736 | tf_op jit(solution)/shard_map/cotangent_core/ppermute | solution.py:100
  1.2 6.2 %collective-permute-start.2 = (bf16[28,128,128]{2,1,0:T(8,128)(2,1)}, bf16[28,128,128]{2,1,0:T(8,128)(2,1)}, u32[]{:S(2)}, u32[]{:S(2)}) collective-permute-start(bf16[28,128,128]{2,1,0:T(8,128)(2,1)} %bitcast.27), channel_id=1, source_target_pairs={{0,4},{4,0},{8,12},{12,8},{1,5},{5,1},{9,13},{13,9},{2,6},{6,2},{1... | collective-permute-start | bytes 2752520 | tf_op jit(solution)/shard_map/gate_core/ppermute | solution.py:100
  1.3 19.4 %collective-permute-start = (bf16[28,128,128]{2,1,0:T(8,128)(2,1)}, bf16[28,128,128]{2,1,0:T(8,128)(2,1)S(1)}, u32[]{:S(2)}, u32[]{:S(2)}) collective-permute-start(bf16[28,128,128]{2,1,0:T(8,128)(2,1)} %bitcast.30), channel_id=1, source_target_pairs={{0,4},{4,0},{8,12},{12,8},{1,5},{5,1},{9,13},{13,9},{2,6},{6,2},{1... | collective-permute-start | bytes 2752520 | tf_op jit(solution)/shard_map/up_core/ppermute | solution.py:100
  3.5 13.9 %collective-permute-start.1 = (bf16[14,128,128]{2,1,0:T(8,128)(2,1)}, bf16[14,128,128]{2,1,0:T(8,128)(2,1)S(1)}, u32[]{:S(2)}, u32[]{:S(2)}) collective-permute-start(bf16[14,128,128]{2,1,0:T(8,128)(2,1)} %dynamic-slice_bitcast_fusion.1), channel_id=1, source_target_pairs={{0,8},{4,12},{8,0},{12,4},{1,9},{5,13},{9,1},{13,5},{2,10},{6,14},... | collective-permute-start | bytes 1376264 | tf_op jit(solution)/shard_map/gate_chip/ppermute | solution.py:104
  6.1 17.3 %collective-permute-start.6 = (bf16[28,128,128]{2,1,0:T(8,128)(2,1)}, bf16[28,128,128]{2,1,0:T(8,128)(2,1)}, u32[]{:S(2)}, u32[]{:S(2)}) collective-permute-start(bf16[28,128,128]{2,1,0:T(8,128)(2,1)} %bitcast.33), channel_id=1, source_target_pairs={{0,4},{4,0},{8,12},{12,8},{1,5},{5,1},{9,13},{13,9},{2,6},{6,2},{1... | collective-permute-start | bytes 2752520 | tf_op jit(solution)/shard_map/down_core/ppermute | solution.py:100
  7.4 1.2 copy-start.2
  8.6 12.1 %copy-start.4 = (bf16[1,28,128,128]{3,2,1,0:T(8,128)(2,1)S(1)}, bf16[1,28,128,128]{3,2,1,0:T(8,128)(2,1)}, u32[]{:S(2)}) copy-start(bf16[1,28,128,128]{3,2,1,0:T(8,128)(2,1)} %param.12) | copy-start | bytes 2752516
  8.6 12.1 %copy-start.7 = (s32[2,1,112]{2,1,0:T(1,128)S(1)}, s32[2,1,112]{2,1,0:T(1,128)}, u32[]{:S(2)}) copy-start(s32[2,1,112]{2,1,0:T(1,128)} %param.15) | copy-start | bytes 2692
  17.4 12.3 %collective-permute-start.4 = (bf16[14,128,128]{2,1,0:T(8,128)(2,1)S(1)}, bf16[14,128,128]{2,1,0:T(8,128)(2,1)S(1)}, u32[]{:S(2)}, u32[]{:S(2)}) collective-permute-start(bf16[14,128,128]{2,1,0:T(8,128)(2,1)S(1)} %dynamic-slice_bitcast_fusion.2), channel_id=1, source_target_pairs={{0,8},{4,12},{8,0},{12,4},{1,9},{5,13},{9,1},{13,5},{2,10},{6,14},... | collective-permute-start | bytes 1376264 | tf_op jit(solution)/shard_map/up_chip/ppermute | solution.py:104
  19.2 11.8 %collective-permute-start.5 = (bf16[14,128,128]{2,1,0:T(8,128)(2,1)S(1)}, bf16[14,128,128]{2,1,0:T(8,128)(2,1)S(1)}, u32[]{:S(2)}, u32[]{:S(2)}) collective-permute-start(bf16[14,128,128]{2,1,0:T(8,128)(2,1)S(1)} %collective-permute-done.1.refs_0_.refs_4_), channel_id=1, source_target_pairs={{0,16},{16,0},{1,17},{17,1},{2,18},{18,2},{3,19},{19,3},{4,20},{20... | collective-permute-start | bytes 1376264 | tf_op jit(solution)/shard_map/gate_part/ppermute | solution.py:110
  20.7 2.6 %copy-start.5 = (bf16[1,28,128,128]{3,2,1,0:T(8,128)(2,1)S(1)}, bf16[1,28,128,128]{3,2,1,0:T(8,128)(2,1)}, u32[]{:S(2)}) copy-start(bf16[1,28,128,128]{3,2,1,0:T(8,128)(2,1)} %param.13) | copy-start | bytes 2752516
  20.7 2.7 %copy-start.1 = (bf16[128,4096]{1,0:T(8,128)(2,1)S(1)}, bf16[128,4096]{1,0:T(8,128)(2,1)}, u32[]{:S(2)}) copy-start(bf16[128,4096]{1,0:T(8,128)(2,1)} %refs_8_.3) | copy-start | bytes 3145732
  20.7 2.7 %copy-start.8 = (s32[2,1,112]{2,1,0:T(1,128)S(1)}, s32[2,1,112]{2,1,0:T(1,128)}, u32[]{:S(2)}) copy-start(s32[2,1,112]{2,1,0:T(1,128)} %param.16) | copy-start | bytes 2692
  23.3 9.7 %collective-permute-start.7 = (bf16[14,128,128]{2,1,0:T(8,128)(2,1)S(1)}, bf16[14,128,128]{2,1,0:T(8,128)(2,1)S(1)}, u32[]{:S(2)}, u32[]{:S(2)}) collective-permute-start(bf16[14,128,128]{2,1,0:T(8,128)(2,1)S(1)} %collective-permute-done.1.refs_0_.refs_4_), channel_id=1, source_target_pairs={{0,4},{4,0},{8,12},{12,8},{1,5},{5,1},{9,13},{13,9},{2,6},{6,2},{1... | collective-permute-start | bytes 1376264 | tf_op jit(solution)/shard_map/gate_x_core/ppermute | solution.py:100
  31.0 10.9 %collective-permute-start.10 = (bf16[14,128,128]{2,1,0:T(8,128)(2,1)S(1)}, bf16[14,128,128]{2,1,0:T(8,128)(2,1)S(1)}, u32[]{:S(2)}, u32[]{:S(2)}) collective-permute-start(bf16[14,128,128]{2,1,0:T(8,128)(2,1)S(1)} %dynamic-slice_bitcast_fusion), channel_id=1, source_target_pairs={{0,8},{4,12},{8,0},{12,4},{1,9},{5,13},{9,1},{13,5},{2,10},{6,14},... | collective-permute-start | bytes 1376264 | tf_op jit(solution)/shard_map/down_chip/ppermute | solution.py:104
  31.4 10.8 %collective-permute-start.12 = (bf16[14,128,128]{2,1,0:T(8,128)(2,1)S(1)}, bf16[14,128,128]{2,1,0:T(8,128)(2,1)S(1)}, u32[]{:S(2)}, u32[]{:S(2)}) collective-permute-start(bf16[14,128,128]{2,1,0:T(8,128)(2,1)S(1)} %collective-permute-done.4.refs_2_.refs_0_.refs_3_), channel_id=1, source_target_pairs={{0,16},{16,0},{1,17},{17,1},{2,18},{18,2},{3,19},{19,3},{4,20},{20... | collective-permute-start | bytes 1376264 | tf_op jit(solution)/shard_map/up_part/ppermute | solution.py:110
  35.3 1.5 %collective-permute-start.8 = (bf16[7,128,128]{2,1,0:T(8,128)(2,1)S(1)}, bf16[7,128,128]{2,1,0:T(8,128)(2,1)S(1)}, u32[]{:S(2)}, u32[]{:S(2)}) collective-permute-start(bf16[7,128,128]{2,1,0:T(8,128)(2,1)S(1)} %get-tuple-element.62), channel_id=1, source_target_pairs={{0,4},{4,0},{8,12},{12,8},{1,5},{5,1},{9,13},{13,9},{2,6},{6,2},{1... | collective-permute-start | bytes 688136 | tf_op jit(solution)/shard_map/up_x_core/ppermute | solution.py:100
  35.3 1.8 %collective-permute-start.9 = (bf16[7,128,128]{2,1,0:T(8,128)(2,1)S(1)}, bf16[7,128,128]{2,1,0:T(8,128)(2,1)S(1)}, u32[]{:S(2)}, u32[]{:S(2)}) collective-permute-start(bf16[7,128,128]{2,1,0:T(8,128)(2,1)S(1)} %get-tuple-element.63), channel_id=1, source_target_pairs={{0,4},{4,0},{8,12},{12,8},{1,5},{5,1},{9,13},{13,9},{2,6},{6,2},{1... | collective-permute-start | bytes 688136 | tf_op jit(solution)/shard_map/up_x_core/ppermute | solution.py:100
  41.9 2.0 %collective-permute-start.11 = (bf16[14,128,128]{2,1,0:T(8,128)(2,1)S(1)}, bf16[14,128,128]{2,1,0:T(8,128)(2,1)S(1)}, u32[]{:S(2)}, u32[]{:S(2)}) collective-permute-start(bf16[14,128,128]{2,1,0:T(8,128)(2,1)S(1)} %collective-permute-done.5.refs_0_.refs_6_), channel_id=1, source_target_pairs={{0,4},{4,0},{8,12},{12,8},{1,5},{5,1},{9,13},{13,9},{2,6},{6,2},{1... | collective-permute-start | bytes 1376264 | tf_op jit(solution)/shard_map/gate_y_core/ppermute | solution.py:100
  42.2 4.7 %collective-permute-start.13 = (bf16[14,128,128]{2,1,0:T(8,128)(2,1)S(1)}, bf16[14,128,128]{2,1,0:T(8,128)(2,1)S(1)}, u32[]{:S(2)}, u32[]{:S(2)}) collective-permute-start(bf16[14,128,128]{2,1,0:T(8,128)(2,1)S(1)} %collective-permute-done.12.refs_0_.refs_6_), channel_id=1, source_target_pairs={{0,4},{4,0},{8,12},{12,8},{1,5},{5,1},{9,13},{13,9},{2,6},{6,2},{1... | collective-permute-start | bytes 1376264 | tf_op jit(solution)/shard_map/up_y_core/ppermute | solution.py:100
  42.4 12.8 %collective-permute-start.19 = (bf16[14,128,128]{2,1,0:T(8,128)(2,1)S(1)}, bf16[14,128,128]{2,1,0:T(8,128)(2,1)S(1)}, u32[]{:S(2)}, u32[]{:S(2)}) collective-permute-start(bf16[14,128,128]{2,1,0:T(8,128)(2,1)S(1)} %collective-permute-done.10.refs_0_.refs_6_), channel_id=1, source_target_pairs={{0,16},{16,0},{1,17},{17,1},{2,18},{18,2},{3,19},{19,3},{4,20},{20... | collective-permute-start | bytes 1376264 | tf_op jit(solution)/shard_map/down_part/ppermute | solution.py:110
  47.8 1.6 %collective-permute-start.14 = (bf16[28,32,128]{2,1,0:T(8,128)(2,1)S(1)}, bf16[28,32,128]{2,1,0:T(8,128)(2,1)S(1)}, u32[]{:S(2)}, u32[]{:S(2)}) collective-permute-start(bf16[28,32,128]{2,1,0:T(8,128)(2,1)S(1)} %get-tuple-element.100.refs_0_), channel_id=1, source_target_pairs={{0,4},{4,0},{8,12},{12,8},{1,5},{5,1},{9,13},{13,9},{2,6},{6,2},{1... | collective-permute-start | bytes 688136 | tf_op jit(solution)/shard_map/hidden_core/ppermute | solution.py:100
  47.9 1.8 %collective-permute-start.15 = (bf16[28,32,128]{2,1,0:T(8,128)(2,1)S(1)}, bf16[28,32,128]{2,1,0:T(8,128)(2,1)S(1)}, u32[]{:S(2)}, u32[]{:S(2)}) collective-permute-start(bf16[28,32,128]{2,1,0:T(8,128)(2,1)S(1)} %get-tuple-element.101.refs_1_), channel_id=1, source_target_pairs={{0,4},{4,0},{8,12},{12,8},{1,5},{5,1},{9,13},{13,9},{2,6},{6,2},{1... | collective-permute-start | bytes 688136 | tf_op jit(solution)/shard_map/hidden_core/ppermute | solution.py:100
  48.4 1.6 %collective-permute-start.16 = (bf16[28,32,128]{2,1,0:T(8,128)(2,1)S(1)}, bf16[28,32,128]{2,1,0:T(8,128)(2,1)S(1)}, u32[]{:S(2)}, u32[]{:S(2)}) collective-permute-start(bf16[28,32,128]{2,1,0:T(8,128)(2,1)S(1)} %get-tuple-element.102.refs_2_), channel_id=1, source_target_pairs={{0,4},{4,0},{8,12},{12,8},{1,5},{5,1},{9,13},{13,9},{2,6},{6,2},{1... | collective-permute-start | bytes 688136 | tf_op jit(solution)/shard_map/hidden_core/ppermute | solution.py:100
  48.5 1.9 %collective-permute-start.17 = (bf16[28,32,128]{2,1,0:T(8,128)(2,1)S(1)}, bf16[28,32,128]{2,1,0:T(8,128)(2,1)S(1)}, u32[]{:S(2)}, u32[]{:S(2)}) collective-permute-start(bf16[28,32,128]{2,1,0:T(8,128)(2,1)S(1)} %get-tuple-element.103.refs_3_), channel_id=1, source_target_pairs={{0,4},{4,0},{8,12},{12,8},{1,5},{5,1},{9,13},{13,9},{2,6},{6,2},{1... | collective-permute-start | bytes 688136 | tf_op jit(solution)/shard_map/hidden_core/ppermute | solution.py:100
  49.4 18.3 %collective-permute-start.23 = (bf16[128,4096]{1,0:T(8,128)(2,1)S(1)}, bf16[128,4096]{1,0:T(8,128)(2,1)S(1)}, u32[]{:S(2)}, u32[]{:S(2)}) collective-permute-start(bf16[128,4096]{1,0:T(8,128)(2,1)S(1)} %copy-done), channel_id=1, source_target_pairs={{0,4},{4,0},{8,12},{12,8},{1,5},{5,1},{9,13},{13,9},{2,6},{6,2},{1... | collective-permute-start | bytes 3145736 | tf_op jit(solution)/shard_map/tokens_core/ppermute | solution.py:100
  49.7 6.8 %collective-permute-start.18 = (bf16[14,128,128]{2,1,0:T(8,128)(2,1)S(1)}, bf16[14,128,128]{2,1,0:T(8,128)(2,1)S(1)}, u32[]{:S(2)}, u32[]{:S(2)}) collective-permute-start(bf16[14,128,128]{2,1,0:T(8,128)(2,1)S(1)} %collective-permute-done.10.refs_0_.refs_6_), channel_id=1, source_target_pairs={{0,4},{4,0},{8,12},{12,8},{1,5},{5,1},{9,13},{13,9},{2,6},{6,2},{1... | collective-permute-start | bytes 1376264 | tf_op jit(solution)/shard_map/down_x_core/ppermute | solution.py:100
  55.2 3.2 %collective-permute-start.20 = (bf16[14,128,128]{2,1,0:T(8,128)(2,1)S(1)}, bf16[14,128,128]{2,1,0:T(8,128)(2,1)S(1)}, u32[]{:S(2)}, u32[]{:S(2)}) collective-permute-start(bf16[14,128,128]{2,1,0:T(8,128)(2,1)S(1)} %collective-permute-done.19.refs_0_.refs_8_), channel_id=1, source_target_pairs={{0,4},{4,0},{8,12},{12,8},{1,5},{5,1},{9,13},{13,9},{2,6},{6,2},{1... | collective-permute-start | bytes 1376264 | tf_op jit(solution)/shard_map/down_y_core/ppermute | solution.py:100
  55.2 23.5 %collective-permute-start.22 = (bf16[28,128,128]{2,1,0:T(8,128)(2,1)S(1)}, bf16[28,128,128]{2,1,0:T(8,128)(2,1)S(1)}, u32[]{:S(2)}, u32[]{:S(2)}) collective-permute-start(bf16[28,128,128]{2,1,0:T(8,128)(2,1)S(1)} %shard_map.135), channel_id=1, source_target_pairs={{0,8},{4,12},{8,0},{12,4},{1,9},{5,13},{9,1},{13,5},{2,10},{6,14},... | collective-permute-start | bytes 2752520 | tf_op jit(solution)/shard_map/down_grad_chip/ppermute | solution.py:104
  60.6 6.7 %collective-permute-start.24 = (bf16[28,64,128]{2,1,0:T(8,128)(2,1)S(1)}, bf16[28,64,128]{2,1,0:T(8,128)(2,1)S(1)}, u32[]{:S(2)}, u32[]{:S(2)}) collective-permute-start(bf16[28,64,128]{2,1,0:T(8,128)(2,1)S(1)} %get-tuple-element.92.refs_2_.refs_0_), channel_id=1, source_target_pairs={{0,4},{4,0},{8,12},{12,8},{1,5},{5,1},{9,13},{13,9},{2,6},{6,2},{1... | collective-permute-start | bytes 1376264 | tf_op jit(solution)/shard_map/grads_core/ppermute | solution.py:100
  61.0 6.8 %collective-permute-start.25 = (bf16[28,64,128]{2,1,0:T(8,128)(2,1)S(1)}, bf16[28,64,128]{2,1,0:T(8,128)(2,1)S(1)}, u32[]{:S(2)}, u32[]{:S(2)}) collective-permute-start(bf16[28,64,128]{2,1,0:T(8,128)(2,1)S(1)} %get-tuple-element.93.refs_3_.refs_1_), channel_id=1, source_target_pairs={{0,4},{4,0},{8,12},{12,8},{1,5},{5,1},{9,13},{13,9},{2,6},{6,2},{1... | collective-permute-start | bytes 1376264 | tf_op jit(solution)/shard_map/grads_core/ppermute | solution.py:100
  67.3 21.8 %collective-permute-start.21 = (bf16[2,128,1024]{2,1,0:T(8,128)(2,1)S(1)}, bf16[2,128,1024]{2,1,0:T(8,128)(2,1)S(1)}, u32[]{:S(2)}, u32[]{:S(2)}) collective-permute-start(bf16[2,128,1024]{2,1,0:T(8,128)(2,1)S(1)} %get-tuple-element.88), channel_id=1, source_target_pairs={{0,1},{1,0},{2,3},{3,2},{4,5},{5,4},{6,7},{7,6},{8,9},{9,8},{10,11... | collective-permute-start | bytes 1572872 | tf_op jit(solution)/shard_map/out_group/ppermute | solution.py:114
  67.4 28.2 %collective-permute-start.30 = (bf16[28,128,128]{2,1,0:T(8,128)(2,1)S(1)}, bf16[28,128,128]{2,1,0:T(8,128)(2,1)S(1)}, u32[]{:S(2)}, u32[]{:S(2)}) collective-permute-start(bf16[28,128,128]{2,1,0:T(8,128)(2,1)S(1)} %get-tuple-element.95.refs_0_.refs_2_), channel_id=1, source_target_pairs={{0,4},{4,0},{8,12},{12,8},{1,5},{5,1},{9,13},{13,9},{2,6},{6,2},{1... | collective-permute-start | bytes 2752520 | tf_op jit(solution)/shard_map/grads_core/ppermute | solution.py:100
  67.7 2.7 %copy-start.3 = (bf16[1,28,128,128]{3,2,1,0:T(8,128)(2,1)S(1)}, bf16[1,28,128,128]{3,2,1,0:T(8,128)(2,1)}, u32[]{:S(2)}) copy-start(bf16[1,28,128,128]{3,2,1,0:T(8,128)(2,1)} %param.11) | copy-start | bytes 2752516
  78.6 23.8 %collective-permute-start.27 = (bf16[28,128,128]{2,1,0:T(8,128)(2,1)S(1)}, bf16[28,128,128]{2,1,0:T(8,128)(2,1)S(1)}, u32[]{:S(2)}, u32[]{:S(2)}) collective-permute-start(bf16[28,128,128]{2,1,0:T(8,128)(2,1)S(1)} %shard_map.139), channel_id=1, source_target_pairs={{0,8},{4,12},{8,0},{12,4},{1,9},{5,13},{9,1},{13,5},{2,10},{6,14},... | collective-permute-start | bytes 2752520 | tf_op jit(solution)/shard_map/gate_grad_chip/ppermute | solution.py:104
  84.3 21.9 %collective-permute-start.28 = (bf16[2,128,1024]{2,1,0:T(8,128)(2,1)S(1)}, bf16[2,128,1024]{2,1,0:T(8,128)(2,1)S(1)}, u32[]{:S(2)}, u32[]{:S(2)}) collective-permute-start(bf16[2,128,1024]{2,1,0:T(8,128)(2,1)S(1)} %get-tuple-element.97), channel_id=1, source_target_pairs={{0,1},{1,0},{2,3},{3,2},{4,5},{5,4},{6,7},{7,6},{8,9},{9,8},{10,11... | collective-permute-start | bytes 1572872 | tf_op jit(solution)/shard_map/token_group/ppermute | solution.py:114
  89.3 26.0 %collective-permute-start.26 = (bf16[1,128,1024]{2,1,0:T(8,128)(2,1)S(1)}, bf16[1,128,1024]{2,1,0:T(8,128)(2,1)S(1)}, u32[]{:S(2)}, u32[]{:S(2)}) collective-permute-start(bf16[1,128,1024]{2,1,0:T(8,128)(2,1)S(1)} %slice.21), channel_id=1, source_target_pairs={{0,2},{1,3},{2,0},{3,1},{4,6},{5,7},{6,4},{7,5},{8,10},{9,11},{10,... | collective-permute-start | bytes 786440 | tf_op jit(solution)/shard_map/out_group/ppermute | solution.py:114
  96.3 25.4 %collective-permute-start.31 = (bf16[28,128,128]{2,1,0:T(8,128)(2,1)S(1)}, bf16[28,128,128]{2,1,0:T(8,128)(2,1)S(1)}, u32[]{:S(2)}, u32[]{:S(2)}) collective-permute-start(bf16[28,128,128]{2,1,0:T(8,128)(2,1)S(1)} %shard_map.145), channel_id=1, source_target_pairs={{0,8},{4,12},{8,0},{12,4},{1,9},{5,13},{9,1},{13,5},{2,10},{6,14},... | collective-permute-start | bytes 2752520 | tf_op jit(solution)/shard_map/up_grad_chip/ppermute | solution.py:104
  106.4 13.7 %collective-permute-start.29 = (bf16[1,128,1024]{2,1,0:T(8,128)(2,1)S(1)}, bf16[1,128,1024]{2,1,0:T(8,128)(2,1)S(1)}, u32[]{:S(2)}, u32[]{:S(2)}) collective-permute-start(bf16[1,128,1024]{2,1,0:T(8,128)(2,1)S(1)} %slice.23), channel_id=1, source_target_pairs={{0,2},{1,3},{2,0},{3,1},{4,6},{5,7},{6,4},{7,5},{8,10},{9,11},{10,... | collective-permute-start | bytes 786440 | tf_op jit(solution)/shard_map/token_group/ppermute | solution.py:114

commit v4 on v3

--- a/solution.py
+++ b/solution.py
@@ -10,7 +10,7 @@
 FF = 14336
 F32 = jnp.float32
 BF16 = jnp.bfloat16
-UNROLL = 4
+UNROLL = 7
 NN = (((1,), (0,)), ((), ()))
 NT = (((1,), (1,)), ((), ()))
 TN = (((0,), (0,)), ((), ()))
@@ -64,13 +64,20 @@
             store(slot, value)
         return 0
 
-    def single(slot, _):
-        store(slot, terms(slot))
-        return 0
-
     rounds = lax.div(live, UNROLL)
     lax.fori_loop(0, rounds, several, 0)
-    lax.fori_loop(rounds * UNROLL, live, single, 0)
+    done = rounds * UNROLL
+
+    @pl.when(done < live)
+    def _():
+        slots = [jnp.minimum(done + u, live - 1) for u in range(UNROLL - 1)]
+        values = [terms(slot) for slot in slots]
+        store(slots[0], values[0])
+        for u in range(1, UNROLL - 1):
+
+            @pl.when(done + u < live)
+            def _(u=u):
+                store(slots[u], values[u])
 
 
 def live_in(count, first, extent):
@@ -486,7 +493,7 @@
 
         gate_sent = after(gate_away, *down_far)
         gate_far = [chip_shift(g, k, "gate_grad") for g, k in zip(gate_sent, away)]
-        out_first, *out_terms = swap_groups("out", out_parts, *token_parts)
+        out_first, *out_terms = swap_groups("out", after(out_parts, *gate_away), *token_parts)
         up_sent = after(up_away, out_first)
         up_far = [chip_shift(g, k, "up_grad") for g, k in zip(up_sent, away)]
         late_h, late_t = after(hidden, out_first), after(tokens, *gate_far)

time: 125 us -> 121 us (0.968); the launches traced: 123 us -> 121 us
  waiting for transfers between devices: 29.4 us -> 48.7 us
  Pallas kernels: 52.9 us -> 40.2 us
  starting transfers between devices: 29.8 us -> 21 us
    ppermute x6, waiting for transfers between devices: 15.3 us -> 31.2 us  [chip_shift(): lax.ppermute(a, 'dp', [(i, (i // 2 + k) % chips * 2 + i % 2) for i in ran...]
    pallas_call x18, Pallas kernels: 52.9 us -> 40.2 us  [call(): pl.pallas_call(body, out_shape=outs, in_specs=[SMEM] * len(ints) + [VMEM]...]
    ppermute x4, starting transfers between devices: 9.57 us -> 4.06 us  [group_swap(): return lax.ppermute(a, 'tensor', [(i, i ^ bit) for i in range(groups)])]
    ppermute x6, starting transfers between devices: 11.4 us -> 8.11 us  [chip_shift(): lax.ppermute(a, 'dp', [(i, (i // 2 + k) % chips * 2 + i % 2) for i in ran...]
    ppermute x3, waiting for transfers between devices: 3.84 us -> 5.69 us  [part_swap(): return lax.ppermute(a, 'parts', [(0, 1), (1, 0)])]
    ppermute x4, waiting for transfers between devices: 7.73 us -> 9.34 us  [group_swap(): return lax.ppermute(a, 'tensor', [(i, i ^ bit) for i in range(groups)])]
  transfers between devices with their start and end apart: 32 -> 32, of which waited for: 16 -> 17; matrix products, arithmetic and copies ran while one was open for 6% -> 6% of each run, Pallas kernels for 43% -> 33%
where the time goes in v4:
time: 121 us
  waiting for transfers between devices  48.7 us (40%)
  Pallas kernels  40.2 us (33%)
  starting transfers between devices  21 us (17%)
  other arithmetic  5.75 us (5%)
  local copies, waits for them, and re-layouts  4.17 us (3%)
    pallas_call x18, Pallas kernels, call(): pl.pallas_call(body, out_shape=outs, in_specs=[SMEM] * len(ints) + [VMEM]...  40.2 us
    ppermute x6, waiting for transfers between devices, chip_shift(): lax.ppermute(a, 'dp', [(i, (i // 2 + k) % chips * 2 + i % 2) for i in ran...  31.2 us
    ppermute x4, waiting for transfers between devices, group_swap(): return lax.ppermute(a, 'tensor', [(i, i ^ bit) for i in range(groups)])  9.34 us
    ppermute x6, starting transfers between devices, chip_shift(): lax.ppermute(a, 'dp', [(i, (i // 2 + k) % chips * 2 + i % 2) for i in ran...  8.11 us
    ppermute x3, waiting for transfers between devices, part_swap(): return lax.ppermute(a, 'parts', [(0, 1), (1, 0)])  5.69 us
    ppermute x3, starting transfers between devices, part_swap(): return lax.ppermute(a, 'parts', [(0, 1), (1, 0)])  4.63 us
    ppermute x19, starting transfers between devices, pair_swap(): return lax.ppermute(a, 'dp', [(i, i ^ 1) for i in range(dp)])  4.18 us
    ppermute x4, starting transfers between devices, group_swap(): return lax.ppermute(a, 'tensor', [(i, i ^ bit) for i in range(groups)])  4.06 us
  transfers between devices with their start and end apart: 32, of which 17 were waited for; matrix products, arithmetic and copies ran while one was open for 6% of the time, Pallas kernels for 33%

profile of v4, /device:TPU:0, one launch (start us, length us, event | category | flops | bytes accessed | tf_op | source)
XLA Modules:
  0.0 120.8 jit_solution(10707114841505944371)
XLA Ops:
  0.7 0.5 collective-permute-start.3
  1.7 1.8 %dynamic-slice_bitcast_fusion.1 = bf16[14,128,128]{2,1,0:T(8,128)(2,1)} fusion(bf16[1,28,128,128]{3,2,1,0:T(8,128)(2,1)} %param.11, s32[]{:T(128)S(6)} %select_n.18), kind=kLoop, calls=%fused_computation.11 | loop fusion | bytes 917508 | tf_op jit(solution)/shard_map/dynamic_slice | solution.py:153
  3.5 2.6 %collective-permute-start.1 = (bf16[14,128,128]{2,1,0:T(8,128)(2,1)}, bf16[14,128,128]{2,1,0:T(8,128)(2,1)S(1)}, u32[]{:S(2)}, u32[]{:S(2)}) collective-permute-start(bf16[14,128,128]{2,1,0:T(8,128)(2,1)} %dynamic-slice_bitcast_fusion.1), channel_id=1, source_target_pairs={{0,8},{4,12},{8,0},{12,4},{1,9},{5,13},{9,1},{13,5},{2,10},{6,14},... | collective-permute-start | bytes 1376264 | tf_op jit(solution)/shard_map/gate_chip/ppermute | solution.py:111
  6.3 1.1 dynamic-slice_bitcast_fusion.2
  7.4 1.2 copy-done.2
  8.6 3.0 %shard_map.129.acc_in = f32[28,128,128]{2,1,0:T(8,128)S(1)} custom-call(s32[4]{0:T(128)S(1)} %pad_add_fusion.where_ref, s32[3]{0:T(128)S(1)} %bitcast.36, s32[2,112]{1,0:T(2,128)S(1)} %bitcast.66, bf16[128,4096]{1,0:T(8,128)(2,1)S(1)} %copy-done, bf16[28,128,128]{2,1,0:T(8,128)(2,1)S(1)} %bitcast.28, bf16[28,128,128]{2,1,0:T(8,128)(2,1)} %collective-permute-done.2.refs_1_.refs_3_), custom_call_target="tpu_custom_call" | custom-call | flops 56 | bytes 56 | tf_op jit(solution)/shard_map/pallas_call | solution.py:30
  11.6 5.8 %collective-permute-done.1.refs_0_.refs_4_ = bf16[14,128,128]{2,1,0:T(8,128)(2,1)S(1)} collective-permute-done((bf16[14,128,128]{2,1,0:T(8,128)(2,1)}, bf16[14,128,128]{2,1,0:T(8,128)(2,1)S(1)}, u32[]{:S(2)}, u32[]{:S(2)}) %collective-permute-start.1) | collective-permute-done | bytes 458784 | tf_op jit(solution)/shard_map/gate_chip/ppermute | solution.py:111
  17.4 1.8 %collective-permute-start.4 = (bf16[14,128,128]{2,1,0:T(8,128)(2,1)S(1)}, bf16[14,128,128]{2,1,0:T(8,128)(2,1)S(1)}, u32[]{:S(2)}, u32[]{:S(2)}) collective-permute-start(bf16[14,128,128]{2,1,0:T(8,128)(2,1)S(1)} %dynamic-slice_bitcast_fusion.2), channel_id=1, source_target_pairs={{0,8},{4,12},{8,0},{12,4},{1,9},{5,13},{9,1},{13,5},{2,10},{6,14},... | collective-permute-start | bytes 1376264 | tf_op jit(solution)/shard_map/up_chip/ppermute | solution.py:111
  19.2 1.5 %collective-permute-start.5 = (bf16[14,128,128]{2,1,0:T(8,128)(2,1)S(1)}, bf16[14,128,128]{2,1,0:T(8,128)(2,1)S(1)}, u32[]{:S(2)}, u32[]{:S(2)}) collective-permute-start(bf16[14,128,128]{2,1,0:T(8,128)(2,1)S(1)} %collective-permute-done.1.refs_0_.refs_4_), channel_id=1, source_target_pairs={{0,16},{16,0},{1,17},{17,1},{2,18},{18,2},{3,19},{19,3},{4,20},{20... | collective-permute-start | bytes 1376264 | tf_op jit(solution)/shard_map/gate_part/ppermute | solution.py:117
  20.7 2.5 %shard_map.128.acc_in = f32[28,128,128]{2,1,0:T(8,128)S(1)} custom-call(s32[4]{0:T(128)S(1)} %pad_add_fusion.where_ref, s32[3]{0:T(128)S(1)} %bitcast.37, s32[2,112]{1,0:T(2,128)S(1)} %bitcast.54, bf16[128,4096]{1,0:T(8,128)(2,1)S(1)} %copy-done, bf16[28,128,128]{2,1,0:T(8,128)(2,1)S(1)} %bitcast.31, ...), custom_call_target="tpu_custom_call" | custom-call | flops 56 | bytes 56 | tf_op jit(solution)/shard_map/pallas_call | solution.py:30
  23.4 3.6 %shard_map.130.acc_in = f32[28,128,128]{2,1,0:T(8,128)S(1)} custom-call(s32[4]{0:T(128)S(1)} %pad_add_fusion.where_ref, s32[3]{0:T(128)S(1)} %bitcast.38, s32[2,112]{1,0:T(2,128)S(1)} %bitcast.60, bf16[128,4096]{1,0:T(8,128)(2,1)S(1)} %copy-done.1, bf16[28,128,128]{2,1,0:T(8,128)(2,1)S(1)} %bitcast.34, ...), custom_call_target="tpu_custom_call" | custom-call | flops 56 | bytes 56 | tf_op jit(solution)/shard_map/pallas_call | solution.py:30
  27.0 2.6 %collective-permute-done.4.refs_2_.refs_0_.refs_3_ = bf16[14,128,128]{2,1,0:T(8,128)(2,1)S(1)} collective-permute-done((bf16[14,128,128]{2,1,0:T(8,128)(2,1)S(1)}, bf16[14,128,128]{2,1,0:T(8,128)(2,1)S(1)}, u32[]{:S(2)}, u32[]{:S(2)}) %collective-permute-start.4) | collective-permute-done | bytes 458784 | tf_op jit(solution)/shard_map/up_chip/ppermute | solution.py:111
  29.7 1.3 %collective-permute-done.5.refs_0_.refs_6_ = bf16[14,128,128]{2,1,0:T(8,128)(2,1)S(1)} collective-permute-done((bf16[14,128,128]{2,1,0:T(8,128)(2,1)S(1)}, bf16[14,128,128]{2,1,0:T(8,128)(2,1)S(1)}, u32[]{:S(2)}, u32[]{:S(2)}) %collective-permute-start.5) | collective-permute-done | bytes 458784 | tf_op jit(solution)/shard_map/gate_part/ppermute | solution.py:117
  31.4 1.6 %collective-permute-start.12 = (bf16[14,128,128]{2,1,0:T(8,128)(2,1)S(1)}, bf16[14,128,128]{2,1,0:T(8,128)(2,1)S(1)}, u32[]{:S(2)}, u32[]{:S(2)}) collective-permute-start(bf16[14,128,128]{2,1,0:T(8,128)(2,1)S(1)} %collective-permute-done.4.refs_2_.refs_0_.refs_3_), channel_id=1, source_target_pairs={{0,16},{16,0},{1,17},{17,1},{2,18},{18,2},{3,19},{19,3},{4,20},{20... | collective-permute-start | bytes 1376264 | tf_op jit(solution)/shard_map/up_part/ppermute | solution.py:117
  33.0 0.6 shard_map.131
  34.2 1.0 collective-permute-done.8.refs_1_.refs_4_
  35.5 1.5 %shard_map.132.acc_in = f32[28,128,128]{2,1,0:T(8,128)S(1)} custom-call(s32[4]{0:T(128)S(1)} %pad_add_fusion.where_ref, s32[3]{0:T(128)S(1)} %bitcast.40, s32[2,112]{1,0:T(2,128)S(1)} %bitcast.55, f32[28,128,128]{2,1,0:T(8,128)S(1)} %shard_map.128.acc_in, bf16[128,4096]{1,0:T(8,128)(2,1)S(1)} %copy-done, ...), custom_call_target="tpu_custom_call", output_to_operand_aliasing={{}: (3, {})} | custom-call | flops 28 | bytes 28 | tf_op jit(solution)/shard_map/pallas_call | solution.py:30
  37.1 4.8 %collective-permute-done.10.refs_0_.refs_6_ = bf16[14,128,128]{2,1,0:T(8,128)(2,1)S(1)} collective-permute-done((bf16[14,128,128]{2,1,0:T(8,128)(2,1)S(1)}, bf16[14,128,128]{2,1,0:T(8,128)(2,1)S(1)}, u32[]{:S(2)}, u32[]{:S(2)}) %collective-permute-start.10) | collective-permute-done | bytes 458784 | tf_op jit(solution)/shard_map/down_chip/ppermute | solution.py:111
  42.4 1.5 %collective-permute-start.19 = (bf16[14,128,128]{2,1,0:T(8,128)(2,1)S(1)}, bf16[14,128,128]{2,1,0:T(8,128)(2,1)S(1)}, u32[]{:S(2)}, u32[]{:S(2)}) collective-permute-start(bf16[14,128,128]{2,1,0:T(8,128)(2,1)S(1)} %collective-permute-done.10.refs_0_.refs_6_), channel_id=1, source_target_pairs={{0,16},{16,0},{1,17},{17,1},{2,18},{18,2},{3,19},{19,3},{4,20},{20... | collective-permute-start | bytes 1376264 | tf_op jit(solution)/shard_map/down_part/ppermute | solution.py:117
  43.9 1.4 %shard_map.133 = (f32[28,128,128]{2,1,0:T(8,128)S(1)}, f32[28,128,128]{2,1,0:T(8,128)S(1)}) custom-call(s32[4]{0:T(128)S(1)} %pad_add_fusion.where_ref, s32[3]{0:T(128)S(1)} %bitcast.41, s32[2,112]{1,0:T(2,128)S(1)} %bitcast.68, f32[28,128,128]{2,1,0:T(8,128)S(1)} %get-tuple-element.66.acc_in, bf16[128,4096]{1,0:T(8,128)(2,1)S(1)} %copy-done, ...), custom_call_target="tpu_custom_call" | custom-call | flops 28 | bytes 28 | tf_op jit(solution)/shard_map/pallas_call | solution.py:30
  45.3 1.8 %shard_map.134 = (f32[28,128,128]{2,1,0:T(8,128)S(1)}, bf16[28,32,128]{2,1,0:T(8,128)(2,1)S(1)}, bf16[28,32,128]{2,1,0:T(8,128)(2,1)S(1)}, bf16[28,32,128]{2,1,0:T(8,128)(2,1)S(1)}, bf16[28,32,128]{2,1,0:T(8,128)(2,1)S(1)}) custom-call(s32[4]{0:T(128)S(1)} %pad_add_fusion.where_ref, s32[3]{0:T(128)S(1)} %bitcast.42, ...), custom_call_target="tpu_custom_call", output_to_operand_aliasing={{0}: (3, {})} | custom-call | flops 48 | bytes 48 | tf_op jit(solution)/shard_map/pallas_call | solution.py:30
  49.7 1.4 %shard_map.135 = bf16[28,128,128]{2,1,0:T(8,128)(2,1)S(1)} custom-call(s32[4]{0:T(128)S(1)} %pad_add_fusion.where_ref, s32[3]{0:T(128)S(1)} %bitcast.43, s32[2,112]{1,0:T(2,128)S(1)} %bitcast.61, bf16[28,32,128]{2,1,0:T(8,128)(2,1)S(1)} %get-tuple-element.104.refs_0_, bf16[28,32,128]{2,1,0:T(8,128)(2,1)S(1)} %get-tuple-element.105.refs_1_, ...), custom_call_target="tpu_custom_call" | custom-call | flops 28 | bytes 28 | tf_op jit(solution)/shard_map/pallas_call | solution.py:30
  51.1 4.0 %collective-permute-done.19.refs_0_.refs_8_ = bf16[14,128,128]{2,1,0:T(8,128)(2,1)S(1)} collective-permute-done((bf16[14,128,128]{2,1,0:T(8,128)(2,1)S(1)}, bf16[14,128,128]{2,1,0:T(8,128)(2,1)S(1)}, u32[]{:S(2)}, u32[]{:S(2)}) %collective-permute-start.19) | collective-permute-done | bytes 458784 | tf_op jit(solution)/shard_map/down_part/ppermute | solution.py:117
  55.2 1.4 %collective-permute-start.25 = (bf16[28,128,128]{2,1,0:T(8,128)(2,1)S(1)}, bf16[28,128,128]{2,1,0:T(8,128)(2,1)S(1)}, u32[]{:S(2)}, u32[]{:S(2)}) collective-permute-start(bf16[28,128,128]{2,1,0:T(8,128)(2,1)S(1)} %shard_map.135), channel_id=1, source_target_pairs={{0,8},{4,12},{8,0},{12,4},{1,9},{5,13},{9,1},{13,5},{2,10},{6,14},... | collective-permute-start | bytes 2752520 | tf_op jit(solution)/shard_map/down_grad_chip/ppermute | solution.py:111
  56.5 1.2 shard_map.136.acc_in
  57.8 1.2 %shard_map.137 = (bf16[28,64,128]{2,1,0:T(8,128)(2,1)S(1)}, bf16[28,64,128]{2,1,0:T(8,128)(2,1)S(1)}, bf16[28,128,128]{2,1,0:T(8,128)(2,1)S(1)}) custom-call(s32[4]{0:T(128)S(1)} %pad_add_fusion.where_ref, s32[3]{0:T(128)S(1)} %bitcast.45, s32[2,112]{1,0:T(2,128)S(1)} %bitcast.63, f32[28,128,128]{2,1,0:T(8,128)S(1)} %shard_map.136.acc_in, ...), custom_call_target="tpu_custom_call" | custom-call | flops 38 | bytes 38 | tf_op jit(solution)/shard_map/pallas_call | solution.py:30
  59.8 4.1 %shard_map.138 = (bf16[2,128,1024]{2,1,0:T(8,128)(2,1)S(1)}, bf16[2,128,1024]{2,1,0:T(8,128)(2,1)S(1)}) custom-call(s32[4]{0:T(128)S(1)} %pad_add_fusion.where_ref, s32[3]{0:T(128)S(1)} %bitcast.46, s32[2,112]{1,0:T(2,128)S(1)} %bitcast.64, bf16[28,32,128]{2,1,0:T(8,128)(2,1)S(1)} %get-tuple-element.104.refs_0_, ...), custom_call_target="tpu_custom_call" | custom-call | flops 112 | bytes 112 | tf_op jit(solution)/shard_map/pallas_call | solution.py:30
  63.9 0.8 shard_map.139
  64.8 1.4 %collective-permute-start.24 = (bf16[2,128,1024]{2,1,0:T(8,128)(2,1)S(1)}, bf16[2,128,1024]{2,1,0:T(8,128)(2,1)S(1)}, u32[]{:S(2)}, u32[]{:S(2)}) collective-permute-start(bf16[2,128,1024]{2,1,0:T(8,128)(2,1)S(1)} %get-tuple-element.94), channel_id=1, source_target_pairs={{0,1},{1,0},{2,3},{3,2},{4,5},{5,4},{6,7},{7,6},{8,9},{9,8},{10,11... | collective-permute-start | bytes 1572872 | tf_op jit(solution)/shard_map/out_group/ppermute | solution.py:121
  66.2 3.5 %shard_map.140.refs_8_ = f32[32,128,128]{2,1,0:T(8,128)S(1)} custom-call(s32[4]{0:T(128)S(1)} %pad_add_fusion.where_ref, s32[3]{0:T(128)S(1)} %bitcast.48, s32[2,112]{1,0:T(2,128)S(1)} %bitcast.70, bf16[28,64,128]{2,1,0:T(8,128)(2,1)S(1)} %get-tuple-element.96.refs_2_.refs_0_, bf16[28,64,128]{2,1,0:T(8,128)(2,1)S(1)} %get-tuple-element.97.refs_3_.refs_1_, ...), custom_call_target="tpu_custom_call" | custom-call | flops 112 | bytes 112 | tf_op jit(solution)/shard_map/pallas_call | solution.py:30
  69.7 8.2 %collective-permute-done.25 = bf16[28,128,128]{2,1,0:T(8,128)(2,1)S(1)} collective-permute-done((bf16[28,128,128]{2,1,0:T(8,128)(2,1)S(1)}, bf16[28,128,128]{2,1,0:T(8,128)(2,1)S(1)}, u32[]{:S(2)}, u32[]{:S(2)}) %collective-permute-start.25) | collective-permute-done | bytes 917536 | tf_op jit(solution)/shard_map/down_grad_chip/ppermute | solution.py:111
  77.9 1.4 %collective-permute-start.27 = (bf16[28,128,128]{2,1,0:T(8,128)(2,1)S(1)}, bf16[28,128,128]{2,1,0:T(8,128)(2,1)S(1)}, u32[]{:S(2)}, u32[]{:S(2)}) collective-permute-start(bf16[28,128,128]{2,1,0:T(8,128)(2,1)S(1)} %shard_map.139), channel_id=1, source_target_pairs={{0,8},{4,12},{8,0},{12,4},{1,9},{5,13},{9,1},{13,5},{2,10},{6,14},... | collective-permute-start | bytes 2752520 | tf_op jit(solution)/shard_map/gate_grad_chip/ppermute | solution.py:111
  79.3 5.5 %shard_map.141 = (bf16[2,128,1024]{2,1,0:T(8,128)(2,1)S(1)}, bf16[2,128,1024]{2,1,0:T(8,128)(2,1)S(1)}, f32[32,128,128]{2,1,0:T(8,128)S(1)}) custom-call(s32[4]{0:T(128)S(1)} %pad_add_fusion.where_ref, s32[3]{0:T(128)S(1)} %bitcast.49, s32[2,112]{1,0:T(2,128)S(1)} %bitcast.57, ...), custom_call_target="tpu_custom_call", output_to_operand_aliasing={{2}: (11, {})} | custom-call | flops 112 | bytes 112 | tf_op jit(solution)/shard_map/pallas_call | solution.py:30
  84.8 2.0 %shard_map.145 = bf16[28,128,128]{2,1,0:T(8,128)(2,1)S(1)} custom-call(s32[4]{0:T(128)S(1)} %pad_add_fusion.where_ref, s32[3]{0:T(128)S(1)} %bitcast.50, s32[2,112]{1,0:T(2,128)S(1)} %bitcast.58, bf16[128,4096]{1,0:T(8,128)(2,1)S(1)} %copy-done, bf16[128,4096]{1,0:T(8,128)(2,1)S(1)} %collective-permute-done.21.refs_1_, ...), custom_call_target="tpu_custom_call" | custom-call | flops 28 | bytes 28 | tf_op jit(solution)/shard_map/pallas_call | solution.py:30
  87.1 2.4 %collective-permute-start.26 = (bf16[1,128,1024]{2,1,0:T(8,128)(2,1)S(1)}, bf16[1,128,1024]{2,1,0:T(8,128)(2,1)S(1)}, u32[]{:S(2)}, u32[]{:S(2)}) collective-permute-start(bf16[1,128,1024]{2,1,0:T(8,128)(2,1)S(1)} %slice.21), channel_id=1, source_target_pairs={{0,2},{1,3},{2,0},{3,1},{4,6},{5,7},{6,4},{7,5},{8,10},{9,11},{10,... | collective-permute-start | bytes 786440 | tf_op jit(solution)/shard_map/out_group/ppermute | solution.py:121
  89.4 0.6 collective-permute-start.31
  90.0 2.0 %shard_map.142 = bf16[28,128,128]{2,1,0:T(8,128)(2,1)S(1)} custom-call(s32[4]{0:T(128)S(1)} %pad_add_fusion.where_ref, s32[3]{0:T(128)S(1)} %bitcast.51, s32[2,112]{1,0:T(2,128)S(1)} %bitcast.65, bf16[28,32,128]{2,1,0:T(8,128)(2,1)S(1)} %get-tuple-element.104.refs_0_, bf16[28,32,128]{2,1,0:T(8,128)(2,1)S(1)} %get-tuple-element.105.refs_1_, ...), custom_call_target="tpu_custom_call" | custom-call | flops 28 | bytes 28 | tf_op jit(solution)/shard_map/pallas_call | solution.py:30
  92.0 1.2 %fusion = bf16[1,28,128,128]{3,2,1,0:T(8,128)(2,1)} fusion(bf16[28,128,128]{2,1,0:T(8,128)(2,1)S(1)} %collective-permute-done.25, bf16[28,128,128]{2,1,0:T(8,128)(2,1)S(1)} %shard_map.142), kind=kLoop, calls=%fused_computation.5 | loop fusion | flops 1835008 | bytes 2752512 | tf_op jit(solution)/shard_map/broadcast_in_dim | solution.py:357
  93.3 7.9 %collective-permute-done.27 = bf16[28,128,128]{2,1,0:T(8,128)(2,1)S(1)} collective-permute-done((bf16[28,128,128]{2,1,0:T(8,128)(2,1)S(1)}, bf16[28,128,128]{2,1,0:T(8,128)(2,1)S(1)}, u32[]{:S(2)}, u32[]{:S(2)}) %collective-permute-start.27) | collective-permute-done | bytes 917536 | tf_op jit(solution)/shard_map/gate_grad_chip/ppermute | solution.py:111
  101.2 2.5 %collective-permute-done.28 = bf16[2,128,1024]{2,1,0:T(8,128)(2,1)S(1)} collective-permute-done((bf16[2,128,1024]{2,1,0:T(8,128)(2,1)S(1)}, bf16[2,128,1024]{2,1,0:T(8,128)(2,1)S(1)}, u32[]{:S(2)}, u32[]{:S(2)}) %collective-permute-start.28) | collective-permute-done | bytes 524320 | tf_op jit(solution)/shard_map/token_group/ppermute | solution.py:121
  104.1 2.0 %shard_map.143 = bf16[28,128,128]{2,1,0:T(8,128)(2,1)S(1)} custom-call(s32[4]{0:T(128)S(1)} %pad_add_fusion.where_ref, s32[3]{0:T(128)S(1)} %bitcast.52, s32[2,112]{1,0:T(2,128)S(1)} %bitcast.71, bf16[128,4096]{1,0:T(8,128)(2,1)S(1)} %copy-done, bf16[128,4096]{1,0:T(8,128)(2,1)S(1)} %collective-permute-done.21.refs_1_, ...), custom_call_target="tpu_custom_call" | custom-call | flops 28 | bytes 28 | tf_op jit(solution)/shard_map/pallas_call | solution.py:30
  106.1 1.3 %fusion.1 = bf16[1,28,128,128]{3,2,1,0:T(8,128)(2,1)} fusion(bf16[28,128,128]{2,1,0:T(8,128)(2,1)S(1)} %collective-permute-done.27, bf16[28,128,128]{2,1,0:T(8,128)(2,1)S(1)} %shard_map.143), kind=kLoop, calls=%fused_computation.6 | loop fusion | flops 1835008 | bytes 2752512 | tf_op jit(solution)/shard_map/broadcast_in_dim | solution.py:357
  107.4 2.0 %shard_map.144 = bf16[28,128,128]{2,1,0:T(8,128)(2,1)S(1)} custom-call(s32[4]{0:T(128)S(1)} %pad_add_fusion.where_ref, s32[3]{0:T(128)S(1)} %bitcast.53, s32[2,112]{1,0:T(2,128)S(1)} %bitcast.59, bf16[128,4096]{1,0:T(8,128)(2,1)S(1)} %copy-done, bf16[128,4096]{1,0:T(8,128)(2,1)S(1)} %collective-permute-done.21.refs_1_, ...), custom_call_target="tpu_custom_call" | custom-call | flops 28 | bytes 28 | tf_op jit(solution)/shard_map/pallas_call | solution.py:30
  109.4 0.8 fusion.3
  110.2 6.8 %collective-permute-done.29 = bf16[1,128,1024]{2,1,0:T(8,128)(2,1)S(1)} collective-permute-done((bf16[1,128,1024]{2,1,0:T(8,128)(2,1)S(1)}, bf16[1,128,1024]{2,1,0:T(8,128)(2,1)S(1)}, u32[]{:S(2)}, u32[]{:S(2)}) %collective-permute-start.29) | collective-permute-done | bytes 262176 | tf_op jit(solution)/shard_map/token_group/ppermute | solution.py:121
  117.0 0.8 fusion.4
  117.7 1.8 %collective-permute-done.31 = bf16[28,128,128]{2,1,0:T(8,128)(2,1)S(1)} collective-permute-done((bf16[28,128,128]{2,1,0:T(8,128)(2,1)S(1)}, bf16[28,128,128]{2,1,0:T(8,128)(2,1)S(1)}, u32[]{:S(2)}, u32[]{:S(2)}) %collective-permute-start.31) | collective-permute-done | bytes 917536 | tf_op jit(solution)/shard_map/up_grad_chip/ppermute | solution.py:111
  119.6 1.2 %fusion.2 = bf16[1,28,128,128]{3,2,1,0:T(8,128)(2,1)} fusion(bf16[28,128,128]{2,1,0:T(8,128)(2,1)S(1)} %collective-permute-done.31, bf16[28,128,128]{2,1,0:T(8,128)(2,1)S(1)} %shard_map.144), kind=kLoop, calls=%fused_computation.7 | loop fusion | flops 1835008 | bytes 2752512 | tf_op jit(solution)/shard_map/broadcast_in_dim | solution.py:357
  (67 shorter events, 6.8 us)
Async XLA Ops:
  0.6 6.8 %copy-start.6 = (s32[3,1]{0,1:T(1,128)S(1)}, s32[3,1]{0,1:T(1,128)}, u32[]{:S(2)}) copy-start(s32[3,1]{0,1:T(1,128)} %param.17) | copy-start | bytes 40
  0.6 6.8 %copy-start = (bf16[128,4096]{1,0:T(8,128)(2,1)S(1)}, bf16[128,4096]{1,0:T(8,128)(2,1)}, u32[]{:S(2)}) copy-start(bf16[128,4096]{1,0:T(8,128)(2,1)} %refs_0_.5) | copy-start | bytes 3145732
  0.7 6.8 %copy-start.9 = (s32[2,1,112]{2,1,0:T(1,128)S(1)}, s32[2,1,112]{2,1,0:T(1,128)}, u32[]{:S(2)}) copy-start(s32[2,1,112]{2,1,0:T(1,128)} %param.14) | copy-start | bytes 2692
  0.7 16.7 %collective-permute-start.3 = (bf16[128,4096]{1,0:T(8,128)(2,1)}, bf16[128,4096]{1,0:T(8,128)(2,1)S(1)}, u32[]{:S(2)}, u32[]{:S(2)}) collective-permute-start(bf16[128,4096]{1,0:T(8,128)(2,1)} %refs_8_.3), channel_id=1, source_target_pairs={{0,4},{4,0},{8,12},{12,8},{1,5},{5,1},{9,13},{13,9},{2,6},{6,2},{1... | collective-permute-start | bytes 3145736 | tf_op jit(solution)/shard_map/cotangent_core/ppermute | solution.py:107
  1.2 6.2 %collective-permute-start.2 = (bf16[28,128,128]{2,1,0:T(8,128)(2,1)}, bf16[28,128,128]{2,1,0:T(8,128)(2,1)}, u32[]{:S(2)}, u32[]{:S(2)}) collective-permute-start(bf16[28,128,128]{2,1,0:T(8,128)(2,1)} %bitcast.27), channel_id=1, source_target_pairs={{0,4},{4,0},{8,12},{12,8},{1,5},{5,1},{9,13},{13,9},{2,6},{6,2},{1... | collective-permute-start | bytes 2752520 | tf_op jit(solution)/shard_map/gate_core/ppermute | solution.py:107
  1.3 19.4 %collective-permute-start = (bf16[28,128,128]{2,1,0:T(8,128)(2,1)}, bf16[28,128,128]{2,1,0:T(8,128)(2,1)S(1)}, u32[]{:S(2)}, u32[]{:S(2)}) collective-permute-start(bf16[28,128,128]{2,1,0:T(8,128)(2,1)} %bitcast.30), channel_id=1, source_target_pairs={{0,4},{4,0},{8,12},{12,8},{1,5},{5,1},{9,13},{13,9},{2,6},{6,2},{1... | collective-permute-start | bytes 2752520 | tf_op jit(solution)/shard_map/up_core/ppermute | solution.py:107
  3.5 13.9 %collective-permute-start.1 = (bf16[14,128,128]{2,1,0:T(8,128)(2,1)}, bf16[14,128,128]{2,1,0:T(8,128)(2,1)S(1)}, u32[]{:S(2)}, u32[]{:S(2)}) collective-permute-start(bf16[14,128,128]{2,1,0:T(8,128)(2,1)} %dynamic-slice_bitcast_fusion.1), channel_id=1, source_target_pairs={{0,8},{4,12},{8,0},{12,4},{1,9},{5,13},{9,1},{13,5},{2,10},{6,14},... | collective-permute-start | bytes 1376264 | tf_op jit(solution)/shard_map/gate_chip/ppermute | solution.py:111
  6.1 17.3 %collective-permute-start.6 = (bf16[28,128,128]{2,1,0:T(8,128)(2,1)}, bf16[28,128,128]{2,1,0:T(8,128)(2,1)}, u32[]{:S(2)}, u32[]{:S(2)}) collective-permute-start(bf16[28,128,128]{2,1,0:T(8,128)(2,1)} %bitcast.33), channel_id=1, source_target_pairs={{0,4},{4,0},{8,12},{12,8},{1,5},{5,1},{9,13},{13,9},{2,6},{6,2},{1... | collective-permute-start | bytes 2752520 | tf_op jit(solution)/shard_map/down_core/ppermute | solution.py:107
  7.4 1.2 copy-start.2
  8.6 12.1 %copy-start.4 = (bf16[1,28,128,128]{3,2,1,0:T(8,128)(2,1)S(1)}, bf16[1,28,128,128]{3,2,1,0:T(8,128)(2,1)}, u32[]{:S(2)}) copy-start(bf16[1,28,128,128]{3,2,1,0:T(8,128)(2,1)} %param.12) | copy-start | bytes 2752516
  8.6 12.1 %copy-start.7 = (s32[2,1,112]{2,1,0:T(1,128)S(1)}, s32[2,1,112]{2,1,0:T(1,128)}, u32[]{:S(2)}) copy-start(s32[2,1,112]{2,1,0:T(1,128)} %param.15) | copy-start | bytes 2692
  17.4 12.3 %collective-permute-start.4 = (bf16[14,128,128]{2,1,0:T(8,128)(2,1)S(1)}, bf16[14,128,128]{2,1,0:T(8,128)(2,1)S(1)}, u32[]{:S(2)}, u32[]{:S(2)}) collective-permute-start(bf16[14,128,128]{2,1,0:T(8,128)(2,1)S(1)} %dynamic-slice_bitcast_fusion.2), channel_id=1, source_target_pairs={{0,8},{4,12},{8,0},{12,4},{1,9},{5,13},{9,1},{13,5},{2,10},{6,14},... | collective-permute-start | bytes 1376264 | tf_op jit(solution)/shard_map/up_chip/ppermute | solution.py:111
  19.2 11.8 %collective-permute-start.5 = (bf16[14,128,128]{2,1,0:T(8,128)(2,1)S(1)}, bf16[14,128,128]{2,1,0:T(8,128)(2,1)S(1)}, u32[]{:S(2)}, u32[]{:S(2)}) collective-permute-start(bf16[14,128,128]{2,1,0:T(8,128)(2,1)S(1)} %collective-permute-done.1.refs_0_.refs_4_), channel_id=1, source_target_pairs={{0,16},{16,0},{1,17},{17,1},{2,18},{18,2},{3,19},{19,3},{4,20},{20... | collective-permute-start | bytes 1376264 | tf_op jit(solution)/shard_map/gate_part/ppermute | solution.py:117
  20.7 2.6 %copy-start.5 = (bf16[1,28,128,128]{3,2,1,0:T(8,128)(2,1)S(1)}, bf16[1,28,128,128]{3,2,1,0:T(8,128)(2,1)}, u32[]{:S(2)}) copy-start(bf16[1,28,128,128]{3,2,1,0:T(8,128)(2,1)} %param.13) | copy-start | bytes 2752516
  20.7 2.7 %copy-start.1 = (bf16[128,4096]{1,0:T(8,128)(2,1)S(1)}, bf16[128,4096]{1,0:T(8,128)(2,1)}, u32[]{:S(2)}) copy-start(bf16[128,4096]{1,0:T(8,128)(2,1)} %refs_8_.3) | copy-start | bytes 3145732
  20.7 2.7 %copy-start.8 = (s32[2,1,112]{2,1,0:T(1,128)S(1)}, s32[2,1,112]{2,1,0:T(1,128)}, u32[]{:S(2)}) copy-start(s32[2,1,112]{2,1,0:T(1,128)} %param.16) | copy-start | bytes 2692
  23.2 9.8 %collective-permute-start.7 = (bf16[14,128,128]{2,1,0:T(8,128)(2,1)S(1)}, bf16[14,128,128]{2,1,0:T(8,128)(2,1)S(1)}, u32[]{:S(2)}, u32[]{:S(2)}) collective-permute-start(bf16[14,128,128]{2,1,0:T(8,128)(2,1)S(1)} %collective-permute-done.1.refs_0_.refs_4_), channel_id=1, source_target_pairs={{0,4},{4,0},{8,12},{12,8},{1,5},{5,1},{9,13},{13,9},{2,6},{6,2},{1... | collective-permute-start | bytes 1376264 | tf_op jit(solution)/shard_map/gate_x_core/ppermute | solution.py:107
  31.0 10.9 %collective-permute-start.10 = (bf16[14,128,128]{2,1,0:T(8,128)(2,1)S(1)}, bf16[14,128,128]{2,1,0:T(8,128)(2,1)S(1)}, u32[]{:S(2)}, u32[]{:S(2)}) collective-permute-start(bf16[14,128,128]{2,1,0:T(8,128)(2,1)S(1)} %dynamic-slice_bitcast_fusion), channel_id=1, source_target_pairs={{0,8},{4,12},{8,0},{12,4},{1,9},{5,13},{9,1},{13,5},{2,10},{6,14},... | collective-permute-start | bytes 1376264 | tf_op jit(solution)/shard_map/down_chip/ppermute | solution.py:111
  31.4 10.8 %collective-permute-start.12 = (bf16[14,128,128]{2,1,0:T(8,128)(2,1)S(1)}, bf16[14,128,128]{2,1,0:T(8,128)(2,1)S(1)}, u32[]{:S(2)}, u32[]{:S(2)}) collective-permute-start(bf16[14,128,128]{2,1,0:T(8,128)(2,1)S(1)} %collective-permute-done.4.refs_2_.refs_0_.refs_3_), channel_id=1, source_target_pairs={{0,16},{16,0},{1,17},{17,1},{2,18},{18,2},{3,19},{19,3},{4,20},{20... | collective-permute-start | bytes 1376264 | tf_op jit(solution)/shard_map/up_part/ppermute | solution.py:117
  33.7 1.6 %collective-permute-start.8 = (bf16[7,128,128]{2,1,0:T(8,128)(2,1)S(1)}, bf16[7,128,128]{2,1,0:T(8,128)(2,1)S(1)}, u32[]{:S(2)}, u32[]{:S(2)}) collective-permute-start(bf16[7,128,128]{2,1,0:T(8,128)(2,1)S(1)} %get-tuple-element.64), channel_id=1, source_target_pairs={{0,4},{4,0},{8,12},{12,8},{1,5},{5,1},{9,13},{13,9},{2,6},{6,2},{1... | collective-permute-start | bytes 688136 | tf_op jit(solution)/shard_map/up_x_core/ppermute | solution.py:107
  33.7 1.8 %collective-permute-start.9 = (bf16[7,128,128]{2,1,0:T(8,128)(2,1)S(1)}, bf16[7,128,128]{2,1,0:T(8,128)(2,1)S(1)}, u32[]{:S(2)}, u32[]{:S(2)}) collective-permute-start(bf16[7,128,128]{2,1,0:T(8,128)(2,1)S(1)} %get-tuple-element.65), channel_id=1, source_target_pairs={{0,4},{4,0},{8,12},{12,8},{1,5},{5,1},{9,13},{13,9},{2,6},{6,2},{1... | collective-permute-start | bytes 688136 | tf_op jit(solution)/shard_map/up_x_core/ppermute | solution.py:107
  41.9 2.0 %collective-permute-start.11 = (bf16[14,128,128]{2,1,0:T(8,128)(2,1)S(1)}, bf16[14,128,128]{2,1,0:T(8,128)(2,1)S(1)}, u32[]{:S(2)}, u32[]{:S(2)}) collective-permute-start(bf16[14,128,128]{2,1,0:T(8,128)(2,1)S(1)} %collective-permute-done.5.refs_0_.refs_6_), channel_id=1, source_target_pairs={{0,4},{4,0},{8,12},{12,8},{1,5},{5,1},{9,13},{13,9},{2,6},{6,2},{1... | collective-permute-start | bytes 1376264 | tf_op jit(solution)/shard_map/gate_y_core/ppermute | solution.py:107
  42.2 3.1 %collective-permute-start.13 = (bf16[14,128,128]{2,1,0:T(8,128)(2,1)S(1)}, bf16[14,128,128]{2,1,0:T(8,128)(2,1)S(1)}, u32[]{:S(2)}, u32[]{:S(2)}) collective-permute-start(bf16[14,128,128]{2,1,0:T(8,128)(2,1)S(1)} %collective-permute-done.12.refs_0_.refs_6_), channel_id=1, source_target_pairs={{0,4},{4,0},{8,12},{12,8},{1,5},{5,1},{9,13},{13,9},{2,6},{6,2},{1... | collective-permute-start | bytes 1376264 | tf_op jit(solution)/shard_map/up_y_core/ppermute | solution.py:107
  42.4 12.8 %collective-permute-start.19 = (bf16[14,128,128]{2,1,0:T(8,128)(2,1)S(1)}, bf16[14,128,128]{2,1,0:T(8,128)(2,1)S(1)}, u32[]{:S(2)}, u32[]{:S(2)}) collective-permute-start(bf16[14,128,128]{2,1,0:T(8,128)(2,1)S(1)} %collective-permute-done.10.refs_0_.refs_6_), channel_id=1, source_target_pairs={{0,16},{16,0},{1,17},{17,1},{2,18},{18,2},{3,19},{19,3},{4,20},{20... | collective-permute-start | bytes 1376264 | tf_op jit(solution)/shard_map/down_part/ppermute | solution.py:117
  47.2 1.6 %collective-permute-start.14 = (bf16[28,32,128]{2,1,0:T(8,128)(2,1)S(1)}, bf16[28,32,128]{2,1,0:T(8,128)(2,1)S(1)}, u32[]{:S(2)}, u32[]{:S(2)}) collective-permute-start(bf16[28,32,128]{2,1,0:T(8,128)(2,1)S(1)} %get-tuple-element.104.refs_0_), channel_id=1, source_target_pairs={{0,4},{4,0},{8,12},{12,8},{1,5},{5,1},{9,13},{13,9},{2,6},{6,2},{1... | collective-permute-start | bytes 688136 | tf_op jit(solution)/shard_map/hidden_core/ppermute | solution.py:107
  47.3 1.8 %collective-permute-start.15 = (bf16[28,32,128]{2,1,0:T(8,128)(2,1)S(1)}, bf16[28,32,128]{2,1,0:T(8,128)(2,1)S(1)}, u32[]{:S(2)}, u32[]{:S(2)}) collective-permute-start(bf16[28,32,128]{2,1,0:T(8,128)(2,1)S(1)} %get-tuple-element.105.refs_1_), channel_id=1, source_target_pairs={{0,4},{4,0},{8,12},{12,8},{1,5},{5,1},{9,13},{13,9},{2,6},{6,2},{1... | collective-permute-start | bytes 688136 | tf_op jit(solution)/shard_map/hidden_core/ppermute | solution.py:107
  47.7 1.6 %collective-permute-start.16 = (bf16[28,32,128]{2,1,0:T(8,128)(2,1)S(1)}, bf16[28,32,128]{2,1,0:T(8,128)(2,1)S(1)}, u32[]{:S(2)}, u32[]{:S(2)}) collective-permute-start(bf16[28,32,128]{2,1,0:T(8,128)(2,1)S(1)} %get-tuple-element.106.refs_2_), channel_id=1, source_target_pairs={{0,4},{4,0},{8,12},{12,8},{1,5},{5,1},{9,13},{13,9},{2,6},{6,2},{1... | collective-permute-start | bytes 688136 | tf_op jit(solution)/shard_map/hidden_core/ppermute | solution.py:107
  47.8 1.9 %collective-permute-start.17 = (bf16[28,32,128]{2,1,0:T(8,128)(2,1)S(1)}, bf16[28,32,128]{2,1,0:T(8,128)(2,1)S(1)}, u32[]{:S(2)}, u32[]{:S(2)}) collective-permute-start(bf16[28,32,128]{2,1,0:T(8,128)(2,1)S(1)} %get-tuple-element.107.refs_3_), channel_id=1, source_target_pairs={{0,4},{4,0},{8,12},{12,8},{1,5},{5,1},{9,13},{13,9},{2,6},{6,2},{1... | collective-permute-start | bytes 688136 | tf_op jit(solution)/shard_map/hidden_core/ppermute | solution.py:107
  48.7 15.2 %collective-permute-start.21 = (bf16[128,4096]{1,0:T(8,128)(2,1)S(1)}, bf16[128,4096]{1,0:T(8,128)(2,1)S(1)}, u32[]{:S(2)}, u32[]{:S(2)}) collective-permute-start(bf16[128,4096]{1,0:T(8,128)(2,1)S(1)} %copy-done), channel_id=1, source_target_pairs={{0,4},{4,0},{8,12},{12,8},{1,5},{5,1},{9,13},{13,9},{2,6},{6,2},{1... | collective-permute-start | bytes 3145736 | tf_op jit(solution)/shard_map/tokens_core/ppermute | solution.py:107
  49.0 7.5 %collective-permute-start.18 = (bf16[14,128,128]{2,1,0:T(8,128)(2,1)S(1)}, bf16[14,128,128]{2,1,0:T(8,128)(2,1)S(1)}, u32[]{:S(2)}, u32[]{:S(2)}) collective-permute-start(bf16[14,128,128]{2,1,0:T(8,128)(2,1)S(1)} %collective-permute-done.10.refs_0_.refs_6_), channel_id=1, source_target_pairs={{0,4},{4,0},{8,12},{12,8},{1,5},{5,1},{9,13},{13,9},{2,6},{6,2},{1... | collective-permute-start | bytes 1376264 | tf_op jit(solution)/shard_map/down_x_core/ppermute | solution.py:107
  55.2 2.6 %collective-permute-start.20 = (bf16[14,128,128]{2,1,0:T(8,128)(2,1)S(1)}, bf16[14,128,128]{2,1,0:T(8,128)(2,1)S(1)}, u32[]{:S(2)}, u32[]{:S(2)}) collective-permute-start(bf16[14,128,128]{2,1,0:T(8,128)(2,1)S(1)} %collective-permute-done.19.refs_0_.refs_8_), channel_id=1, source_target_pairs={{0,4},{4,0},{8,12},{12,8},{1,5},{5,1},{9,13},{13,9},{2,6},{6,2},{1... | collective-permute-start | bytes 1376264 | tf_op jit(solution)/shard_map/down_y_core/ppermute | solution.py:107
  55.2 22.8 %collective-permute-start.25 = (bf16[28,128,128]{2,1,0:T(8,128)(2,1)S(1)}, bf16[28,128,128]{2,1,0:T(8,128)(2,1)S(1)}, u32[]{:S(2)}, u32[]{:S(2)}) collective-permute-start(bf16[28,128,128]{2,1,0:T(8,128)(2,1)S(1)} %shard_map.135), channel_id=1, source_target_pairs={{0,8},{4,12},{8,0},{12,4},{1,9},{5,13},{9,1},{13,5},{2,10},{6,14},... | collective-permute-start | bytes 2752520 | tf_op jit(solution)/shard_map/down_grad_chip/ppermute | solution.py:111
  59.0 4.9 %collective-permute-start.22 = (bf16[28,64,128]{2,1,0:T(8,128)(2,1)S(1)}, bf16[28,64,128]{2,1,0:T(8,128)(2,1)S(1)}, u32[]{:S(2)}, u32[]{:S(2)}) collective-permute-start(bf16[28,64,128]{2,1,0:T(8,128)(2,1)S(1)} %get-tuple-element.96.refs_2_.refs_0_), channel_id=1, source_target_pairs={{0,4},{4,0},{8,12},{12,8},{1,5},{5,1},{9,13},{13,9},{2,6},{6,2},{1... | collective-permute-start | bytes 1376264 | tf_op jit(solution)/shard_map/grads_core/ppermute | solution.py:107
  59.3 4.6 %collective-permute-start.23 = (bf16[28,64,128]{2,1,0:T(8,128)(2,1)S(1)}, bf16[28,64,128]{2,1,0:T(8,128)(2,1)S(1)}, u32[]{:S(2)}, u32[]{:S(2)}) collective-permute-start(bf16[28,64,128]{2,1,0:T(8,128)(2,1)S(1)} %get-tuple-element.97.refs_3_.refs_1_), channel_id=1, source_target_pairs={{0,4},{4,0},{8,12},{12,8},{1,5},{5,1},{9,13},{13,9},{2,6},{6,2},{1... | collective-permute-start | bytes 1376264 | tf_op jit(solution)/shard_map/grads_core/ppermute | solution.py:107
  59.6 25.3 %collective-permute-start.30 = (bf16[28,128,128]{2,1,0:T(8,128)(2,1)S(1)}, bf16[28,128,128]{2,1,0:T(8,128)(2,1)S(1)}, u32[]{:S(2)}, u32[]{:S(2)}) collective-permute-start(bf16[28,128,128]{2,1,0:T(8,128)(2,1)S(1)} %get-tuple-element.99.refs_0_.refs_2_), channel_id=1, source_target_pairs={{0,4},{4,0},{8,12},{12,8},{1,5},{5,1},{9,13},{13,9},{2,6},{6,2},{1... | collective-permute-start | bytes 2752520 | tf_op jit(solution)/shard_map/grads_core/ppermute | solution.py:107
  63.9 2.3 %copy-start.3 = (bf16[1,28,128,128]{3,2,1,0:T(8,128)(2,1)S(1)}, bf16[1,28,128,128]{3,2,1,0:T(8,128)(2,1)}, u32[]{:S(2)}) copy-start(bf16[1,28,128,128]{3,2,1,0:T(8,128)(2,1)} %param.11) | copy-start | bytes 2752516
  64.8 22.1 %collective-permute-start.24 = (bf16[2,128,1024]{2,1,0:T(8,128)(2,1)S(1)}, bf16[2,128,1024]{2,1,0:T(8,128)(2,1)S(1)}, u32[]{:S(2)}, u32[]{:S(2)}) collective-permute-start(bf16[2,128,1024]{2,1,0:T(8,128)(2,1)S(1)} %get-tuple-element.94), channel_id=1, source_target_pairs={{0,1},{1,0},{2,3},{3,2},{4,5},{5,4},{6,7},{7,6},{8,9},{9,8},{10,11... | collective-permute-start | bytes 1572872 | tf_op jit(solution)/shard_map/out_group/ppermute | solution.py:121
  77.9 23.3 %collective-permute-start.27 = (bf16[28,128,128]{2,1,0:T(8,128)(2,1)S(1)}, bf16[28,128,128]{2,1,0:T(8,128)(2,1)S(1)}, u32[]{:S(2)}, u32[]{:S(2)}) collective-permute-start(bf16[28,128,128]{2,1,0:T(8,128)(2,1)S(1)} %shard_map.139), channel_id=1, source_target_pairs={{0,8},{4,12},{8,0},{12,4},{1,9},{5,13},{9,1},{13,5},{2,10},{6,14},... | collective-permute-start | bytes 2752520 | tf_op jit(solution)/shard_map/gate_grad_chip/ppermute | solution.py:111
  84.8 19.0 %collective-permute-start.28 = (bf16[2,128,1024]{2,1,0:T(8,128)(2,1)S(1)}, bf16[2,128,1024]{2,1,0:T(8,128)(2,1)S(1)}, u32[]{:S(2)}, u32[]{:S(2)}) collective-permute-start(bf16[2,128,1024]{2,1,0:T(8,128)(2,1)S(1)} %get-tuple-element.101), channel_id=1, source_target_pairs={{0,1},{1,0},{2,3},{3,2},{4,5},{5,4},{6,7},{7,6},{8,9},{9,8},{10,11... | collective-permute-start | bytes 1572872 | tf_op jit(solution)/shard_map/token_group/ppermute | solution.py:121
  87.1 22.3 %collective-permute-start.26 = (bf16[1,128,1024]{2,1,0:T(8,128)(2,1)S(1)}, bf16[1,128,1024]{2,1,0:T(8,128)(2,1)S(1)}, u32[]{:S(2)}, u32[]{:S(2)}) collective-permute-start(bf16[1,128,1024]{2,1,0:T(8,128)(2,1)S(1)} %slice.21), channel_id=1, source_target_pairs={{0,2},{1,3},{2,0},{3,1},{4,6},{5,7},{6,4},{7,5},{8,10},{9,11},{10,... | collective-permute-start | bytes 786440 | tf_op jit(solution)/shard_map/out_group/ppermute | solution.py:121
  89.4 30.1 %collective-permute-start.31 = (bf16[28,128,128]{2,1,0:T(8,128)(2,1)S(1)}, bf16[28,128,128]{2,1,0:T(8,128)(2,1)S(1)}, u32[]{:S(2)}, u32[]{:S(2)}) collective-permute-start(bf16[28,128,128]{2,1,0:T(8,128)(2,1)S(1)} %shard_map.145), channel_id=1, source_target_pairs={{0,8},{4,12},{8,0},{12,4},{1,9},{5,13},{9,1},{13,5},{2,10},{6,14},... | collective-permute-start | bytes 2752520 | tf_op jit(solution)/shard_map/up_grad_chip/ppermute | solution.py:111
  103.9 13.0 %collective-permute-start.29 = (bf16[1,128,1024]{2,1,0:T(8,128)(2,1)S(1)}, bf16[1,128,1024]{2,1,0:T(8,128)(2,1)S(1)}, u32[]{:S(2)}, u32[]{:S(2)}) collective-permute-start(bf16[1,128,1024]{2,1,0:T(8,128)(2,1)S(1)} %slice.23), channel_id=1, source_target_pairs={{0,2},{1,3},{2,0},{3,1},{4,6},{5,7},{6,4},{7,5},{8,10},{9,11},{10,... | collective-permute-start | bytes 786440 | tf_op jit(solution)/shard_map/token_group/ppermute | solution.py:121

commit v5 on v4

--- a/solution.py
+++ b/solution.py
@@ -360,24 +360,21 @@
         down_away = block_grads(2, away, *down_operands)
         down_far = [chip_shift(g, k, "down_grad") for g, k in zip(down_away, away)]
 
-        relay.append(both("down_y", after(y_d, *down_away)))
+        relay.append(both("down_y", after(y_d, tokens_pair, *down_away)))
         acc_h = go_on(2, after(acc_h, *down_away), cotangent, direct[2], direct_keys)
 
-        half_tokens = token_count // 2
-
         def back_body(where_ref, counts_ref, td, acc_in, c_ref, silu_ref, slope_ref, up_ref, *refs):
-            outs, acc = refs[-4:-1], refs[-1]
+            outs, acc = refs[-6:-1], refs[-1]
             acc[...] = acc_in[...]
-            add_pieces(acc, 2, c_ref, refs[:-4], relay_keys, td, counts_ref, where_ref)
+            add_pieces(acc, 2, c_ref, refs[:-6], relay_keys, td, counts_ref, where_ref)
 
             def finish(b, _):
                 grad = acc[b]
                 gate = (grad * up_ref[b] * slope_ref[b]).astype(BF16)
                 up = (grad * silu_ref[b]).astype(BF16)
-                for i in range(2):
-                    rows = slice(i * half_tokens, (i + 1) * half_tokens)
-                    outs[i][b] = gate[rows]
-                outs[2][b] = up
+                for i in range(4):
+                    outs[i][b] = gate[i * quarter : (i + 1) * quarter]
+                outs[4][b] = up
                 return 0
 
             lax.fori_loop(0, hidden_blocks, finish, 0)
@@ -386,7 +383,7 @@
             back_body,
             [where, counts, tables[2]],
             [acc_h, cotangent, silu, slope, up_value, *relay[2]],
-            [jax.ShapeDtypeStruct((hidden_blocks, half_tokens, size), BF16)] * 2 + [hidden_bf16],
+            [jax.ShapeDtypeStruct((hidden_blocks, quarter, size), BF16)] * 4 + [hidden_bf16],
             scratch=[pltpu.VMEM(hidden_f32.shape, F32)],
             products=shard + 10,
         )
@@ -429,15 +426,15 @@
         )
 
         grads_pair = [pair_swap(g, "grads") for g in grads]
-        grads_pair[:2] = after(grads_pair[:2], *out_parts)
-        gate_operands = ([tokens, tokens_pair], [*grads[:2], *grads_pair[:2]])
-        up_operands = ([tokens, tokens_pair], [grads[2], grads_pair[2]])
+        grads_pair[:4] = after(grads_pair[:4], *out_parts)
+        gate_operands = ([tokens, tokens_pair], [*grads[:4], *grads_pair[:4]])
+        up_operands = ([tokens, tokens_pair], [grads[4], grads_pair[4]])
         gate_away = block_grads(0, away, *gate_operands)
         up_away = block_grads(1, away, *up_operands)
         down_far = after(down_far, *gate_away)
 
         def token_body(m, last, where_ref, counts_ref, table, *refs):
-            n, n_y = len(all_keys[m]), 1 if m else 2
+            n, n_y = len(all_keys[m]), 1 if m else 4
             ys, w_refs, acc = refs[:n_y], refs[n_y : n_y + n], refs[-1]
             if not last:
                 zero(acc)
@@ -460,12 +457,11 @@
         (token_acc,) = call(
             functools.partial(token_body, 0, False),
             [where, counts, tables[0]],
-            [*after(grads[:2], *gate_away), *pieces[0]],
+            [*after(grads[:4], *down_far), *pieces[0]],
             [model_f32],
             products=4 * shard,
         )
-        down_far = after(down_far, token_acc)
-        y_up = after(grads[2], *down_far)
+        y_up = after(grads[4], token_acc)
         *token_parts, _ = call(
             functools.partial(token_body, 1, True),
             [where, counts, tables[1]],
@@ -493,7 +489,7 @@
 
         gate_sent = after(gate_away, *down_far)
         gate_far = [chip_shift(g, k, "gate_grad") for g, k in zip(gate_sent, away)]
-        out_first, *out_terms = swap_groups("out", after(out_parts, *gate_away), *token_parts)
+        out_first, *out_terms = swap_groups("out", out_parts, *token_parts)
         up_sent = after(up_away, out_first)
         up_far = [chip_shift(g, k, "up_grad") for g, k in zip(up_sent, away)]
         late_h, late_t = after(hidden, out_first), after(tokens, *gate_far)

time: 121 us -> 122 us (level); the launches traced: 121 us -> 121 us
  waiting for transfers between devices: 48.7 us -> 42.7 us
  Pallas kernels: 40.2 us -> 43.3 us
  starting transfers between devices: 21 us -> 23.7 us
    ppermute x6, waiting for transfers between devices: 31.2 us -> 17.3 us  [chip_shift(): lax.ppermute(a, 'dp', [(i, (i // 2 + k) % chips * 2 + i % 2) for i in ran...]
    ppermute x4, waiting for transfers between devices: 9.34 us -> 14 us  [group_swap(): return lax.ppermute(a, 'tensor', [(i, i ^ bit) for i in range(groups)])]
    pallas_call x18, Pallas kernels: 40.2 us -> 43.3 us  [call(): pl.pallas_call(body, out_shape=outs, in_specs=[SMEM] * len(ints) + [VMEM]...]
    ppermute x4, starting transfers between devices: 4.06 us -> 5.98 us  [group_swap(): return lax.ppermute(a, 'tensor', [(i, i ^ bit) for i in range(groups)])]
    ppermute x19 -> x21, waiting for transfers between devices: 2.46 us -> 4.17 us  [pair_swap(): return lax.ppermute(a, 'dp', [(i, i ^ 1) for i in range(dp)])]
    ppermute x3, waiting for transfers between devices: 5.69 us -> 7.26 us  [part_swap(): return lax.ppermute(a, 'parts', [(0, 1), (1, 0)])]
    ppermute x19 -> x21, starting transfers between devices: 4.18 us -> 4.46 us  [pair_swap(): return lax.ppermute(a, 'dp', [(i, i ^ 1) for i in range(dp)])]
  transfers between devices with their start and end apart: 32 -> 34, of which waited for: 17 -> 16; matrix products, arithmetic and copies ran while one was open for 6% -> 6% of each run, Pallas kernels for 33% -> 36%
where the time goes in v5:
time: 122 us; the launch traced here: 121 us
  Pallas kernels  43.3 us (35%)
  waiting for transfers between devices  42.7 us (35%)
  starting transfers between devices  23.7 us (19%)
  other arithmetic  5.75 us (5%)
  local copies, waits for them, and re-layouts  4.16 us (3%)
    pallas_call x18, Pallas kernels, call(): pl.pallas_call(body, out_shape=outs, in_specs=[SMEM] * len(ints) + [VMEM]...  43.3 us
    ppermute x6, waiting for transfers between devices, chip_shift(): lax.ppermute(a, 'dp', [(i, (i // 2 + k) % chips * 2 + i % 2) for i in ran...  17.3 us
    ppermute x4, waiting for transfers between devices, group_swap(): return lax.ppermute(a, 'tensor', [(i, i ^ bit) for i in range(groups)])  14 us
    ppermute x6, starting transfers between devices, chip_shift(): lax.ppermute(a, 'dp', [(i, (i // 2 + k) % chips * 2 + i % 2) for i in ran...  8.58 us
    ppermute x3, waiting for transfers between devices, part_swap(): return lax.ppermute(a, 'parts', [(0, 1), (1, 0)])  7.26 us
    ppermute x4, starting transfers between devices, group_swap(): return lax.ppermute(a, 'tensor', [(i, i ^ bit) for i in range(groups)])  5.98 us
    ppermute x3, starting transfers between devices, part_swap(): return lax.ppermute(a, 'parts', [(0, 1), (1, 0)])  4.64 us
    ppermute x21, starting transfers between devices, pair_swap(): return lax.ppermute(a, 'dp', [(i, i ^ 1) for i in range(dp)])  4.46 us
  transfers between devices with their start and end apart: 34, of which 16 were waited for; matrix products, arithmetic and copies ran while one was open for 6% of the time, Pallas kernels for 36%

profile of v5, /device:TPU:0, one launch (start us, length us, event | category | flops | bytes accessed | tf_op | source)
XLA Modules:
  0.0 120.6 jit_solution(18207088495553240586)
XLA Ops:
  1.7 1.8 %dynamic-slice_bitcast_fusion.1 = bf16[14,128,128]{2,1,0:T(8,128)(2,1)} fusion(bf16[1,28,128,128]{3,2,1,0:T(8,128)(2,1)} %param.11, s32[]{:T(128)S(6)} %select_n.18), kind=kLoop, calls=%fused_computation.11 | loop fusion | bytes 917508 | tf_op jit(solution)/shard_map/dynamic_slice | solution.py:153
  3.5 2.6 %collective-permute-start.1 = (bf16[14,128,128]{2,1,0:T(8,128)(2,1)}, bf16[14,128,128]{2,1,0:T(8,128)(2,1)S(1)}, u32[]{:S(2)}, u32[]{:S(2)}) collective-permute-start(bf16[14,128,128]{2,1,0:T(8,128)(2,1)} %dynamic-slice_bitcast_fusion.1), channel_id=1, source_target_pairs={{0,8},{4,12},{8,0},{12,4},{1,9},{5,13},{9,1},{13,5},{2,10},{6,14},... | collective-permute-start | bytes 1376264 | tf_op jit(solution)/shard_map/gate_chip/ppermute | solution.py:111
  6.3 1.1 dynamic-slice_bitcast_fusion.2
  7.4 1.2 copy-done.2
  8.6 3.0 %shard_map.129.acc_in = f32[28,128,128]{2,1,0:T(8,128)S(1)} custom-call(s32[4]{0:T(128)S(1)} %pad_add_fusion.where_ref, s32[3]{0:T(128)S(1)} %bitcast.36, s32[2,112]{1,0:T(2,128)S(1)} %bitcast.66, bf16[128,4096]{1,0:T(8,128)(2,1)S(1)} %copy-done, bf16[28,128,128]{2,1,0:T(8,128)(2,1)S(1)} %bitcast.28, bf16[28,128,128]{2,1,0:T(8,128)(2,1)} %collective-permute-done.2.refs_1_.refs_5_), custom_call_target="tpu_custom_call" | custom-call | flops 56 | bytes 56 | tf_op jit(solution)/shard_map/pallas_call | solution.py:30
  11.6 5.8 %collective-permute-done.1.refs_0_.refs_6_ = bf16[14,128,128]{2,1,0:T(8,128)(2,1)S(1)} collective-permute-done((bf16[14,128,128]{2,1,0:T(8,128)(2,1)}, bf16[14,128,128]{2,1,0:T(8,128)(2,1)S(1)}, u32[]{:S(2)}, u32[]{:S(2)}) %collective-permute-start.1) | collective-permute-done | bytes 458784 | tf_op jit(solution)/shard_map/gate_chip/ppermute | solution.py:111
  17.4 1.8 %collective-permute-start.4 = (bf16[14,128,128]{2,1,0:T(8,128)(2,1)S(1)}, bf16[14,128,128]{2,1,0:T(8,128)(2,1)S(1)}, u32[]{:S(2)}, u32[]{:S(2)}) collective-permute-start(bf16[14,128,128]{2,1,0:T(8,128)(2,1)S(1)} %dynamic-slice_bitcast_fusion.2), channel_id=1, source_target_pairs={{0,8},{4,12},{8,0},{12,4},{1,9},{5,13},{9,1},{13,5},{2,10},{6,14},... | collective-permute-start | bytes 1376264 | tf_op jit(solution)/shard_map/up_chip/ppermute | solution.py:111
  19.2 1.5 %collective-permute-start.5 = (bf16[14,128,128]{2,1,0:T(8,128)(2,1)S(1)}, bf16[14,128,128]{2,1,0:T(8,128)(2,1)S(1)}, u32[]{:S(2)}, u32[]{:S(2)}) collective-permute-start(bf16[14,128,128]{2,1,0:T(8,128)(2,1)S(1)} %collective-permute-done.1.refs_0_.refs_6_), channel_id=1, source_target_pairs={{0,16},{16,0},{1,17},{17,1},{2,18},{18,2},{3,19},{19,3},{4,20},{20... | collective-permute-start | bytes 1376264 | tf_op jit(solution)/shard_map/gate_part/ppermute | solution.py:117
  20.7 2.5 %shard_map.128.acc_in = f32[28,128,128]{2,1,0:T(8,128)S(1)} custom-call(s32[4]{0:T(128)S(1)} %pad_add_fusion.where_ref, s32[3]{0:T(128)S(1)} %bitcast.37, s32[2,112]{1,0:T(2,128)S(1)} %bitcast.54, bf16[128,4096]{1,0:T(8,128)(2,1)S(1)} %copy-done, bf16[28,128,128]{2,1,0:T(8,128)(2,1)S(1)} %bitcast.31, ...), custom_call_target="tpu_custom_call" | custom-call | flops 56 | bytes 56 | tf_op jit(solution)/shard_map/pallas_call | solution.py:30
  23.4 3.6 %shard_map.130.acc_in = f32[28,128,128]{2,1,0:T(8,128)S(1)} custom-call(s32[4]{0:T(128)S(1)} %pad_add_fusion.where_ref, s32[3]{0:T(128)S(1)} %bitcast.38, s32[2,112]{1,0:T(2,128)S(1)} %bitcast.60, bf16[128,4096]{1,0:T(8,128)(2,1)S(1)} %copy-done.1, bf16[28,128,128]{2,1,0:T(8,128)(2,1)S(1)} %bitcast.34, ...), custom_call_target="tpu_custom_call" | custom-call | flops 56 | bytes 56 | tf_op jit(solution)/shard_map/pallas_call | solution.py:30
  27.0 2.7 %collective-permute-done.4.refs_2_.refs_0_.refs_3_ = bf16[14,128,128]{2,1,0:T(8,128)(2,1)S(1)} collective-permute-done((bf16[14,128,128]{2,1,0:T(8,128)(2,1)S(1)}, bf16[14,128,128]{2,1,0:T(8,128)(2,1)S(1)}, u32[]{:S(2)}, u32[]{:S(2)}) %collective-permute-start.4) | collective-permute-done | bytes 458784 | tf_op jit(solution)/shard_map/up_chip/ppermute | solution.py:111
  29.7 1.3 %collective-permute-done.5.refs_0_.refs_8_ = bf16[14,128,128]{2,1,0:T(8,128)(2,1)S(1)} collective-permute-done((bf16[14,128,128]{2,1,0:T(8,128)(2,1)S(1)}, bf16[14,128,128]{2,1,0:T(8,128)(2,1)S(1)}, u32[]{:S(2)}, u32[]{:S(2)}) %collective-permute-start.5) | collective-permute-done | bytes 458784 | tf_op jit(solution)/shard_map/gate_part/ppermute | solution.py:117
  31.4 1.6 %collective-permute-start.12 = (bf16[14,128,128]{2,1,0:T(8,128)(2,1)S(1)}, bf16[14,128,128]{2,1,0:T(8,128)(2,1)S(1)}, u32[]{:S(2)}, u32[]{:S(2)}) collective-permute-start(bf16[14,128,128]{2,1,0:T(8,128)(2,1)S(1)} %collective-permute-done.4.refs_2_.refs_0_.refs_3_), channel_id=1, source_target_pairs={{0,16},{16,0},{1,17},{17,1},{2,18},{18,2},{3,19},{19,3},{4,20},{20... | collective-permute-start | bytes 1376264 | tf_op jit(solution)/shard_map/up_part/ppermute | solution.py:117
  33.0 0.6 shard_map.131
  34.3 0.9 collective-permute-done.8.refs_1_.refs_4_
  35.5 1.5 %shard_map.132.acc_in = f32[28,128,128]{2,1,0:T(8,128)S(1)} custom-call(s32[4]{0:T(128)S(1)} %pad_add_fusion.where_ref, s32[3]{0:T(128)S(1)} %bitcast.40, s32[2,112]{1,0:T(2,128)S(1)} %bitcast.55, f32[28,128,128]{2,1,0:T(8,128)S(1)} %shard_map.128.acc_in, bf16[128,4096]{1,0:T(8,128)(2,1)S(1)} %copy-done, ...), custom_call_target="tpu_custom_call", output_to_operand_aliasing={{}: (3, {})} | custom-call | flops 28 | bytes 28 | tf_op jit(solution)/shard_map/pallas_call | solution.py:30
  37.1 4.8 %collective-permute-done.10.refs_0_.refs_6_ = bf16[14,128,128]{2,1,0:T(8,128)(2,1)S(1)} collective-permute-done((bf16[14,128,128]{2,1,0:T(8,128)(2,1)S(1)}, bf16[14,128,128]{2,1,0:T(8,128)(2,1)S(1)}, u32[]{:S(2)}, u32[]{:S(2)}) %collective-permute-start.10) | collective-permute-done | bytes 458784 | tf_op jit(solution)/shard_map/down_chip/ppermute | solution.py:111
  42.4 1.3 %collective-permute-done.11.refs_1_.refs_9_ = bf16[14,128,128]{2,1,0:T(8,128)(2,1)S(1)} collective-permute-done((bf16[14,128,128]{2,1,0:T(8,128)(2,1)S(1)}, bf16[14,128,128]{2,1,0:T(8,128)(2,1)S(1)}, u32[]{:S(2)}, u32[]{:S(2)}) %collective-permute-start.11) | collective-permute-done | bytes 458784 | tf_op jit(solution)/shard_map/gate_y_core/ppermute | solution.py:107
  43.7 1.4 %shard_map.133 = (f32[28,128,128]{2,1,0:T(8,128)S(1)}, f32[28,128,128]{2,1,0:T(8,128)S(1)}) custom-call(s32[4]{0:T(128)S(1)} %pad_add_fusion.where_ref, s32[3]{0:T(128)S(1)} %bitcast.41, s32[2,112]{1,0:T(2,128)S(1)} %bitcast.68, f32[28,128,128]{2,1,0:T(8,128)S(1)} %get-tuple-element.69.acc_in, bf16[128,4096]{1,0:T(8,128)(2,1)S(1)} %copy-done, ...), custom_call_target="tpu_custom_call" | custom-call | flops 28 | bytes 28 | tf_op jit(solution)/shard_map/pallas_call | solution.py:30
  45.1 1.8 %shard_map.134 = (f32[28,128,128]{2,1,0:T(8,128)S(1)}, bf16[28,32,128]{2,1,0:T(8,128)(2,1)S(1)}, bf16[28,32,128]{2,1,0:T(8,128)(2,1)S(1)}, bf16[28,32,128]{2,1,0:T(8,128)(2,1)S(1)}, bf16[28,32,128]{2,1,0:T(8,128)(2,1)S(1)}) custom-call(s32[4]{0:T(128)S(1)} %pad_add_fusion.where_ref, s32[3]{0:T(128)S(1)} %bitcast.42, ...), custom_call_target="tpu_custom_call", output_to_operand_aliasing={{0}: (3, {})} | custom-call | flops 48 | bytes 48 | tf_op jit(solution)/shard_map/pallas_call | solution.py:30
  47.1 1.5 %collective-permute-start.19 = (bf16[14,128,128]{2,1,0:T(8,128)(2,1)S(1)}, bf16[14,128,128]{2,1,0:T(8,128)(2,1)S(1)}, u32[]{:S(2)}, u32[]{:S(2)}) collective-permute-start(bf16[14,128,128]{2,1,0:T(8,128)(2,1)S(1)} %collective-permute-done.10.refs_0_.refs_6_), channel_id=1, source_target_pairs={{0,16},{16,0},{1,17},{17,1},{2,18},{18,2},{3,19},{19,3},{4,20},{20... | collective-permute-start | bytes 1376264 | tf_op jit(solution)/shard_map/down_part/ppermute | solution.py:117
  49.3 0.9 collective-permute-done.15.refs_5_
  50.8 2.0 %shard_map.135 = bf16[28,128,128]{2,1,0:T(8,128)(2,1)S(1)} custom-call(s32[4]{0:T(128)S(1)} %pad_add_fusion.where_ref, s32[3]{0:T(128)S(1)} %bitcast.43, s32[2,112]{1,0:T(2,128)S(1)} %bitcast.61, bf16[28,32,128]{2,1,0:T(8,128)(2,1)S(1)} %get-tuple-element.110.refs_0_, bf16[28,32,128]{2,1,0:T(8,128)(2,1)S(1)} %get-tuple-element.111.refs_1_, ...), custom_call_target="tpu_custom_call" | custom-call | flops 28 | bytes 28 | tf_op jit(solution)/shard_map/pallas_call | solution.py:30
  52.8 1.5 %collective-permute-start.23 = (bf16[28,128,128]{2,1,0:T(8,128)(2,1)S(1)}, bf16[28,128,128]{2,1,0:T(8,128)(2,1)S(1)}, u32[]{:S(2)}, u32[]{:S(2)}) collective-permute-start(bf16[28,128,128]{2,1,0:T(8,128)(2,1)S(1)} %shard_map.135), channel_id=1, source_target_pairs={{0,8},{4,12},{8,0},{12,4},{1,9},{5,13},{9,1},{13,5},{2,10},{6,14},... | collective-permute-start | bytes 2752520 | tf_op jit(solution)/shard_map/down_grad_chip/ppermute | solution.py:111
  54.4 5.6 %collective-permute-done.19.refs_0_.refs_8_ = bf16[14,128,128]{2,1,0:T(8,128)(2,1)S(1)} collective-permute-done((bf16[14,128,128]{2,1,0:T(8,128)(2,1)S(1)}, bf16[14,128,128]{2,1,0:T(8,128)(2,1)S(1)}, u32[]{:S(2)}, u32[]{:S(2)}) %collective-permute-start.19) | collective-permute-done | bytes 458784 | tf_op jit(solution)/shard_map/down_part/ppermute | solution.py:117
  60.0 1.8 %shard_map.136.acc_in = f32[28,128,128]{2,1,0:T(8,128)S(1)} custom-call(s32[4]{0:T(128)S(1)} %pad_add_fusion.where_ref, s32[3]{0:T(128)S(1)} %bitcast.44, s32[2,112]{1,0:T(2,128)S(1)} %bitcast.62, f32[28,128,128]{2,1,0:T(8,128)S(1)} %shard_map.130.acc_in, bf16[128,4096]{1,0:T(8,128)(2,1)S(1)} %copy-done.1, ...), custom_call_target="tpu_custom_call", output_to_operand_aliasing={{}: (3, {})} | custom-call | flops 28 | bytes 28 | tf_op jit(solution)/shard_map/pallas_call | solution.py:30
  61.8 2.1 %shard_map.137 = (bf16[28,32,128]{2,1,0:T(8,128)(2,1)S(1)}, bf16[28,32,128]{2,1,0:T(8,128)(2,1)S(1)}, bf16[28,32,128]{2,1,0:T(8,128)(2,1)S(1)}, bf16[28,32,128]{...) custom-call(s32[4]{0:T(128)S(1)} %pad_add_fusion.where_ref, s32[3]{0:T(128)S(1)} %bitcast.45, s32[2,112]{1,0:T(2,128)S(1)} %bitcast.63, ...), custom_call_target="tpu_custom_call" | custom-call | flops 38 | bytes 38 | tf_op jit(solution)/shard_map/pallas_call | solution.py:30
  65.0 5.2 %shard_map.138 = (bf16[2,128,1024]{2,1,0:T(8,128)(2,1)S(1)}, bf16[2,128,1024]{2,1,0:T(8,128)(2,1)S(1)}) custom-call(s32[4]{0:T(128)S(1)} %pad_add_fusion.where_ref, s32[3]{0:T(128)S(1)} %bitcast.46, s32[2,112]{1,0:T(2,128)S(1)} %bitcast.64, bf16[28,32,128]{2,1,0:T(8,128)(2,1)S(1)} %get-tuple-element.110.refs_0_, ...), custom_call_target="tpu_custom_call" | custom-call | flops 112 | bytes 112 | tf_op jit(solution)/shard_map/pallas_call | solution.py:30
  70.8 0.8 shard_map.139
  71.6 3.5 %collective-permute-done.23 = bf16[28,128,128]{2,1,0:T(8,128)(2,1)S(1)} collective-permute-done((bf16[28,128,128]{2,1,0:T(8,128)(2,1)S(1)}, bf16[28,128,128]{2,1,0:T(8,128)(2,1)S(1)}, u32[]{:S(2)}, u32[]{:S(2)}) %collective-permute-start.23) | collective-permute-done | bytes 917536 | tf_op jit(solution)/shard_map/down_grad_chip/ppermute | solution.py:111
  75.1 1.7 %collective-permute-start.29 = (bf16[28,128,128]{2,1,0:T(8,128)(2,1)S(1)}, bf16[28,128,128]{2,1,0:T(8,128)(2,1)S(1)}, u32[]{:S(2)}, u32[]{:S(2)}) collective-permute-start(bf16[28,128,128]{2,1,0:T(8,128)(2,1)S(1)} %shard_map.139), channel_id=1, source_target_pairs={{0,8},{4,12},{8,0},{12,4},{1,9},{5,13},{9,1},{13,5},{2,10},{6,14},... | collective-permute-start | bytes 2752520 | tf_op jit(solution)/shard_map/gate_grad_chip/ppermute | solution.py:111
  76.8 3.5 %shard_map.140.refs_8_ = f32[32,128,128]{2,1,0:T(8,128)S(1)} custom-call(s32[4]{0:T(128)S(1)} %pad_add_fusion.where_ref, s32[3]{0:T(128)S(1)} %bitcast.48, s32[2,112]{1,0:T(2,128)S(1)} %bitcast.70, bf16[28,32,128]{2,1,0:T(8,128)(2,1)S(1)} %get-tuple-element.101.refs_2_.refs_0_, bf16[28,32,128]{2,1,0:T(8,128)(2,1)S(1)} %get-tuple-element.102.refs_3_.refs_1_, ...), custom_call_target="tpu_custom_call" | custom-call | flops 112 | bytes 112 | tf_op jit(solution)/shard_map/pallas_call | solution.py:30
  80.3 5.5 %shard_map.141 = (bf16[2,128,1024]{2,1,0:T(8,128)(2,1)S(1)}, bf16[2,128,1024]{2,1,0:T(8,128)(2,1)S(1)}, f32[32,128,128]{2,1,0:T(8,128)S(1)}) custom-call(s32[4]{0:T(128)S(1)} %pad_add_fusion.where_ref, s32[3]{0:T(128)S(1)} %bitcast.49, s32[2,112]{1,0:T(2,128)S(1)} %bitcast.57, ...), custom_call_target="tpu_custom_call", output_to_operand_aliasing={{2}: (11, {})} | custom-call | flops 112 | bytes 112 | tf_op jit(solution)/shard_map/pallas_call | solution.py:30
  85.7 2.5 %collective-permute-start.30 = (bf16[2,128,1024]{2,1,0:T(8,128)(2,1)S(1)}, bf16[2,128,1024]{2,1,0:T(8,128)(2,1)S(1)}, u32[]{:S(2)}, u32[]{:S(2)}) collective-permute-start(bf16[2,128,1024]{2,1,0:T(8,128)(2,1)S(1)} %get-tuple-element.107), channel_id=1, source_target_pairs={{0,1},{1,0},{2,3},{3,2},{4,5},{5,4},{6,7},{7,6},{8,9},{9,8},{10,11... | collective-permute-start | bytes 1572872 | tf_op jit(solution)/shard_map/token_group/ppermute | solution.py:121
  88.5 2.1 %collective-permute-start.28 = (bf16[1,128,1024]{2,1,0:T(8,128)(2,1)S(1)}, bf16[1,128,1024]{2,1,0:T(8,128)(2,1)S(1)}, u32[]{:S(2)}, u32[]{:S(2)}) collective-permute-start(bf16[1,128,1024]{2,1,0:T(8,128)(2,1)S(1)} %slice.21), channel_id=1, source_target_pairs={{0,2},{1,3},{2,0},{3,1},{4,6},{5,7},{6,4},{7,5},{8,10},{9,11},{10,... | collective-permute-start | bytes 786440 | tf_op jit(solution)/shard_map/out_group/ppermute | solution.py:121
  90.6 2.0 %shard_map.142 = bf16[28,128,128]{2,1,0:T(8,128)(2,1)S(1)} custom-call(s32[4]{0:T(128)S(1)} %pad_add_fusion.where_ref, s32[3]{0:T(128)S(1)} %bitcast.50, s32[2,112]{1,0:T(2,128)S(1)} %bitcast.65, bf16[28,32,128]{2,1,0:T(8,128)(2,1)S(1)} %get-tuple-element.110.refs_0_, bf16[28,32,128]{2,1,0:T(8,128)(2,1)S(1)} %get-tuple-element.111.refs_1_, ...), custom_call_target="tpu_custom_call" | custom-call | flops 28 | bytes 28 | tf_op jit(solution)/shard_map/pallas_call | solution.py:30
  92.6 1.2 %fusion = bf16[1,28,128,128]{3,2,1,0:T(8,128)(2,1)} fusion(bf16[28,128,128]{2,1,0:T(8,128)(2,1)S(1)} %collective-permute-done.23, bf16[28,128,128]{2,1,0:T(8,128)(2,1)S(1)} %shard_map.142), kind=kLoop, calls=%fused_computation.5 | loop fusion | flops 1835008 | bytes 2752512 | tf_op jit(solution)/shard_map/broadcast_in_dim | solution.py:357
  93.8 2.0 %shard_map.145 = bf16[28,128,128]{2,1,0:T(8,128)(2,1)S(1)} custom-call(s32[4]{0:T(128)S(1)} %pad_add_fusion.where_ref, s32[3]{0:T(128)S(1)} %bitcast.51, s32[2,112]{1,0:T(2,128)S(1)} %bitcast.58, bf16[128,4096]{1,0:T(8,128)(2,1)S(1)} %copy-done, bf16[128,4096]{1,0:T(8,128)(2,1)S(1)} %collective-permute-done.20.refs_1_, ...), custom_call_target="tpu_custom_call" | custom-call | flops 28 | bytes 28 | tf_op jit(solution)/shard_map/pallas_call | solution.py:30
  96.4 0.6 collective-permute-done.29
  96.9 8.1 %collective-permute-done.30 = bf16[2,128,1024]{2,1,0:T(8,128)(2,1)S(1)} collective-permute-done((bf16[2,128,1024]{2,1,0:T(8,128)(2,1)S(1)}, bf16[2,128,1024]{2,1,0:T(8,128)(2,1)S(1)}, u32[]{:S(2)}, u32[]{:S(2)}) %collective-permute-start.30) | collective-permute-done | bytes 524320 | tf_op jit(solution)/shard_map/token_group/ppermute | solution.py:121
  105.3 1.3 %collective-permute-start.31 = (bf16[1,128,1024]{2,1,0:T(8,128)(2,1)S(1)}, bf16[1,128,1024]{2,1,0:T(8,128)(2,1)S(1)}, u32[]{:S(2)}, u32[]{:S(2)}) collective-permute-start(bf16[1,128,1024]{2,1,0:T(8,128)(2,1)S(1)} %slice.23), channel_id=1, source_target_pairs={{0,2},{1,3},{2,0},{3,1},{4,6},{5,7},{6,4},{7,5},{8,10},{9,11},{10,... | collective-permute-start | bytes 786440 | tf_op jit(solution)/shard_map/token_group/ppermute | solution.py:121
  106.6 2.1 %shard_map.143 = bf16[28,128,128]{2,1,0:T(8,128)(2,1)S(1)} custom-call(s32[4]{0:T(128)S(1)} %pad_add_fusion.where_ref, s32[3]{0:T(128)S(1)} %bitcast.52, s32[2,112]{1,0:T(2,128)S(1)} %bitcast.71, bf16[128,4096]{1,0:T(8,128)(2,1)S(1)} %copy-done, bf16[128,4096]{1,0:T(8,128)(2,1)S(1)} %collective-permute-done.20.refs_1_, ...), custom_call_target="tpu_custom_call" | custom-call | flops 28 | bytes 28 | tf_op jit(solution)/shard_map/pallas_call | solution.py:30
  108.7 1.3 %fusion.1 = bf16[1,28,128,128]{3,2,1,0:T(8,128)(2,1)} fusion(bf16[28,128,128]{2,1,0:T(8,128)(2,1)S(1)} %collective-permute-done.29, bf16[28,128,128]{2,1,0:T(8,128)(2,1)S(1)} %shard_map.143), kind=kLoop, calls=%fused_computation.6 | loop fusion | flops 1835008 | bytes 2752512 | tf_op jit(solution)/shard_map/broadcast_in_dim | solution.py:357
  110.0 2.0 %shard_map.144 = bf16[28,128,128]{2,1,0:T(8,128)(2,1)S(1)} custom-call(s32[4]{0:T(128)S(1)} %pad_add_fusion.where_ref, s32[3]{0:T(128)S(1)} %bitcast.53, s32[2,112]{1,0:T(2,128)S(1)} %bitcast.59, bf16[128,4096]{1,0:T(8,128)(2,1)S(1)} %copy-done, bf16[128,4096]{1,0:T(8,128)(2,1)S(1)} %collective-permute-done.20.refs_1_, ...), custom_call_target="tpu_custom_call" | custom-call | flops 28 | bytes 28 | tf_op jit(solution)/shard_map/pallas_call | solution.py:30
  112.0 0.8 fusion.3
  112.7 5.8 %collective-permute-done.31 = bf16[1,128,1024]{2,1,0:T(8,128)(2,1)S(1)} collective-permute-done((bf16[1,128,1024]{2,1,0:T(8,128)(2,1)S(1)}, bf16[1,128,1024]{2,1,0:T(8,128)(2,1)S(1)}, u32[]{:S(2)}, u32[]{:S(2)}) %collective-permute-start.31) | collective-permute-done | bytes 262176 | tf_op jit(solution)/shard_map/token_group/ppermute | solution.py:121
  118.6 0.8 fusion.4
  119.3 1.2 %fusion.2 = bf16[1,28,128,128]{3,2,1,0:T(8,128)(2,1)} fusion(bf16[28,128,128]{2,1,0:T(8,128)(2,1)S(1)} %collective-permute-done.33, bf16[28,128,128]{2,1,0:T(8,128)(2,1)S(1)} %shard_map.144), kind=kLoop, calls=%fused_computation.7 | loop fusion | flops 1835008 | bytes 2752512 | tf_op jit(solution)/shard_map/broadcast_in_dim | solution.py:357
  (71 shorter events, 7.6 us)
Async XLA Ops:
  0.6 6.8 %copy-start = (bf16[128,4096]{1,0:T(8,128)(2,1)S(1)}, bf16[128,4096]{1,0:T(8,128)(2,1)}, u32[]{:S(2)}) copy-start(bf16[128,4096]{1,0:T(8,128)(2,1)} %refs_0_.5) | copy-start | bytes 3145732
  0.6 6.8 %copy-start.6 = (s32[3,1]{0,1:T(1,128)S(1)}, s32[3,1]{0,1:T(1,128)}, u32[]{:S(2)}) copy-start(s32[3,1]{0,1:T(1,128)} %param.17) | copy-start | bytes 40
  0.7 6.8 %copy-start.9 = (s32[2,1,112]{2,1,0:T(1,128)S(1)}, s32[2,1,112]{2,1,0:T(1,128)}, u32[]{:S(2)}) copy-start(s32[2,1,112]{2,1,0:T(1,128)} %param.14) | copy-start | bytes 2692
  0.7 16.7 %collective-permute-start.3 = (bf16[128,4096]{1,0:T(8,128)(2,1)}, bf16[128,4096]{1,0:T(8,128)(2,1)S(1)}, u32[]{:S(2)}, u32[]{:S(2)}) collective-permute-start(bf16[128,4096]{1,0:T(8,128)(2,1)} %refs_8_.3), channel_id=1, source_target_pairs={{0,4},{4,0},{8,12},{12,8},{1,5},{5,1},{9,13},{13,9},{2,6},{6,2},{1... | collective-permute-start | bytes 3145736 | tf_op jit(solution)/shard_map/cotangent_core/ppermute | solution.py:107
  1.2 6.2 %collective-permute-start.2 = (bf16[28,128,128]{2,1,0:T(8,128)(2,1)}, bf16[28,128,128]{2,1,0:T(8,128)(2,1)}, u32[]{:S(2)}, u32[]{:S(2)}) collective-permute-start(bf16[28,128,128]{2,1,0:T(8,128)(2,1)} %bitcast.27), channel_id=1, source_target_pairs={{0,4},{4,0},{8,12},{12,8},{1,5},{5,1},{9,13},{13,9},{2,6},{6,2},{1... | collective-permute-start | bytes 2752520 | tf_op jit(solution)/shard_map/gate_core/ppermute | solution.py:107
  1.3 19.4 %collective-permute-start = (bf16[28,128,128]{2,1,0:T(8,128)(2,1)}, bf16[28,128,128]{2,1,0:T(8,128)(2,1)S(1)}, u32[]{:S(2)}, u32[]{:S(2)}) collective-permute-start(bf16[28,128,128]{2,1,0:T(8,128)(2,1)} %bitcast.30), channel_id=1, source_target_pairs={{0,4},{4,0},{8,12},{12,8},{1,5},{5,1},{9,13},{13,9},{2,6},{6,2},{1... | collective-permute-start | bytes 2752520 | tf_op jit(solution)/shard_map/up_core/ppermute | solution.py:107
  3.5 13.9 %collective-permute-start.1 = (bf16[14,128,128]{2,1,0:T(8,128)(2,1)}, bf16[14,128,128]{2,1,0:T(8,128)(2,1)S(1)}, u32[]{:S(2)}, u32[]{:S(2)}) collective-permute-start(bf16[14,128,128]{2,1,0:T(8,128)(2,1)} %dynamic-slice_bitcast_fusion.1), channel_id=1, source_target_pairs={{0,8},{4,12},{8,0},{12,4},{1,9},{5,13},{9,1},{13,5},{2,10},{6,14},... | collective-permute-start | bytes 1376264 | tf_op jit(solution)/shard_map/gate_chip/ppermute | solution.py:111
  6.1 17.3 %collective-permute-start.6 = (bf16[28,128,128]{2,1,0:T(8,128)(2,1)}, bf16[28,128,128]{2,1,0:T(8,128)(2,1)}, u32[]{:S(2)}, u32[]{:S(2)}) collective-permute-start(bf16[28,128,128]{2,1,0:T(8,128)(2,1)} %bitcast.33), channel_id=1, source_target_pairs={{0,4},{4,0},{8,12},{12,8},{1,5},{5,1},{9,13},{13,9},{2,6},{6,2},{1... | collective-permute-start | bytes 2752520 | tf_op jit(solution)/shard_map/down_core/ppermute | solution.py:107
  7.4 1.2 copy-start.2
  8.6 12.1 %copy-start.4 = (bf16[1,28,128,128]{3,2,1,0:T(8,128)(2,1)S(1)}, bf16[1,28,128,128]{3,2,1,0:T(8,128)(2,1)}, u32[]{:S(2)}) copy-start(bf16[1,28,128,128]{3,2,1,0:T(8,128)(2,1)} %param.12) | copy-start | bytes 2752516
  8.6 12.1 %copy-start.7 = (s32[2,1,112]{2,1,0:T(1,128)S(1)}, s32[2,1,112]{2,1,0:T(1,128)}, u32[]{:S(2)}) copy-start(s32[2,1,112]{2,1,0:T(1,128)} %param.15) | copy-start | bytes 2692
  17.4 12.3 %collective-permute-start.4 = (bf16[14,128,128]{2,1,0:T(8,128)(2,1)S(1)}, bf16[14,128,128]{2,1,0:T(8,128)(2,1)S(1)}, u32[]{:S(2)}, u32[]{:S(2)}) collective-permute-start(bf16[14,128,128]{2,1,0:T(8,128)(2,1)S(1)} %dynamic-slice_bitcast_fusion.2), channel_id=1, source_target_pairs={{0,8},{4,12},{8,0},{12,4},{1,9},{5,13},{9,1},{13,5},{2,10},{6,14},... | collective-permute-start | bytes 1376264 | tf_op jit(solution)/shard_map/up_chip/ppermute | solution.py:111
  19.2 11.8 %collective-permute-start.5 = (bf16[14,128,128]{2,1,0:T(8,128)(2,1)S(1)}, bf16[14,128,128]{2,1,0:T(8,128)(2,1)S(1)}, u32[]{:S(2)}, u32[]{:S(2)}) collective-permute-start(bf16[14,128,128]{2,1,0:T(8,128)(2,1)S(1)} %collective-permute-done.1.refs_0_.refs_6_), channel_id=1, source_target_pairs={{0,16},{16,0},{1,17},{17,1},{2,18},{18,2},{3,19},{19,3},{4,20},{20... | collective-permute-start | bytes 1376264 | tf_op jit(solution)/shard_map/gate_part/ppermute | solution.py:117
  20.7 2.6 %copy-start.5 = (bf16[1,28,128,128]{3,2,1,0:T(8,128)(2,1)S(1)}, bf16[1,28,128,128]{3,2,1,0:T(8,128)(2,1)}, u32[]{:S(2)}) copy-start(bf16[1,28,128,128]{3,2,1,0:T(8,128)(2,1)} %param.13) | copy-start | bytes 2752516
  20.7 2.7 %copy-start.1 = (bf16[128,4096]{1,0:T(8,128)(2,1)S(1)}, bf16[128,4096]{1,0:T(8,128)(2,1)}, u32[]{:S(2)}) copy-start(bf16[128,4096]{1,0:T(8,128)(2,1)} %refs_8_.3) | copy-start | bytes 3145732
  20.7 2.7 %copy-start.8 = (s32[2,1,112]{2,1,0:T(1,128)S(1)}, s32[2,1,112]{2,1,0:T(1,128)}, u32[]{:S(2)}) copy-start(s32[2,1,112]{2,1,0:T(1,128)} %param.16) | copy-start | bytes 2692
  23.2 9.8 %collective-permute-start.7 = (bf16[14,128,128]{2,1,0:T(8,128)(2,1)S(1)}, bf16[14,128,128]{2,1,0:T(8,128)(2,1)S(1)}, u32[]{:S(2)}, u32[]{:S(2)}) collective-permute-start(bf16[14,128,128]{2,1,0:T(8,128)(2,1)S(1)} %collective-permute-done.1.refs_0_.refs_6_), channel_id=1, source_target_pairs={{0,4},{4,0},{8,12},{12,8},{1,5},{5,1},{9,13},{13,9},{2,6},{6,2},{1... | collective-permute-start | bytes 1376264 | tf_op jit(solution)/shard_map/gate_x_core/ppermute | solution.py:107
  31.0 10.9 %collective-permute-start.10 = (bf16[14,128,128]{2,1,0:T(8,128)(2,1)S(1)}, bf16[14,128,128]{2,1,0:T(8,128)(2,1)S(1)}, u32[]{:S(2)}, u32[]{:S(2)}) collective-permute-start(bf16[14,128,128]{2,1,0:T(8,128)(2,1)S(1)} %dynamic-slice_bitcast_fusion), channel_id=1, source_target_pairs={{0,8},{4,12},{8,0},{12,4},{1,9},{5,13},{9,1},{13,5},{2,10},{6,14},... | collective-permute-start | bytes 1376264 | tf_op jit(solution)/shard_map/down_chip/ppermute | solution.py:111
  31.4 10.8 %collective-permute-start.12 = (bf16[14,128,128]{2,1,0:T(8,128)(2,1)S(1)}, bf16[14,128,128]{2,1,0:T(8,128)(2,1)S(1)}, u32[]{:S(2)}, u32[]{:S(2)}) collective-permute-start(bf16[14,128,128]{2,1,0:T(8,128)(2,1)S(1)} %collective-permute-done.4.refs_2_.refs_0_.refs_3_), channel_id=1, source_target_pairs={{0,16},{16,0},{1,17},{17,1},{2,18},{18,2},{3,19},{19,3},{4,20},{20... | collective-permute-start | bytes 1376264 | tf_op jit(solution)/shard_map/up_part/ppermute | solution.py:117
  33.7 1.6 %collective-permute-start.8 = (bf16[7,128,128]{2,1,0:T(8,128)(2,1)S(1)}, bf16[7,128,128]{2,1,0:T(8,128)(2,1)S(1)}, u32[]{:S(2)}, u32[]{:S(2)}) collective-permute-start(bf16[7,128,128]{2,1,0:T(8,128)(2,1)S(1)} %get-tuple-element.67), channel_id=1, source_target_pairs={{0,4},{4,0},{8,12},{12,8},{1,5},{5,1},{9,13},{13,9},{2,6},{6,2},{1... | collective-permute-start | bytes 688136 | tf_op jit(solution)/shard_map/up_x_core/ppermute | solution.py:107
  33.7 1.8 %collective-permute-start.9 = (bf16[7,128,128]{2,1,0:T(8,128)(2,1)S(1)}, bf16[7,128,128]{2,1,0:T(8,128)(2,1)S(1)}, u32[]{:S(2)}, u32[]{:S(2)}) collective-permute-start(bf16[7,128,128]{2,1,0:T(8,128)(2,1)S(1)} %get-tuple-element.68), channel_id=1, source_target_pairs={{0,4},{4,0},{8,12},{12,8},{1,5},{5,1},{9,13},{13,9},{2,6},{6,2},{1... | collective-permute-start | bytes 688136 | tf_op jit(solution)/shard_map/up_x_core/ppermute | solution.py:107
  34.2 20.1 %collective-permute-start.20 = (bf16[128,4096]{1,0:T(8,128)(2,1)S(1)}, bf16[128,4096]{1,0:T(8,128)(2,1)S(1)}, u32[]{:S(2)}, u32[]{:S(2)}) collective-permute-start(bf16[128,4096]{1,0:T(8,128)(2,1)S(1)} %copy-done), channel_id=1, source_target_pairs={{0,4},{4,0},{8,12},{12,8},{1,5},{5,1},{9,13},{13,9},{2,6},{6,2},{1... | collective-permute-start | bytes 3145736 | tf_op jit(solution)/shard_map/tokens_core/ppermute | solution.py:107
  41.9 1.8 %collective-permute-start.11 = (bf16[14,128,128]{2,1,0:T(8,128)(2,1)S(1)}, bf16[14,128,128]{2,1,0:T(8,128)(2,1)S(1)}, u32[]{:S(2)}, u32[]{:S(2)}) collective-permute-start(bf16[14,128,128]{2,1,0:T(8,128)(2,1)S(1)} %collective-permute-done.5.refs_0_.refs_8_), channel_id=1, source_target_pairs={{0,4},{4,0},{8,12},{12,8},{1,5},{5,1},{9,13},{13,9},{2,6},{6,2},{1... | collective-permute-start | bytes 1376264 | tf_op jit(solution)/shard_map/gate_y_core/ppermute | solution.py:107
  42.2 2.9 %collective-permute-start.13 = (bf16[14,128,128]{2,1,0:T(8,128)(2,1)S(1)}, bf16[14,128,128]{2,1,0:T(8,128)(2,1)S(1)}, u32[]{:S(2)}, u32[]{:S(2)}) collective-permute-start(bf16[14,128,128]{2,1,0:T(8,128)(2,1)S(1)} %collective-permute-done.12.refs_0_.refs_6_), channel_id=1, source_target_pairs={{0,4},{4,0},{8,12},{12,8},{1,5},{5,1},{9,13},{13,9},{2,6},{6,2},{1... | collective-permute-start | bytes 1376264 | tf_op jit(solution)/shard_map/up_y_core/ppermute | solution.py:107
  46.9 2.2 %collective-permute-start.14 = (bf16[28,32,128]{2,1,0:T(8,128)(2,1)S(1)}, bf16[28,32,128]{2,1,0:T(8,128)(2,1)S(1)}, u32[]{:S(2)}, u32[]{:S(2)}) collective-permute-start(bf16[28,32,128]{2,1,0:T(8,128)(2,1)S(1)} %get-tuple-element.110.refs_0_), channel_id=1, source_target_pairs={{0,4},{4,0},{8,12},{12,8},{1,5},{5,1},{9,13},{13,9},{2,6},{6,2},{1... | collective-permute-start | bytes 688136 | tf_op jit(solution)/shard_map/hidden_core/ppermute | solution.py:107
  47.1 12.8 %collective-permute-start.19 = (bf16[14,128,128]{2,1,0:T(8,128)(2,1)S(1)}, bf16[14,128,128]{2,1,0:T(8,128)(2,1)S(1)}, u32[]{:S(2)}, u32[]{:S(2)}) collective-permute-start(bf16[14,128,128]{2,1,0:T(8,128)(2,1)S(1)} %collective-permute-done.10.refs_0_.refs_6_), channel_id=1, source_target_pairs={{0,16},{16,0},{1,17},{17,1},{2,18},{18,2},{3,19},{19,3},{4,20},{20... | collective-permute-start | bytes 1376264 | tf_op jit(solution)/shard_map/down_part/ppermute | solution.py:117
  48.7 1.5 %collective-permute-start.15 = (bf16[28,32,128]{2,1,0:T(8,128)(2,1)S(1)}, bf16[28,32,128]{2,1,0:T(8,128)(2,1)S(1)}, u32[]{:S(2)}, u32[]{:S(2)}) collective-permute-start(bf16[28,32,128]{2,1,0:T(8,128)(2,1)S(1)} %get-tuple-element.111.refs_1_), channel_id=1, source_target_pairs={{0,4},{4,0},{8,12},{12,8},{1,5},{5,1},{9,13},{13,9},{2,6},{6,2},{1... | collective-permute-start | bytes 688136 | tf_op jit(solution)/shard_map/hidden_core/ppermute | solution.py:107
  48.8 1.7 %collective-permute-start.16 = (bf16[28,32,128]{2,1,0:T(8,128)(2,1)S(1)}, bf16[28,32,128]{2,1,0:T(8,128)(2,1)S(1)}, u32[]{:S(2)}, u32[]{:S(2)}) collective-permute-start(bf16[28,32,128]{2,1,0:T(8,128)(2,1)S(1)} %get-tuple-element.112.refs_2_), channel_id=1, source_target_pairs={{0,4},{4,0},{8,12},{12,8},{1,5},{5,1},{9,13},{13,9},{2,6},{6,2},{1... | collective-permute-start | bytes 688136 | tf_op jit(solution)/shard_map/hidden_core/ppermute | solution.py:107
  49.2 1.6 %collective-permute-start.17 = (bf16[28,32,128]{2,1,0:T(8,128)(2,1)S(1)}, bf16[28,32,128]{2,1,0:T(8,128)(2,1)S(1)}, u32[]{:S(2)}, u32[]{:S(2)}) collective-permute-start(bf16[28,32,128]{2,1,0:T(8,128)(2,1)S(1)} %get-tuple-element.113.refs_3_), channel_id=1, source_target_pairs={{0,4},{4,0},{8,12},{12,8},{1,5},{5,1},{9,13},{13,9},{2,6},{6,2},{1... | collective-permute-start | bytes 688136 | tf_op jit(solution)/shard_map/hidden_core/ppermute | solution.py:107
  52.8 22.3 %collective-permute-start.23 = (bf16[28,128,128]{2,1,0:T(8,128)(2,1)S(1)}, bf16[28,128,128]{2,1,0:T(8,128)(2,1)S(1)}, u32[]{:S(2)}, u32[]{:S(2)}) collective-permute-start(bf16[28,128,128]{2,1,0:T(8,128)(2,1)S(1)} %shard_map.135), channel_id=1, source_target_pairs={{0,8},{4,12},{8,0},{12,4},{1,9},{5,13},{9,1},{13,5},{2,10},{6,14},... | collective-permute-start | bytes 2752520 | tf_op jit(solution)/shard_map/down_grad_chip/ppermute | solution.py:111
  54.3 5.6 %collective-permute-start.18 = (bf16[14,128,128]{2,1,0:T(8,128)(2,1)S(1)}, bf16[14,128,128]{2,1,0:T(8,128)(2,1)S(1)}, u32[]{:S(2)}, u32[]{:S(2)}) collective-permute-start(bf16[14,128,128]{2,1,0:T(8,128)(2,1)S(1)} %collective-permute-done.10.refs_0_.refs_6_), channel_id=1, source_target_pairs={{0,4},{4,0},{8,12},{12,8},{1,5},{5,1},{9,13},{13,9},{2,6},{6,2},{1... | collective-permute-start | bytes 1376264 | tf_op jit(solution)/shard_map/down_x_core/ppermute | solution.py:107
  59.9 1.8 %collective-permute-start.21 = (bf16[14,128,128]{2,1,0:T(8,128)(2,1)S(1)}, bf16[14,128,128]{2,1,0:T(8,128)(2,1)S(1)}, u32[]{:S(2)}, u32[]{:S(2)}) collective-permute-start(bf16[14,128,128]{2,1,0:T(8,128)(2,1)S(1)} %collective-permute-done.19.refs_0_.refs_8_), channel_id=1, source_target_pairs={{0,4},{4,0},{8,12},{12,8},{1,5},{5,1},{9,13},{13,9},{2,6},{6,2},{1... | collective-permute-start | bytes 1376264 | tf_op jit(solution)/shard_map/down_y_core/ppermute | solution.py:107
  63.8 6.4 %collective-permute-start.24 = (bf16[28,32,128]{2,1,0:T(8,128)(2,1)S(1)}, bf16[28,32,128]{2,1,0:T(8,128)(2,1)S(1)}, u32[]{:S(2)}, u32[]{:S(2)}) collective-permute-start(bf16[28,32,128]{2,1,0:T(8,128)(2,1)S(1)} %get-tuple-element.101.refs_2_.refs_0_), channel_id=1, source_target_pairs={{0,4},{4,0},{8,12},{12,8},{1,5},{5,1},{9,13},{13,9},{2,6},{6,2},{1... | collective-permute-start | bytes 688136 | tf_op jit(solution)/shard_map/grads_core/ppermute | solution.py:107
  64.4 5.9 %collective-permute-start.25 = (bf16[28,32,128]{2,1,0:T(8,128)(2,1)S(1)}, bf16[28,32,128]{2,1,0:T(8,128)(2,1)S(1)}, u32[]{:S(2)}, u32[]{:S(2)}) collective-permute-start(bf16[28,32,128]{2,1,0:T(8,128)(2,1)S(1)} %get-tuple-element.102.refs_3_.refs_1_), channel_id=1, source_target_pairs={{0,4},{4,0},{8,12},{12,8},{1,5},{5,1},{9,13},{13,9},{2,6},{6,2},{1... | collective-permute-start | bytes 688136 | tf_op jit(solution)/shard_map/grads_core/ppermute | solution.py:107
  64.5 6.3 %collective-permute-start.26 = (bf16[28,32,128]{2,1,0:T(8,128)(2,1)S(1)}, bf16[28,32,128]{2,1,0:T(8,128)(2,1)S(1)}, u32[]{:S(2)}, u32[]{:S(2)}) collective-permute-start(bf16[28,32,128]{2,1,0:T(8,128)(2,1)S(1)} %get-tuple-element.103.refs_4_.refs_2_), channel_id=1, source_target_pairs={{0,4},{4,0},{8,12},{12,8},{1,5},{5,1},{9,13},{13,9},{2,6},{6,2},{1... | collective-permute-start | bytes 688136 | tf_op jit(solution)/shard_map/grads_core/ppermute | solution.py:107
  64.9 5.9 %collective-permute-start.27 = (bf16[28,32,128]{2,1,0:T(8,128)(2,1)S(1)}, bf16[28,32,128]{2,1,0:T(8,128)(2,1)S(1)}, u32[]{:S(2)}, u32[]{:S(2)}) collective-permute-start(bf16[28,32,128]{2,1,0:T(8,128)(2,1)S(1)} %get-tuple-element.104.refs_5_.refs_3_), channel_id=1, source_target_pairs={{0,4},{4,0},{8,12},{12,8},{1,5},{5,1},{9,13},{13,9},{2,6},{6,2},{1... | collective-permute-start | bytes 688136 | tf_op jit(solution)/shard_map/grads_core/ppermute | solution.py:107
  70.2 18.1 %collective-permute-start.22 = (bf16[2,128,1024]{2,1,0:T(8,128)(2,1)S(1)}, bf16[2,128,1024]{2,1,0:T(8,128)(2,1)S(1)}, u32[]{:S(2)}, u32[]{:S(2)}) collective-permute-start(bf16[2,128,1024]{2,1,0:T(8,128)(2,1)S(1)} %get-tuple-element.95), channel_id=1, source_target_pairs={{0,1},{1,0},{2,3},{3,2},{4,5},{5,4},{6,7},{7,6},{8,9},{9,8},{10,11... | collective-permute-start | bytes 1572872 | tf_op jit(solution)/shard_map/out_group/ppermute | solution.py:121
  70.3 23.5 %collective-permute-start.32 = (bf16[28,128,128]{2,1,0:T(8,128)(2,1)S(1)}, bf16[28,128,128]{2,1,0:T(8,128)(2,1)S(1)}, u32[]{:S(2)}, u32[]{:S(2)}) collective-permute-start(bf16[28,128,128]{2,1,0:T(8,128)(2,1)S(1)} %get-tuple-element.105.refs_0_.refs_2_), channel_id=1, source_target_pairs={{0,4},{4,0},{8,12},{12,8},{1,5},{5,1},{9,13},{13,9},{2,6},{6,2},{1... | collective-permute-start | bytes 2752520 | tf_op jit(solution)/shard_map/grads_core/ppermute | solution.py:107
  70.8 6.0 %copy-start.3 = (bf16[1,28,128,128]{3,2,1,0:T(8,128)(2,1)S(1)}, bf16[1,28,128,128]{3,2,1,0:T(8,128)(2,1)}, u32[]{:S(2)}) copy-start(bf16[1,28,128,128]{3,2,1,0:T(8,128)(2,1)} %param.11) | copy-start | bytes 2752516
  75.1 21.9 %collective-permute-start.29 = (bf16[28,128,128]{2,1,0:T(8,128)(2,1)S(1)}, bf16[28,128,128]{2,1,0:T(8,128)(2,1)S(1)}, u32[]{:S(2)}, u32[]{:S(2)}) collective-permute-start(bf16[28,128,128]{2,1,0:T(8,128)(2,1)S(1)} %shard_map.139), channel_id=1, source_target_pairs={{0,8},{4,12},{8,0},{12,4},{1,9},{5,13},{9,1},{13,5},{2,10},{6,14},... | collective-permute-start | bytes 2752520 | tf_op jit(solution)/shard_map/gate_grad_chip/ppermute | solution.py:111
  85.7 19.3 %collective-permute-start.30 = (bf16[2,128,1024]{2,1,0:T(8,128)(2,1)S(1)}, bf16[2,128,1024]{2,1,0:T(8,128)(2,1)S(1)}, u32[]{:S(2)}, u32[]{:S(2)}) collective-permute-start(bf16[2,128,1024]{2,1,0:T(8,128)(2,1)S(1)} %get-tuple-element.107), channel_id=1, source_target_pairs={{0,1},{1,0},{2,3},{3,2},{4,5},{5,4},{6,7},{7,6},{8,9},{9,8},{10,11... | collective-permute-start | bytes 1572872 | tf_op jit(solution)/shard_map/token_group/ppermute | solution.py:121
  88.5 23.5 %collective-permute-start.28 = (bf16[1,128,1024]{2,1,0:T(8,128)(2,1)S(1)}, bf16[1,128,1024]{2,1,0:T(8,128)(2,1)S(1)}, u32[]{:S(2)}, u32[]{:S(2)}) collective-permute-start(bf16[1,128,1024]{2,1,0:T(8,128)(2,1)S(1)} %slice.21), channel_id=1, source_target_pairs={{0,2},{1,3},{2,0},{3,1},{4,6},{5,7},{6,4},{7,5},{8,10},{9,11},{10,... | collective-permute-start | bytes 786440 | tf_op jit(solution)/shard_map/out_group/ppermute | solution.py:121
  95.8 23.5 %collective-permute-start.33 = (bf16[28,128,128]{2,1,0:T(8,128)(2,1)S(1)}, bf16[28,128,128]{2,1,0:T(8,128)(2,1)S(1)}, u32[]{:S(2)}, u32[]{:S(2)}) collective-permute-start(bf16[28,128,128]{2,1,0:T(8,128)(2,1)S(1)} %shard_map.145), channel_id=1, source_target_pairs={{0,8},{4,12},{8,0},{12,4},{1,9},{5,13},{9,1},{13,5},{2,10},{6,14},... | collective-permute-start | bytes 2752520 | tf_op jit(solution)/shard_map/up_grad_chip/ppermute | solution.py:111
  105.3 13.3 %collective-permute-start.31 = (bf16[1,128,1024]{2,1,0:T(8,128)(2,1)S(1)}, bf16[1,128,1024]{2,1,0:T(8,128)(2,1)S(1)}, u32[]{:S(2)}, u32[]{:S(2)}) collective-permute-start(bf16[1,128,1024]{2,1,0:T(8,128)(2,1)S(1)} %slice.23), channel_id=1, source_target_pairs={{0,2},{1,3},{2,0},{3,1},{4,6},{5,7},{6,4},{7,5},{8,10},{9,11},{10,... | collective-permute-start | bytes 786440 | tf_op jit(solution)/shard_map/token_group/ppermute | solution.py:121

commit v6 on v4

--- a/solution.py
+++ b/solution.py
@@ -262,7 +262,7 @@
         y_u = after(y_u, *x_d)
         y_d = relayed("down", x_d, *y_u)
         direct.append(both("down_x", x_d))
-        relay = [both("gate_y", after(y_g, *x_d)), both("up_y", y_u)]
+        relay = [both("gate_y", after(y_g, acc_u)), both("up_y", y_u)]
 
         def gate_body(where_ref, counts_ref, tg, acc_in, x_ref, *refs):
             w_refs, silu_ref, slope_ref, acc = refs[:-3], *refs[-3:]

time: 121 us -> 121 us (level)
  waiting for transfers between devices: 48.7 us -> 41.8 us
  starting transfers between devices: 21 us -> 25.8 us
  Pallas kernels: 40.2 us -> 42.3 us
    ppermute x6, waiting for transfers between devices: 31.2 us -> 25.9 us  [chip_shift(): lax.ppermute(a, 'dp', [(i, (i // 2 + k) % chips * 2 + i % 2) for i in ran...]
    ppermute x4, starting transfers between devices: 4.06 us -> 8.75 us  [group_swap(): return lax.ppermute(a, 'tensor', [(i, i ^ bit) for i in range(groups)])]
    pallas_call x18, Pallas kernels: 40.2 us -> 42.3 us  [call(): pl.pallas_call(body, out_shape=outs, in_specs=[SMEM] * len(ints) + [VMEM]...]
    ppermute x4, waiting for transfers between devices: 9.34 us -> 8.06 us  [group_swap(): return lax.ppermute(a, 'tensor', [(i, i ^ bit) for i in range(groups)])]
  transfers between devices with their start and end apart: 32 -> 32, of which waited for: 17 -> 17; matrix products, arithmetic and copies ran while one was open for 6% -> 6% of each run, Pallas kernels for 33% -> 35%
where the time goes in v6:
time: 121 us
  Pallas kernels  42.3 us (35%)
  waiting for transfers between devices  41.8 us (35%)
  starting transfers between devices  25.8 us (21%)
  other arithmetic  5.75 us (5%)
  local copies, waits for them, and re-layouts  4.17 us (3%)
    pallas_call x18, Pallas kernels, call(): pl.pallas_call(body, out_shape=outs, in_specs=[SMEM] * len(ints) + [VMEM]...  42.3 us
    ppermute x6, waiting for transfers between devices, chip_shift(): lax.ppermute(a, 'dp', [(i, (i // 2 + k) % chips * 2 + i % 2) for i in ran...  25.9 us
    ppermute x4, starting transfers between devices, group_swap(): return lax.ppermute(a, 'tensor', [(i, i ^ bit) for i in range(groups)])  8.75 us
    ppermute x6, starting transfers between devices, chip_shift(): lax.ppermute(a, 'dp', [(i, (i // 2 + k) % chips * 2 + i % 2) for i in ran...  8.07 us
    ppermute x4, waiting for transfers between devices, group_swap(): return lax.ppermute(a, 'tensor', [(i, i ^ bit) for i in range(groups)])  8.06 us
    ppermute x3, waiting for transfers between devices, part_swap(): return lax.ppermute(a, 'parts', [(0, 1), (1, 0)])  5.53 us
    ppermute x3, starting transfers between devices, part_swap(): return lax.ppermute(a, 'parts', [(0, 1), (1, 0)])  4.56 us
    ppermute x19, starting transfers between devices, pair_swap(): return lax.ppermute(a, 'dp', [(i, i ^ 1) for i in range(dp)])  4.43 us
  transfers between devices with their start and end apart: 32, of which 17 were waited for; matrix products, arithmetic and copies ran while one was open for 6% of the time, Pallas kernels for 35%

profile of v6, /device:TPU:0, one launch (start us, length us, event | category | flops | bytes accessed | tf_op | source)
XLA Modules:
  0.0 120.8 jit_solution(8507554246487381250)
XLA Ops:
  1.7 1.8 %dynamic-slice_bitcast_fusion.1 = bf16[14,128,128]{2,1,0:T(8,128)(2,1)} fusion(bf16[1,28,128,128]{3,2,1,0:T(8,128)(2,1)} %param.11, s32[]{:T(128)S(6)} %select_n.18), kind=kLoop, calls=%fused_computation.11 | loop fusion | bytes 917508 | tf_op jit(solution)/shard_map/dynamic_slice | solution.py:153
  3.5 2.6 %collective-permute-start.1 = (bf16[14,128,128]{2,1,0:T(8,128)(2,1)}, bf16[14,128,128]{2,1,0:T(8,128)(2,1)S(1)}, u32[]{:S(2)}, u32[]{:S(2)}) collective-permute-start(bf16[14,128,128]{2,1,0:T(8,128)(2,1)} %dynamic-slice_bitcast_fusion.1), channel_id=1, source_target_pairs={{0,8},{4,12},{8,0},{12,4},{1,9},{5,13},{9,1},{13,5},{2,10},{6,14},... | collective-permute-start | bytes 1376264 | tf_op jit(solution)/shard_map/gate_chip/ppermute | solution.py:111
  6.3 1.1 dynamic-slice_bitcast_fusion.2
  7.4 1.2 copy-done.2
  8.6 2.7 %shard_map.129.acc_in = f32[28,128,128]{2,1,0:T(8,128)S(1)} custom-call(s32[4]{0:T(128)S(1)} %pad_add_fusion.where_ref, s32[3]{0:T(128)S(1)} %bitcast.36, s32[2,112]{1,0:T(2,128)S(1)} %bitcast.66, bf16[128,4096]{1,0:T(8,128)(2,1)S(1)} %copy-done, bf16[28,128,128]{2,1,0:T(8,128)(2,1)S(1)} %bitcast.28, bf16[28,128,128]{2,1,0:T(8,128)(2,1)} %collective-permute-done.2.refs_1_.refs_3_), custom_call_target="tpu_custom_call" | custom-call | flops 56 | bytes 56 | tf_op jit(solution)/shard_map/pallas_call | solution.py:30
  11.3 6.1 %collective-permute-done.1.refs_0_.refs_4_ = bf16[14,128,128]{2,1,0:T(8,128)(2,1)S(1)} collective-permute-done((bf16[14,128,128]{2,1,0:T(8,128)(2,1)}, bf16[14,128,128]{2,1,0:T(8,128)(2,1)S(1)}, u32[]{:S(2)}, u32[]{:S(2)}) %collective-permute-start.1) | collective-permute-done | bytes 458784 | tf_op jit(solution)/shard_map/gate_chip/ppermute | solution.py:111
  17.4 1.8 %collective-permute-start.4 = (bf16[14,128,128]{2,1,0:T(8,128)(2,1)S(1)}, bf16[14,128,128]{2,1,0:T(8,128)(2,1)S(1)}, u32[]{:S(2)}, u32[]{:S(2)}) collective-permute-start(bf16[14,128,128]{2,1,0:T(8,128)(2,1)S(1)} %dynamic-slice_bitcast_fusion.2), channel_id=1, source_target_pairs={{0,8},{4,12},{8,0},{12,4},{1,9},{5,13},{9,1},{13,5},{2,10},{6,14},... | collective-permute-start | bytes 1376264 | tf_op jit(solution)/shard_map/up_chip/ppermute | solution.py:111
  19.2 1.5 %collective-permute-start.5 = (bf16[14,128,128]{2,1,0:T(8,128)(2,1)S(1)}, bf16[14,128,128]{2,1,0:T(8,128)(2,1)S(1)}, u32[]{:S(2)}, u32[]{:S(2)}) collective-permute-start(bf16[14,128,128]{2,1,0:T(8,128)(2,1)S(1)} %collective-permute-done.1.refs_0_.refs_4_), channel_id=1, source_target_pairs={{0,16},{16,0},{1,17},{17,1},{2,18},{18,2},{3,19},{19,3},{4,20},{20... | collective-permute-start | bytes 1376264 | tf_op jit(solution)/shard_map/gate_part/ppermute | solution.py:117
  20.7 2.5 %shard_map.128.acc_in = f32[28,128,128]{2,1,0:T(8,128)S(1)} custom-call(s32[4]{0:T(128)S(1)} %pad_add_fusion.where_ref, s32[3]{0:T(128)S(1)} %bitcast.37, s32[2,112]{1,0:T(2,128)S(1)} %bitcast.54, bf16[128,4096]{1,0:T(8,128)(2,1)S(1)} %copy-done, bf16[28,128,128]{2,1,0:T(8,128)(2,1)S(1)} %bitcast.31, ...), custom_call_target="tpu_custom_call" | custom-call | flops 56 | bytes 56 | tf_op jit(solution)/shard_map/pallas_call | solution.py:30
  23.4 3.6 %shard_map.130.acc_in = f32[28,128,128]{2,1,0:T(8,128)S(1)} custom-call(s32[4]{0:T(128)S(1)} %pad_add_fusion.where_ref, s32[3]{0:T(128)S(1)} %bitcast.38, s32[2,112]{1,0:T(2,128)S(1)} %bitcast.60, bf16[128,4096]{1,0:T(8,128)(2,1)S(1)} %copy-done.1, bf16[28,128,128]{2,1,0:T(8,128)(2,1)S(1)} %bitcast.34, ...), custom_call_target="tpu_custom_call" | custom-call | flops 56 | bytes 56 | tf_op jit(solution)/shard_map/pallas_call | solution.py:30
  27.0 2.7 %collective-permute-done.4.refs_2_.refs_0_.refs_3_ = bf16[14,128,128]{2,1,0:T(8,128)(2,1)S(1)} collective-permute-done((bf16[14,128,128]{2,1,0:T(8,128)(2,1)S(1)}, bf16[14,128,128]{2,1,0:T(8,128)(2,1)S(1)}, u32[]{:S(2)}, u32[]{:S(2)}) %collective-permute-start.4) | collective-permute-done | bytes 458784 | tf_op jit(solution)/shard_map/up_chip/ppermute | solution.py:111
  29.7 1.3 %collective-permute-done.5.refs_0_.refs_6_ = bf16[14,128,128]{2,1,0:T(8,128)(2,1)S(1)} collective-permute-done((bf16[14,128,128]{2,1,0:T(8,128)(2,1)S(1)}, bf16[14,128,128]{2,1,0:T(8,128)(2,1)S(1)}, u32[]{:S(2)}, u32[]{:S(2)}) %collective-permute-start.5) | collective-permute-done | bytes 458784 | tf_op jit(solution)/shard_map/gate_part/ppermute | solution.py:117
  31.4 1.6 %collective-permute-start.11 = (bf16[14,128,128]{2,1,0:T(8,128)(2,1)S(1)}, bf16[14,128,128]{2,1,0:T(8,128)(2,1)S(1)}, u32[]{:S(2)}, u32[]{:S(2)}) collective-permute-start(bf16[14,128,128]{2,1,0:T(8,128)(2,1)S(1)} %collective-permute-done.4.refs_2_.refs_0_.refs_3_), channel_id=1, source_target_pairs={{0,16},{16,0},{1,17},{17,1},{2,18},{18,2},{3,19},{19,3},{4,20},{20... | collective-permute-start | bytes 1376264 | tf_op jit(solution)/shard_map/up_part/ppermute | solution.py:117
  33.0 0.6 shard_map.131
  34.2 1.0 collective-permute-done.8.refs_1_.refs_4_
  35.5 1.5 %shard_map.132.acc_in = f32[28,128,128]{2,1,0:T(8,128)S(1)} custom-call(s32[4]{0:T(128)S(1)} %pad_add_fusion.where_ref, s32[3]{0:T(128)S(1)} %bitcast.40, s32[2,112]{1,0:T(2,128)S(1)} %bitcast.55, f32[28,128,128]{2,1,0:T(8,128)S(1)} %shard_map.128.acc_in, bf16[128,4096]{1,0:T(8,128)(2,1)S(1)} %copy-done, ...), custom_call_target="tpu_custom_call", output_to_operand_aliasing={{}: (3, {})} | custom-call | flops 28 | bytes 28 | tf_op jit(solution)/shard_map/pallas_call | solution.py:30
  37.3 4.5 %collective-permute-done.12.refs_0_.refs_6_ = bf16[14,128,128]{2,1,0:T(8,128)(2,1)S(1)} collective-permute-done((bf16[14,128,128]{2,1,0:T(8,128)(2,1)S(1)}, bf16[14,128,128]{2,1,0:T(8,128)(2,1)S(1)}, u32[]{:S(2)}, u32[]{:S(2)}) %collective-permute-start.12) | collective-permute-done | bytes 458784 | tf_op jit(solution)/shard_map/down_chip/ppermute | solution.py:111
  42.2 1.4 %collective-permute-start.19 = (bf16[14,128,128]{2,1,0:T(8,128)(2,1)S(1)}, bf16[14,128,128]{2,1,0:T(8,128)(2,1)S(1)}, u32[]{:S(2)}, u32[]{:S(2)}) collective-permute-start(bf16[14,128,128]{2,1,0:T(8,128)(2,1)S(1)} %collective-permute-done.12.refs_0_.refs_6_), channel_id=1, source_target_pairs={{0,16},{16,0},{1,17},{17,1},{2,18},{18,2},{3,19},{19,3},{4,20},{20... | collective-permute-start | bytes 1376264 | tf_op jit(solution)/shard_map/down_part/ppermute | solution.py:117
  43.7 1.4 %shard_map.133 = (f32[28,128,128]{2,1,0:T(8,128)S(1)}, f32[28,128,128]{2,1,0:T(8,128)S(1)}) custom-call(s32[4]{0:T(128)S(1)} %pad_add_fusion.where_ref, s32[3]{0:T(128)S(1)} %bitcast.41, s32[2,112]{1,0:T(2,128)S(1)} %bitcast.68, f32[28,128,128]{2,1,0:T(8,128)S(1)} %get-tuple-element.66.acc_in, bf16[128,4096]{1,0:T(8,128)(2,1)S(1)} %copy-done, ...), custom_call_target="tpu_custom_call" | custom-call | flops 28 | bytes 28 | tf_op jit(solution)/shard_map/pallas_call | solution.py:30
  45.1 1.6 %shard_map.134 = (f32[28,128,128]{2,1,0:T(8,128)S(1)}, bf16[28,32,128]{2,1,0:T(8,128)(2,1)S(1)}, bf16[28,32,128]{2,1,0:T(8,128)(2,1)S(1)}, bf16[28,32,128]{2,1,0:T(8,128)(2,1)S(1)}, bf16[28,32,128]{2,1,0:T(8,128)(2,1)S(1)}) custom-call(s32[4]{0:T(128)S(1)} %pad_add_fusion.where_ref, s32[3]{0:T(128)S(1)} %bitcast.42, ...), custom_call_target="tpu_custom_call", output_to_operand_aliasing={{0}: (3, {})} | custom-call | flops 48 | bytes 48 | tf_op jit(solution)/shard_map/pallas_call | solution.py:30
  49.3 2.0 %shard_map.135 = bf16[28,128,128]{2,1,0:T(8,128)(2,1)S(1)} custom-call(s32[4]{0:T(128)S(1)} %pad_add_fusion.where_ref, s32[3]{0:T(128)S(1)} %bitcast.43, s32[2,112]{1,0:T(2,128)S(1)} %bitcast.61, bf16[28,32,128]{2,1,0:T(8,128)(2,1)S(1)} %get-tuple-element.104.refs_0_, bf16[28,32,128]{2,1,0:T(8,128)(2,1)S(1)} %get-tuple-element.105.refs_1_, ...), custom_call_target="tpu_custom_call" | custom-call | flops 28 | bytes 28 | tf_op jit(solution)/shard_map/pallas_call | solution.py:30
  51.3 3.9 %collective-permute-done.19.refs_0_.refs_8_ = bf16[14,128,128]{2,1,0:T(8,128)(2,1)S(1)} collective-permute-done((bf16[14,128,128]{2,1,0:T(8,128)(2,1)S(1)}, bf16[14,128,128]{2,1,0:T(8,128)(2,1)S(1)}, u32[]{:S(2)}, u32[]{:S(2)}) %collective-permute-start.19) | collective-permute-done | bytes 458784 | tf_op jit(solution)/shard_map/down_part/ppermute | solution.py:117
  55.2 1.4 %collective-permute-start.25 = (bf16[28,128,128]{2,1,0:T(8,128)(2,1)S(1)}, bf16[28,128,128]{2,1,0:T(8,128)(2,1)S(1)}, u32[]{:S(2)}, u32[]{:S(2)}) collective-permute-start(bf16[28,128,128]{2,1,0:T(8,128)(2,1)S(1)} %shard_map.135), channel_id=1, source_target_pairs={{0,8},{4,12},{8,0},{12,4},{1,9},{5,13},{9,1},{13,5},{2,10},{6,14},... | collective-permute-start | bytes 2752520 | tf_op jit(solution)/shard_map/down_grad_chip/ppermute | solution.py:111
  56.5 1.7 %shard_map.136.acc_in = f32[28,128,128]{2,1,0:T(8,128)S(1)} custom-call(s32[4]{0:T(128)S(1)} %pad_add_fusion.where_ref, s32[3]{0:T(128)S(1)} %bitcast.44, s32[2,112]{1,0:T(2,128)S(1)} %bitcast.62, f32[28,128,128]{2,1,0:T(8,128)S(1)} %shard_map.130.acc_in, bf16[128,4096]{1,0:T(8,128)(2,1)S(1)} %copy-done.1, ...), custom_call_target="tpu_custom_call", output_to_operand_aliasing={{}: (3, {})} | custom-call | flops 28 | bytes 28 | tf_op jit(solution)/shard_map/pallas_call | solution.py:30
  58.3 2.1 %shard_map.137 = (bf16[28,64,128]{2,1,0:T(8,128)(2,1)S(1)}, bf16[28,64,128]{2,1,0:T(8,128)(2,1)S(1)}, bf16[28,128,128]{2,1,0:T(8,128)(2,1)S(1)}) custom-call(s32[4]{0:T(128)S(1)} %pad_add_fusion.where_ref, s32[3]{0:T(128)S(1)} %bitcast.45, s32[2,112]{1,0:T(2,128)S(1)} %bitcast.63, f32[28,128,128]{2,1,0:T(8,128)S(1)} %shard_map.136.acc_in, ...), custom_call_target="tpu_custom_call" | custom-call | flops 38 | bytes 38 | tf_op jit(solution)/shard_map/pallas_call | solution.py:30
  61.2 5.2 %shard_map.138 = (bf16[2,128,1024]{2,1,0:T(8,128)(2,1)S(1)}, bf16[2,128,1024]{2,1,0:T(8,128)(2,1)S(1)}) custom-call(s32[4]{0:T(128)S(1)} %pad_add_fusion.where_ref, s32[3]{0:T(128)S(1)} %bitcast.46, s32[2,112]{1,0:T(2,128)S(1)} %bitcast.64, bf16[28,32,128]{2,1,0:T(8,128)(2,1)S(1)} %get-tuple-element.104.refs_0_, ...), custom_call_target="tpu_custom_call" | custom-call | flops 112 | bytes 112 | tf_op jit(solution)/shard_map/pallas_call | solution.py:30
  66.4 0.8 shard_map.139
  67.3 3.3 %collective-permute-start.24 = (bf16[2,128,1024]{2,1,0:T(8,128)(2,1)S(1)}, bf16[2,128,1024]{2,1,0:T(8,128)(2,1)S(1)}, u32[]{:S(2)}, u32[]{:S(2)}) collective-permute-start(bf16[2,128,1024]{2,1,0:T(8,128)(2,1)S(1)} %get-tuple-element.94), channel_id=1, source_target_pairs={{0,1},{1,0},{2,3},{3,2},{4,5},{5,4},{6,7},{7,6},{8,9},{9,8},{10,11... | collective-permute-start | bytes 1572872 | tf_op jit(solution)/shard_map/out_group/ppermute | solution.py:121
  70.6 3.2 %shard_map.140.refs_8_ = f32[32,128,128]{2,1,0:T(8,128)S(1)} custom-call(s32[4]{0:T(128)S(1)} %pad_add_fusion.where_ref, s32[3]{0:T(128)S(1)} %bitcast.48, s32[2,112]{1,0:T(2,128)S(1)} %bitcast.70, bf16[28,64,128]{2,1,0:T(8,128)(2,1)S(1)} %get-tuple-element.96.refs_2_.refs_0_, bf16[28,64,128]{2,1,0:T(8,128)(2,1)S(1)} %get-tuple-element.97.refs_3_.refs_1_, ...), custom_call_target="tpu_custom_call" | custom-call | flops 112 | bytes 112 | tf_op jit(solution)/shard_map/pallas_call | solution.py:30
  73.8 4.2 %collective-permute-done.25 = bf16[28,128,128]{2,1,0:T(8,128)(2,1)S(1)} collective-permute-done((bf16[28,128,128]{2,1,0:T(8,128)(2,1)S(1)}, bf16[28,128,128]{2,1,0:T(8,128)(2,1)S(1)}, u32[]{:S(2)}, u32[]{:S(2)}) %collective-permute-start.25) | collective-permute-done | bytes 917536 | tf_op jit(solution)/shard_map/down_grad_chip/ppermute | solution.py:111
  77.9 1.4 %collective-permute-start.27 = (bf16[28,128,128]{2,1,0:T(8,128)(2,1)S(1)}, bf16[28,128,128]{2,1,0:T(8,128)(2,1)S(1)}, u32[]{:S(2)}, u32[]{:S(2)}) collective-permute-start(bf16[28,128,128]{2,1,0:T(8,128)(2,1)S(1)} %shard_map.139), channel_id=1, source_target_pairs={{0,8},{4,12},{8,0},{12,4},{1,9},{5,13},{9,1},{13,5},{2,10},{6,14},... | collective-permute-start | bytes 2752520 | tf_op jit(solution)/shard_map/gate_grad_chip/ppermute | solution.py:111
  79.3 5.2 %shard_map.141 = (bf16[2,128,1024]{2,1,0:T(8,128)(2,1)S(1)}, bf16[2,128,1024]{2,1,0:T(8,128)(2,1)S(1)}, f32[32,128,128]{2,1,0:T(8,128)S(1)}) custom-call(s32[4]{0:T(128)S(1)} %pad_add_fusion.where_ref, s32[3]{0:T(128)S(1)} %bitcast.49, s32[2,112]{1,0:T(2,128)S(1)} %bitcast.57, ...), custom_call_target="tpu_custom_call", output_to_operand_aliasing={{2}: (11, {})} | custom-call | flops 112 | bytes 112 | tf_op jit(solution)/shard_map/pallas_call | solution.py:30
  84.6 2.0 %shard_map.145 = bf16[28,128,128]{2,1,0:T(8,128)(2,1)S(1)} custom-call(s32[4]{0:T(128)S(1)} %pad_add_fusion.where_ref, s32[3]{0:T(128)S(1)} %bitcast.50, s32[2,112]{1,0:T(2,128)S(1)} %bitcast.58, bf16[128,4096]{1,0:T(8,128)(2,1)S(1)} %copy-done, bf16[128,4096]{1,0:T(8,128)(2,1)S(1)} %collective-permute-done.21.refs_1_, ...), custom_call_target="tpu_custom_call" | custom-call | flops 28 | bytes 28 | tf_op jit(solution)/shard_map/pallas_call | solution.py:30
  86.8 3.9 %collective-permute-start.26 = (bf16[1,128,1024]{2,1,0:T(8,128)(2,1)S(1)}, bf16[1,128,1024]{2,1,0:T(8,128)(2,1)S(1)}, u32[]{:S(2)}, u32[]{:S(2)}) collective-permute-start(bf16[1,128,1024]{2,1,0:T(8,128)(2,1)S(1)} %slice.21), channel_id=1, source_target_pairs={{0,2},{1,3},{2,0},{3,1},{4,6},{5,7},{6,4},{7,5},{8,10},{9,11},{10,... | collective-permute-start | bytes 786440 | tf_op jit(solution)/shard_map/out_group/ppermute | solution.py:121
  90.8 0.6 collective-permute-start.31
  91.3 2.0 %shard_map.142 = bf16[28,128,128]{2,1,0:T(8,128)(2,1)S(1)} custom-call(s32[4]{0:T(128)S(1)} %pad_add_fusion.where_ref, s32[3]{0:T(128)S(1)} %bitcast.51, s32[2,112]{1,0:T(2,128)S(1)} %bitcast.65, bf16[28,32,128]{2,1,0:T(8,128)(2,1)S(1)} %get-tuple-element.104.refs_0_, bf16[28,32,128]{2,1,0:T(8,128)(2,1)S(1)} %get-tuple-element.105.refs_1_, ...), custom_call_target="tpu_custom_call" | custom-call | flops 28 | bytes 28 | tf_op jit(solution)/shard_map/pallas_call | solution.py:30
  93.3 1.2 %fusion = bf16[1,28,128,128]{3,2,1,0:T(8,128)(2,1)} fusion(bf16[28,128,128]{2,1,0:T(8,128)(2,1)S(1)} %collective-permute-done.25, bf16[28,128,128]{2,1,0:T(8,128)(2,1)S(1)} %shard_map.142), kind=kLoop, calls=%fused_computation.5 | loop fusion | flops 1835008 | bytes 2752512 | tf_op jit(solution)/shard_map/broadcast_in_dim | solution.py:357
  94.6 6.6 %collective-permute-done.27 = bf16[28,128,128]{2,1,0:T(8,128)(2,1)S(1)} collective-permute-done((bf16[28,128,128]{2,1,0:T(8,128)(2,1)S(1)}, bf16[28,128,128]{2,1,0:T(8,128)(2,1)S(1)}, u32[]{:S(2)}, u32[]{:S(2)}) %collective-permute-start.27) | collective-permute-done | bytes 917536 | tf_op jit(solution)/shard_map/gate_grad_chip/ppermute | solution.py:111
  101.2 2.3 %collective-permute-done.28 = bf16[2,128,1024]{2,1,0:T(8,128)(2,1)S(1)} collective-permute-done((bf16[2,128,1024]{2,1,0:T(8,128)(2,1)S(1)}, bf16[2,128,1024]{2,1,0:T(8,128)(2,1)S(1)}, u32[]{:S(2)}, u32[]{:S(2)}) %collective-permute-start.28) | collective-permute-done | bytes 524320 | tf_op jit(solution)/shard_map/token_group/ppermute | solution.py:121
  103.7 1.5 %collective-permute-start.29 = (bf16[1,128,1024]{2,1,0:T(8,128)(2,1)S(1)}, bf16[1,128,1024]{2,1,0:T(8,128)(2,1)S(1)}, u32[]{:S(2)}, u32[]{:S(2)}) collective-permute-start(bf16[1,128,1024]{2,1,0:T(8,128)(2,1)S(1)} %slice.23), channel_id=1, source_target_pairs={{0,2},{1,3},{2,0},{3,1},{4,6},{5,7},{6,4},{7,5},{8,10},{9,11},{10,... | collective-permute-start | bytes 786440 | tf_op jit(solution)/shard_map/token_group/ppermute | solution.py:121
  105.2 2.0 %shard_map.143 = bf16[28,128,128]{2,1,0:T(8,128)(2,1)S(1)} custom-call(s32[4]{0:T(128)S(1)} %pad_add_fusion.where_ref, s32[3]{0:T(128)S(1)} %bitcast.52, s32[2,112]{1,0:T(2,128)S(1)} %bitcast.71, bf16[128,4096]{1,0:T(8,128)(2,1)S(1)} %copy-done, bf16[128,4096]{1,0:T(8,128)(2,1)S(1)} %collective-permute-done.21.refs_1_, ...), custom_call_target="tpu_custom_call" | custom-call | flops 28 | bytes 28 | tf_op jit(solution)/shard_map/pallas_call | solution.py:30
  107.2 1.3 %fusion.1 = bf16[1,28,128,128]{3,2,1,0:T(8,128)(2,1)} fusion(bf16[28,128,128]{2,1,0:T(8,128)(2,1)S(1)} %collective-permute-done.27, bf16[28,128,128]{2,1,0:T(8,128)(2,1)S(1)} %shard_map.143), kind=kLoop, calls=%fused_computation.6 | loop fusion | flops 1835008 | bytes 2752512 | tf_op jit(solution)/shard_map/broadcast_in_dim | solution.py:357
  108.4 2.0 %shard_map.144 = bf16[28,128,128]{2,1,0:T(8,128)(2,1)S(1)} custom-call(s32[4]{0:T(128)S(1)} %pad_add_fusion.where_ref, s32[3]{0:T(128)S(1)} %bitcast.53, s32[2,112]{1,0:T(2,128)S(1)} %bitcast.59, bf16[128,4096]{1,0:T(8,128)(2,1)S(1)} %copy-done, bf16[128,4096]{1,0:T(8,128)(2,1)S(1)} %collective-permute-done.21.refs_1_, ...), custom_call_target="tpu_custom_call" | custom-call | flops 28 | bytes 28 | tf_op jit(solution)/shard_map/pallas_call | solution.py:30
  110.4 0.8 fusion.3
  111.2 5.8 %collective-permute-done.29 = bf16[1,128,1024]{2,1,0:T(8,128)(2,1)S(1)} collective-permute-done((bf16[1,128,1024]{2,1,0:T(8,128)(2,1)S(1)}, bf16[1,128,1024]{2,1,0:T(8,128)(2,1)S(1)}, u32[]{:S(2)}, u32[]{:S(2)}) %collective-permute-start.29) | collective-permute-done | bytes 262176 | tf_op jit(solution)/shard_map/token_group/ppermute | solution.py:121
  117.0 0.8 fusion.4
  117.7 1.8 %collective-permute-done.31 = bf16[28,128,128]{2,1,0:T(8,128)(2,1)S(1)} collective-permute-done((bf16[28,128,128]{2,1,0:T(8,128)(2,1)S(1)}, bf16[28,128,128]{2,1,0:T(8,128)(2,1)S(1)}, u32[]{:S(2)}, u32[]{:S(2)}) %collective-permute-start.31) | collective-permute-done | bytes 917536 | tf_op jit(solution)/shard_map/up_grad_chip/ppermute | solution.py:111
  119.6 1.2 %fusion.2 = bf16[1,28,128,128]{3,2,1,0:T(8,128)(2,1)} fusion(bf16[28,128,128]{2,1,0:T(8,128)(2,1)S(1)} %collective-permute-done.31, bf16[28,128,128]{2,1,0:T(8,128)(2,1)S(1)} %shard_map.144), kind=kLoop, calls=%fused_computation.7 | loop fusion | flops 1835008 | bytes 2752512 | tf_op jit(solution)/shard_map/broadcast_in_dim | solution.py:357
  (67 shorter events, 7.3 us)
Async XLA Ops:
  0.6 6.8 %copy-start.6 = (s32[3,1]{0,1:T(1,128)S(1)}, s32[3,1]{0,1:T(1,128)}, u32[]{:S(2)}) copy-start(s32[3,1]{0,1:T(1,128)} %param.17) | copy-start | bytes 40
  0.6 6.8 %copy-start = (bf16[128,4096]{1,0:T(8,128)(2,1)S(1)}, bf16[128,4096]{1,0:T(8,128)(2,1)}, u32[]{:S(2)}) copy-start(bf16[128,4096]{1,0:T(8,128)(2,1)} %refs_0_.5) | copy-start | bytes 3145732
  0.7 6.8 %copy-start.9 = (s32[2,1,112]{2,1,0:T(1,128)S(1)}, s32[2,1,112]{2,1,0:T(1,128)}, u32[]{:S(2)}) copy-start(s32[2,1,112]{2,1,0:T(1,128)} %param.14) | copy-start | bytes 2692
  0.7 16.7 %collective-permute-start.3 = (bf16[128,4096]{1,0:T(8,128)(2,1)}, bf16[128,4096]{1,0:T(8,128)(2,1)S(1)}, u32[]{:S(2)}, u32[]{:S(2)}) collective-permute-start(bf16[128,4096]{1,0:T(8,128)(2,1)} %refs_8_.3), channel_id=1, source_target_pairs={{0,4},{4,0},{8,12},{12,8},{1,5},{5,1},{9,13},{13,9},{2,6},{6,2},{1... | collective-permute-start | bytes 3145736 | tf_op jit(solution)/shard_map/cotangent_core/ppermute | solution.py:107
  1.2 6.2 %collective-permute-start.2 = (bf16[28,128,128]{2,1,0:T(8,128)(2,1)}, bf16[28,128,128]{2,1,0:T(8,128)(2,1)}, u32[]{:S(2)}, u32[]{:S(2)}) collective-permute-start(bf16[28,128,128]{2,1,0:T(8,128)(2,1)} %bitcast.27), channel_id=1, source_target_pairs={{0,4},{4,0},{8,12},{12,8},{1,5},{5,1},{9,13},{13,9},{2,6},{6,2},{1... | collective-permute-start | bytes 2752520 | tf_op jit(solution)/shard_map/gate_core/ppermute | solution.py:107
  1.3 19.4 %collective-permute-start = (bf16[28,128,128]{2,1,0:T(8,128)(2,1)}, bf16[28,128,128]{2,1,0:T(8,128)(2,1)S(1)}, u32[]{:S(2)}, u32[]{:S(2)}) collective-permute-start(bf16[28,128,128]{2,1,0:T(8,128)(2,1)} %bitcast.30), channel_id=1, source_target_pairs={{0,4},{4,0},{8,12},{12,8},{1,5},{5,1},{9,13},{13,9},{2,6},{6,2},{1... | collective-permute-start | bytes 2752520 | tf_op jit(solution)/shard_map/up_core/ppermute | solution.py:107
  3.5 13.9 %collective-permute-start.1 = (bf16[14,128,128]{2,1,0:T(8,128)(2,1)}, bf16[14,128,128]{2,1,0:T(8,128)(2,1)S(1)}, u32[]{:S(2)}, u32[]{:S(2)}) collective-permute-start(bf16[14,128,128]{2,1,0:T(8,128)(2,1)} %dynamic-slice_bitcast_fusion.1), channel_id=1, source_target_pairs={{0,8},{4,12},{8,0},{12,4},{1,9},{5,13},{9,1},{13,5},{2,10},{6,14},... | collective-permute-start | bytes 1376264 | tf_op jit(solution)/shard_map/gate_chip/ppermute | solution.py:111
  6.1 17.3 %collective-permute-start.6 = (bf16[28,128,128]{2,1,0:T(8,128)(2,1)}, bf16[28,128,128]{2,1,0:T(8,128)(2,1)}, u32[]{:S(2)}, u32[]{:S(2)}) collective-permute-start(bf16[28,128,128]{2,1,0:T(8,128)(2,1)} %bitcast.33), channel_id=1, source_target_pairs={{0,4},{4,0},{8,12},{12,8},{1,5},{5,1},{9,13},{13,9},{2,6},{6,2},{1... | collective-permute-start | bytes 2752520 | tf_op jit(solution)/shard_map/down_core/ppermute | solution.py:107
  7.4 1.2 copy-start.2
  8.6 12.1 %copy-start.4 = (bf16[1,28,128,128]{3,2,1,0:T(8,128)(2,1)S(1)}, bf16[1,28,128,128]{3,2,1,0:T(8,128)(2,1)}, u32[]{:S(2)}) copy-start(bf16[1,28,128,128]{3,2,1,0:T(8,128)(2,1)} %param.12) | copy-start | bytes 2752516
  8.6 12.1 %copy-start.7 = (s32[2,1,112]{2,1,0:T(1,128)S(1)}, s32[2,1,112]{2,1,0:T(1,128)}, u32[]{:S(2)}) copy-start(s32[2,1,112]{2,1,0:T(1,128)} %param.15) | copy-start | bytes 2692
  17.4 12.3 %collective-permute-start.4 = (bf16[14,128,128]{2,1,0:T(8,128)(2,1)S(1)}, bf16[14,128,128]{2,1,0:T(8,128)(2,1)S(1)}, u32[]{:S(2)}, u32[]{:S(2)}) collective-permute-start(bf16[14,128,128]{2,1,0:T(8,128)(2,1)S(1)} %dynamic-slice_bitcast_fusion.2), channel_id=1, source_target_pairs={{0,8},{4,12},{8,0},{12,4},{1,9},{5,13},{9,1},{13,5},{2,10},{6,14},... | collective-permute-start | bytes 1376264 | tf_op jit(solution)/shard_map/up_chip/ppermute | solution.py:111
  19.2 11.8 %collective-permute-start.5 = (bf16[14,128,128]{2,1,0:T(8,128)(2,1)S(1)}, bf16[14,128,128]{2,1,0:T(8,128)(2,1)S(1)}, u32[]{:S(2)}, u32[]{:S(2)}) collective-permute-start(bf16[14,128,128]{2,1,0:T(8,128)(2,1)S(1)} %collective-permute-done.1.refs_0_.refs_4_), channel_id=1, source_target_pairs={{0,16},{16,0},{1,17},{17,1},{2,18},{18,2},{3,19},{19,3},{4,20},{20... | collective-permute-start | bytes 1376264 | tf_op jit(solution)/shard_map/gate_part/ppermute | solution.py:117
  20.7 2.6 %copy-start.5 = (bf16[1,28,128,128]{3,2,1,0:T(8,128)(2,1)S(1)}, bf16[1,28,128,128]{3,2,1,0:T(8,128)(2,1)}, u32[]{:S(2)}) copy-start(bf16[1,28,128,128]{3,2,1,0:T(8,128)(2,1)} %param.13) | copy-start | bytes 2752516
  20.7 2.7 %copy-start.1 = (bf16[128,4096]{1,0:T(8,128)(2,1)S(1)}, bf16[128,4096]{1,0:T(8,128)(2,1)}, u32[]{:S(2)}) copy-start(bf16[128,4096]{1,0:T(8,128)(2,1)} %refs_8_.3) | copy-start | bytes 3145732
  20.7 2.7 %copy-start.8 = (s32[2,1,112]{2,1,0:T(1,128)S(1)}, s32[2,1,112]{2,1,0:T(1,128)}, u32[]{:S(2)}) copy-start(s32[2,1,112]{2,1,0:T(1,128)} %param.16) | copy-start | bytes 2692
  23.2 9.8 %collective-permute-start.7 = (bf16[14,128,128]{2,1,0:T(8,128)(2,1)S(1)}, bf16[14,128,128]{2,1,0:T(8,128)(2,1)S(1)}, u32[]{:S(2)}, u32[]{:S(2)}) collective-permute-start(bf16[14,128,128]{2,1,0:T(8,128)(2,1)S(1)} %collective-permute-done.1.refs_0_.refs_4_), channel_id=1, source_target_pairs={{0,4},{4,0},{8,12},{12,8},{1,5},{5,1},{9,13},{13,9},{2,6},{6,2},{1... | collective-permute-start | bytes 1376264 | tf_op jit(solution)/shard_map/gate_x_core/ppermute | solution.py:107
  31.0 10.9 %collective-permute-start.12 = (bf16[14,128,128]{2,1,0:T(8,128)(2,1)S(1)}, bf16[14,128,128]{2,1,0:T(8,128)(2,1)S(1)}, u32[]{:S(2)}, u32[]{:S(2)}) collective-permute-start(bf16[14,128,128]{2,1,0:T(8,128)(2,1)S(1)} %dynamic-slice_bitcast_fusion), channel_id=1, source_target_pairs={{0,8},{4,12},{8,0},{12,4},{1,9},{5,13},{9,1},{13,5},{2,10},{6,14},... | collective-permute-start | bytes 1376264 | tf_op jit(solution)/shard_map/down_chip/ppermute | solution.py:111
  31.4 10.8 %collective-permute-start.11 = (bf16[14,128,128]{2,1,0:T(8,128)(2,1)S(1)}, bf16[14,128,128]{2,1,0:T(8,128)(2,1)S(1)}, u32[]{:S(2)}, u32[]{:S(2)}) collective-permute-start(bf16[14,128,128]{2,1,0:T(8,128)(2,1)S(1)} %collective-permute-done.4.refs_2_.refs_0_.refs_3_), channel_id=1, source_target_pairs={{0,16},{16,0},{1,17},{17,1},{2,18},{18,2},{3,19},{19,3},{4,20},{20... | collective-permute-start | bytes 1376264 | tf_op jit(solution)/shard_map/up_part/ppermute | solution.py:117
  33.7 1.6 %collective-permute-start.8 = (bf16[7,128,128]{2,1,0:T(8,128)(2,1)S(1)}, bf16[7,128,128]{2,1,0:T(8,128)(2,1)S(1)}, u32[]{:S(2)}, u32[]{:S(2)}) collective-permute-start(bf16[7,128,128]{2,1,0:T(8,128)(2,1)S(1)} %get-tuple-element.64), channel_id=1, source_target_pairs={{0,4},{4,0},{8,12},{12,8},{1,5},{5,1},{9,13},{13,9},{2,6},{6,2},{1... | collective-permute-start | bytes 688136 | tf_op jit(solution)/shard_map/up_x_core/ppermute | solution.py:107
  33.7 1.8 %collective-permute-start.9 = (bf16[7,128,128]{2,1,0:T(8,128)(2,1)S(1)}, bf16[7,128,128]{2,1,0:T(8,128)(2,1)S(1)}, u32[]{:S(2)}, u32[]{:S(2)}) collective-permute-start(bf16[7,128,128]{2,1,0:T(8,128)(2,1)S(1)} %get-tuple-element.65), channel_id=1, source_target_pairs={{0,4},{4,0},{8,12},{12,8},{1,5},{5,1},{9,13},{13,9},{2,6},{6,2},{1... | collective-permute-start | bytes 688136 | tf_op jit(solution)/shard_map/up_x_core/ppermute | solution.py:107
  37.1 6.6 %collective-permute-start.10 = (bf16[14,128,128]{2,1,0:T(8,128)(2,1)S(1)}, bf16[14,128,128]{2,1,0:T(8,128)(2,1)S(1)}, u32[]{:S(2)}, u32[]{:S(2)}) collective-permute-start(bf16[14,128,128]{2,1,0:T(8,128)(2,1)S(1)} %collective-permute-done.5.refs_0_.refs_6_), channel_id=1, source_target_pairs={{0,4},{4,0},{8,12},{12,8},{1,5},{5,1},{9,13},{13,9},{2,6},{6,2},{1... | collective-permute-start | bytes 1376264 | tf_op jit(solution)/shard_map/gate_y_core/ppermute | solution.py:107
  42.2 2.9 %collective-permute-start.13 = (bf16[14,128,128]{2,1,0:T(8,128)(2,1)S(1)}, bf16[14,128,128]{2,1,0:T(8,128)(2,1)S(1)}, u32[]{:S(2)}, u32[]{:S(2)}) collective-permute-start(bf16[14,128,128]{2,1,0:T(8,128)(2,1)S(1)} %collective-permute-done.11.refs_0_.refs_6_), channel_id=1, source_target_pairs={{0,4},{4,0},{8,12},{12,8},{1,5},{5,1},{9,13},{13,9},{2,6},{6,2},{1... | collective-permute-start | bytes 1376264 | tf_op jit(solution)/shard_map/up_y_core/ppermute | solution.py:107
  42.2 12.9 %collective-permute-start.19 = (bf16[14,128,128]{2,1,0:T(8,128)(2,1)S(1)}, bf16[14,128,128]{2,1,0:T(8,128)(2,1)S(1)}, u32[]{:S(2)}, u32[]{:S(2)}) collective-permute-start(bf16[14,128,128]{2,1,0:T(8,128)(2,1)S(1)} %collective-permute-done.12.refs_0_.refs_6_), channel_id=1, source_target_pairs={{0,16},{16,0},{1,17},{17,1},{2,18},{18,2},{3,19},{19,3},{4,20},{20... | collective-permute-start | bytes 1376264 | tf_op jit(solution)/shard_map/down_part/ppermute | solution.py:117
  46.8 1.6 %collective-permute-start.14 = (bf16[28,32,128]{2,1,0:T(8,128)(2,1)S(1)}, bf16[28,32,128]{2,1,0:T(8,128)(2,1)S(1)}, u32[]{:S(2)}, u32[]{:S(2)}) collective-permute-start(bf16[28,32,128]{2,1,0:T(8,128)(2,1)S(1)} %get-tuple-element.104.refs_0_), channel_id=1, source_target_pairs={{0,4},{4,0},{8,12},{12,8},{1,5},{5,1},{9,13},{13,9},{2,6},{6,2},{1... | collective-permute-start | bytes 688136 | tf_op jit(solution)/shard_map/hidden_core/ppermute | solution.py:107
  47.1 1.6 %collective-permute-start.15 = (bf16[28,32,128]{2,1,0:T(8,128)(2,1)S(1)}, bf16[28,32,128]{2,1,0:T(8,128)(2,1)S(1)}, u32[]{:S(2)}, u32[]{:S(2)}) collective-permute-start(bf16[28,32,128]{2,1,0:T(8,128)(2,1)S(1)} %get-tuple-element.105.refs_1_), channel_id=1, source_target_pairs={{0,4},{4,0},{8,12},{12,8},{1,5},{5,1},{9,13},{13,9},{2,6},{6,2},{1... | collective-permute-start | bytes 688136 | tf_op jit(solution)/shard_map/hidden_core/ppermute | solution.py:107
  47.3 1.6 %collective-permute-start.16 = (bf16[28,32,128]{2,1,0:T(8,128)(2,1)S(1)}, bf16[28,32,128]{2,1,0:T(8,128)(2,1)S(1)}, u32[]{:S(2)}, u32[]{:S(2)}) collective-permute-start(bf16[28,32,128]{2,1,0:T(8,128)(2,1)S(1)} %get-tuple-element.106.refs_2_), channel_id=1, source_target_pairs={{0,4},{4,0},{8,12},{12,8},{1,5},{5,1},{9,13},{13,9},{2,6},{6,2},{1... | collective-permute-start | bytes 688136 | tf_op jit(solution)/shard_map/hidden_core/ppermute | solution.py:107
  47.6 1.7 %collective-permute-start.17 = (bf16[28,32,128]{2,1,0:T(8,128)(2,1)S(1)}, bf16[28,32,128]{2,1,0:T(8,128)(2,1)S(1)}, u32[]{:S(2)}, u32[]{:S(2)}) collective-permute-start(bf16[28,32,128]{2,1,0:T(8,128)(2,1)S(1)} %get-tuple-element.107.refs_3_), channel_id=1, source_target_pairs={{0,4},{4,0},{8,12},{12,8},{1,5},{5,1},{9,13},{13,9},{2,6},{6,2},{1... | collective-permute-start | bytes 688136 | tf_op jit(solution)/shard_map/hidden_core/ppermute | solution.py:107
  48.3 18.1 %collective-permute-start.21 = (bf16[128,4096]{1,0:T(8,128)(2,1)S(1)}, bf16[128,4096]{1,0:T(8,128)(2,1)S(1)}, u32[]{:S(2)}, u32[]{:S(2)}) collective-permute-start(bf16[128,4096]{1,0:T(8,128)(2,1)S(1)} %copy-done), channel_id=1, source_target_pairs={{0,4},{4,0},{8,12},{12,8},{1,5},{5,1},{9,13},{13,9},{2,6},{6,2},{1... | collective-permute-start | bytes 3145736 | tf_op jit(solution)/shard_map/tokens_core/ppermute | solution.py:107
  48.7 7.9 %collective-permute-start.18 = (bf16[14,128,128]{2,1,0:T(8,128)(2,1)S(1)}, bf16[14,128,128]{2,1,0:T(8,128)(2,1)S(1)}, u32[]{:S(2)}, u32[]{:S(2)}) collective-permute-start(bf16[14,128,128]{2,1,0:T(8,128)(2,1)S(1)} %collective-permute-done.12.refs_0_.refs_6_), channel_id=1, source_target_pairs={{0,4},{4,0},{8,12},{12,8},{1,5},{5,1},{9,13},{13,9},{2,6},{6,2},{1... | collective-permute-start | bytes 1376264 | tf_op jit(solution)/shard_map/down_x_core/ppermute | solution.py:107
  55.2 3.1 %collective-permute-start.20 = (bf16[14,128,128]{2,1,0:T(8,128)(2,1)S(1)}, bf16[14,128,128]{2,1,0:T(8,128)(2,1)S(1)}, u32[]{:S(2)}, u32[]{:S(2)}) collective-permute-start(bf16[14,128,128]{2,1,0:T(8,128)(2,1)S(1)} %collective-permute-done.19.refs_0_.refs_8_), channel_id=1, source_target_pairs={{0,4},{4,0},{8,12},{12,8},{1,5},{5,1},{9,13},{13,9},{2,6},{6,2},{1... | collective-permute-start | bytes 1376264 | tf_op jit(solution)/shard_map/down_y_core/ppermute | solution.py:107
  55.2 22.8 %collective-permute-start.25 = (bf16[28,128,128]{2,1,0:T(8,128)(2,1)S(1)}, bf16[28,128,128]{2,1,0:T(8,128)(2,1)S(1)}, u32[]{:S(2)}, u32[]{:S(2)}) collective-permute-start(bf16[28,128,128]{2,1,0:T(8,128)(2,1)S(1)} %shard_map.135), channel_id=1, source_target_pairs={{0,8},{4,12},{8,0},{12,4},{1,9},{5,13},{9,1},{13,5},{2,10},{6,14},... | collective-permute-start | bytes 2752520 | tf_op jit(solution)/shard_map/down_grad_chip/ppermute | solution.py:111
  60.4 6.0 %collective-permute-start.22 = (bf16[28,64,128]{2,1,0:T(8,128)(2,1)S(1)}, bf16[28,64,128]{2,1,0:T(8,128)(2,1)S(1)}, u32[]{:S(2)}, u32[]{:S(2)}) collective-permute-start(bf16[28,64,128]{2,1,0:T(8,128)(2,1)S(1)} %get-tuple-element.96.refs_2_.refs_0_), channel_id=1, source_target_pairs={{0,4},{4,0},{8,12},{12,8},{1,5},{5,1},{9,13},{13,9},{2,6},{6,2},{1... | collective-permute-start | bytes 1376264 | tf_op jit(solution)/shard_map/grads_core/ppermute | solution.py:107
  60.7 5.7 %collective-permute-start.23 = (bf16[28,64,128]{2,1,0:T(8,128)(2,1)S(1)}, bf16[28,64,128]{2,1,0:T(8,128)(2,1)S(1)}, u32[]{:S(2)}, u32[]{:S(2)}) collective-permute-start(bf16[28,64,128]{2,1,0:T(8,128)(2,1)S(1)} %get-tuple-element.97.refs_3_.refs_1_), channel_id=1, source_target_pairs={{0,4},{4,0},{8,12},{12,8},{1,5},{5,1},{9,13},{13,9},{2,6},{6,2},{1... | collective-permute-start | bytes 1376264 | tf_op jit(solution)/shard_map/grads_core/ppermute | solution.py:107
  61.0 23.6 %collective-permute-start.30 = (bf16[28,128,128]{2,1,0:T(8,128)(2,1)S(1)}, bf16[28,128,128]{2,1,0:T(8,128)(2,1)S(1)}, u32[]{:S(2)}, u32[]{:S(2)}) collective-permute-start(bf16[28,128,128]{2,1,0:T(8,128)(2,1)S(1)} %get-tuple-element.99.refs_0_.refs_2_), channel_id=1, source_target_pairs={{0,4},{4,0},{8,12},{12,8},{1,5},{5,1},{9,13},{13,9},{2,6},{6,2},{1... | collective-permute-start | bytes 2752520 | tf_op jit(solution)/shard_map/grads_core/ppermute | solution.py:107
  66.4 4.1 %copy-start.3 = (bf16[1,28,128,128]{3,2,1,0:T(8,128)(2,1)S(1)}, bf16[1,28,128,128]{3,2,1,0:T(8,128)(2,1)}, u32[]{:S(2)}) copy-start(bf16[1,28,128,128]{3,2,1,0:T(8,128)(2,1)} %param.11) | copy-start | bytes 2752516
  67.3 19.3 %collective-permute-start.24 = (bf16[2,128,1024]{2,1,0:T(8,128)(2,1)S(1)}, bf16[2,128,1024]{2,1,0:T(8,128)(2,1)S(1)}, u32[]{:S(2)}, u32[]{:S(2)}) collective-permute-start(bf16[2,128,1024]{2,1,0:T(8,128)(2,1)S(1)} %get-tuple-element.94), channel_id=1, source_target_pairs={{0,1},{1,0},{2,3},{3,2},{4,5},{5,4},{6,7},{7,6},{8,9},{9,8},{10,11... | collective-permute-start | bytes 1572872 | tf_op jit(solution)/shard_map/out_group/ppermute | solution.py:121
  77.9 23.3 %collective-permute-start.27 = (bf16[28,128,128]{2,1,0:T(8,128)(2,1)S(1)}, bf16[28,128,128]{2,1,0:T(8,128)(2,1)S(1)}, u32[]{:S(2)}, u32[]{:S(2)}) collective-permute-start(bf16[28,128,128]{2,1,0:T(8,128)(2,1)S(1)} %shard_map.139), channel_id=1, source_target_pairs={{0,8},{4,12},{8,0},{12,4},{1,9},{5,13},{9,1},{13,5},{2,10},{6,14},... | collective-permute-start | bytes 2752520 | tf_op jit(solution)/shard_map/gate_grad_chip/ppermute | solution.py:111
  84.5 18.9 %collective-permute-start.28 = (bf16[2,128,1024]{2,1,0:T(8,128)(2,1)S(1)}, bf16[2,128,1024]{2,1,0:T(8,128)(2,1)S(1)}, u32[]{:S(2)}, u32[]{:S(2)}) collective-permute-start(bf16[2,128,1024]{2,1,0:T(8,128)(2,1)S(1)} %get-tuple-element.101), channel_id=1, source_target_pairs={{0,1},{1,0},{2,3},{3,2},{4,5},{5,4},{6,7},{7,6},{8,9},{9,8},{10,11... | collective-permute-start | bytes 1572872 | tf_op jit(solution)/shard_map/token_group/ppermute | solution.py:121
  86.8 23.6 %collective-permute-start.26 = (bf16[1,128,1024]{2,1,0:T(8,128)(2,1)S(1)}, bf16[1,128,1024]{2,1,0:T(8,128)(2,1)S(1)}, u32[]{:S(2)}, u32[]{:S(2)}) collective-permute-start(bf16[1,128,1024]{2,1,0:T(8,128)(2,1)S(1)} %slice.21), channel_id=1, source_target_pairs={{0,2},{1,3},{2,0},{3,1},{4,6},{5,7},{6,4},{7,5},{8,10},{9,11},{10,... | collective-permute-start | bytes 786440 | tf_op jit(solution)/shard_map/out_group/ppermute | solution.py:121
  90.8 28.8 %collective-permute-start.31 = (bf16[28,128,128]{2,1,0:T(8,128)(2,1)S(1)}, bf16[28,128,128]{2,1,0:T(8,128)(2,1)S(1)}, u32[]{:S(2)}, u32[]{:S(2)}) collective-permute-start(bf16[28,128,128]{2,1,0:T(8,128)(2,1)S(1)} %shard_map.145), channel_id=1, source_target_pairs={{0,8},{4,12},{8,0},{12,4},{1,9},{5,13},{9,1},{13,5},{2,10},{6,14},... | collective-permute-start | bytes 2752520 | tf_op jit(solution)/shard_map/up_grad_chip/ppermute | solution.py:111
  103.7 13.3 %collective-permute-start.29 = (bf16[1,128,1024]{2,1,0:T(8,128)(2,1)S(1)}, bf16[1,128,1024]{2,1,0:T(8,128)(2,1)S(1)}, u32[]{:S(2)}, u32[]{:S(2)}) collective-permute-start(bf16[1,128,1024]{2,1,0:T(8,128)(2,1)S(1)} %slice.23), channel_id=1, source_target_pairs={{0,2},{1,3},{2,0},{3,1},{4,6},{5,7},{6,4},{7,5},{8,10},{9,11},{10,... | collective-permute-start | bytes 786440 | tf_op jit(solution)/shard_map/token_group/ppermute | solution.py:121
